TPU v7x, 32 devices: a whole 2x2x4 slice. The times are simulated.
32 devices in a mesh: dp: 8 (over y, x, core), mp: 4 (over z).
Axes of the slice: x: 2, y: 2, z: 4, core: 2. Of those that a mesh axis runs over, the one named last changes fastest.
Arguments:
- text_states: bfloat16 [128, 40, 768], P(('dp', 'mp')), may hold values from -6 to 6
- patch_states: bfloat16 [128, 145, 1024], P(('dp', 'mp')), may hold values from -6 to 6
- patch_rows: int32 [128], P('dp'), may hold values from 50 to 145, as said below
- cotangent: bfloat16 [128, 40, 768], P(('dp', 'mp')), may hold values from -6 to 6
- w_attn: bfloat16 [3, 768, 768], P(None, None, 'mp'), may hold values from -0.21875 to 0.21875
- attn_bias: bfloat16 [2, 768], P(None, 'mp'), may hold values from -3 to 3
- w_attn_out: bfloat16 [768, 768], P('mp'), may hold values from -0.4375 to 0.4375
- w_query: bfloat16 [768, 768], P(None, 'mp'), may hold values from -0.21875 to 0.21875
- w_patch: bfloat16 [2, 1024, 768], P(None, None, 'mp'), may hold values from -0.1875 to 0.1875
- cross_bias: bfloat16 [2, 768], P(None, 'mp'), may hold values from -3 to 3
- w_cross_out: bfloat16 [768, 768], P('mp'), may hold values from -0.625 to 0.625
- w_hidden: bfloat16 [768, 3072], P(None, 'mp'), may hold values from -0.21875 to 0.21875
- hidden_bias: bfloat16 [3072], P('mp'), may hold values from -3 to 3
- w_output: bfloat16 [3072, 768], P('mp'), may hold values from -0.15625 to 0.15625
- out_bias: bfloat16 [3, 768], replicated, may hold values from -3 to 3
- norm_gain: bfloat16 [3, 768], replicated, may hold values from 0.5 to 1.5
- norm_shift: bfloat16 [3, 768], replicated, may hold values from -2 to 2
Outputs:
- layer_out: float32 [128, 40, 768], P(('dp', 'mp'))
- text_grad: float32 [128, 40, 768], P(('dp', 'mp'))
- patch_grad: float32 [128, 145, 1024], P(('dp', 'mp'))
- grad_attn: float32 [3, 768, 768], P(None, None, 'mp')
- grad_attn_bias: float32 [2, 768], P(None, 'mp')
- grad_attn_out: float32 [768, 768], P('mp')
- grad_query: float32 [768, 768], P(None, 'mp')
- grad_patch: float32 [2, 1024, 768], P(None, None, 'mp')
- grad_cross_bias: float32 [2, 768], P(None, 'mp')
- grad_cross_out: float32 [768, 768], P('mp')
- grad_hidden: float32 [768, 3072], P(None, 'mp')
- grad_hidden_bias: float32 [3072], P('mp')
- grad_output: float32 [3072, 768], P('mp')
- grad_out_bias: float32 [3, 768], replicated
- grad_gain: float32 [3, 768], replicated
- grad_shift: float32 [3, 768], replicated
Inputs may be any that keep to these rules, and one draw needn't show every extreme that they name: `patch_rows`: each entry is 50 or 145.
All inputs are finite; a program needn't handle non-finite values.
Results may differ from a plain program's by a relative error of at most 0.019.
Values may be sent and summed in bfloat16 or wider, within the bound.
A program may use at most 128 MiB of HBM per device.

v0:
```python
import math

import jax
import jax.numpy as jnp
from jax import lax
from jax.sharding import PartitionSpec as P

HEAD = 64


epsilon = 1e-06


def group_gather(local_rows):
    return lax.all_gather(local_rows, "mp", axis=0, tiled=True)


def row_sum(term_fn, local_count):
    return lax.psum_scatter(
        term_fn(jnp.int32(0), local_count * lax.axis_size("mp")),
        "mp",
        scatter_dimension=0,
        tiled=True,
    )


def rows_term(group_values, weight, form):

    def term(first_row, row_count):
        return jnp.einsum(form, group_values, weight, preferred_element_type=jnp.float32)

    return term


def norm_forward(hidden_sum, gain, shift):
    row_mean = jnp.mean(hidden_sum, -1, keepdims=True)
    centred = hidden_sum - row_mean
    inverse = lax.rsqrt(jnp.mean(centred * centred, -1, keepdims=True) + epsilon)
    normed = centred * inverse
    return (normed * gain.astype(jnp.float32) + shift.astype(jnp.float32), normed, inverse)


def norm_backward(grad_out, normed, inverse, gain):
    scaled = grad_out * gain.astype(jnp.float32)
    grad_in = inverse * (
        scaled
        - jnp.mean(scaled, -1, keepdims=True)
        - normed * jnp.mean(scaled * normed, -1, keepdims=True)
    )
    return (grad_in, jnp.sum(grad_out * normed, axis=(0, 1)), jnp.sum(grad_out, axis=(0, 1)))


def split_heads(flat):
    return flat.reshape(flat.shape[:-1] + (flat.shape[-1] // HEAD, HEAD))


def masked_scores(queries, key_part, valid):
    score_scale = 1.0 / math.sqrt(HEAD)
    scores = (
        jnp.einsum(
            "gqhe,gkhe->ghqk",
            split_heads(queries),
            split_heads(key_part),
            preferred_element_type=jnp.float32,
        )
        * score_scale
    )
    if valid is not None:
        scores = jnp.where(valid, scores, -1e30)
    return scores


def attend_forward(queries, key_part, values, valid):
    scores = masked_scores(queries, key_part, valid)
    highest = jnp.max(scores, -1, keepdims=True)
    log_total = highest + jnp.log(jnp.sum(jnp.exp(scores - highest), -1, keepdims=True))
    attn_prob = jnp.exp(scores - log_total).astype(jnp.bfloat16)
    mixed = jnp.einsum(
        "ghqk,gkhe->gqhe", attn_prob, split_heads(values), preferred_element_type=jnp.float32
    )
    return (mixed.reshape(queries.shape).astype(jnp.bfloat16), log_total)


def attend_backward(queries, key_part, values, valid, log_total, grad_mixed):
    score_scale = 1.0 / math.sqrt(HEAD)
    attn_prob = jnp.exp(masked_scores(queries, key_part, valid) - log_total)
    grad_heads = split_heads(grad_mixed)
    grad_values = jnp.einsum(
        "ghqk,gqhe->gkhe",
        attn_prob.astype(jnp.bfloat16),
        grad_heads,
        preferred_element_type=jnp.float32,
    )
    grad_prob = jnp.einsum(
        "gqhe,gkhe->ghqk", grad_heads, split_heads(values), preferred_element_type=jnp.float32
    )
    row_delta = jnp.sum(attn_prob * grad_prob, -1, keepdims=True)
    grad_scores = (attn_prob * (grad_prob - row_delta)).astype(jnp.bfloat16)
    grad_queries = (
        jnp.einsum(
            "ghqk,gkhe->gqhe",
            grad_scores,
            split_heads(key_part),
            preferred_element_type=jnp.float32,
        )
        * score_scale
    )
    grad_keys = (
        jnp.einsum(
            "ghqk,gqhe->gkhe", grad_scores, split_heads(queries), preferred_element_type=jnp.float32
        )
        * score_scale
    )
    return (
        grad_queries.reshape(queries.shape).astype(jnp.bfloat16),
        grad_keys.reshape(key_part.shape).astype(jnp.bfloat16),
        grad_values.reshape(values.shape).astype(jnp.bfloat16),
    )


def per_device(
    text_states,
    patch_states,
    patch_rows,
    cotangent,
    w_attn,
    attn_bias,
    w_attn_out,
    w_query,
    w_patch,
    cross_bias,
    w_cross_out,
    w_hidden,
    hidden_bias,
    w_output,
    out_bias,
    norm_gain,
    norm_shift,
):
    local_items = text_states.shape[0]
    group_items = patch_rows.shape[0]
    patch_count = patch_states.shape[1]
    bias_rows = out_bias.astype(jnp.float32)
    group_text = group_gather(text_states)
    projected = jnp.einsum("ild,tdc->tilc", group_text, w_attn, preferred_element_type=jnp.float32)
    queries = (projected[0] + attn_bias[0]).astype(jnp.bfloat16)
    key_part = projected[1].astype(jnp.bfloat16)
    values = (projected[2] + attn_bias[1]).astype(jnp.bfloat16)
    self_mixed, self_total = attend_forward(queries, key_part, values, None)
    self_sum = row_sum(rows_term(self_mixed, w_attn_out, "ilc,cd->ild"), local_items)
    first_norm, first_normed, first_inverse = norm_forward(
        text_states.astype(jnp.float32) + self_sum + bias_rows[0], norm_gain[0], norm_shift[0]
    )
    first_low = first_norm.astype(jnp.bfloat16)
    group_first = group_gather(first_low)
    cross_queries = (
        jnp.einsum("ild,dc->ilc", group_first, w_query, preferred_element_type=jnp.float32)
        + cross_bias[0]
    ).astype(jnp.bfloat16)
    group_patches = lax.all_gather(patch_states, "mp", axis=0, tiled=True)
    patch_proj = jnp.einsum(
        "ipc,tcd->tipd", group_patches, w_patch, preferred_element_type=jnp.float32
    )
    cross_keys = patch_proj[0].astype(jnp.bfloat16)
    cross_values = (patch_proj[1] + cross_bias[1]).astype(jnp.bfloat16)
    positions = lax.broadcasted_iota(jnp.int32, (group_items, patch_count), 1)
    patch_valid = (positions < patch_rows[:, None])[:, None, None, :]
    cross_mixed, cross_total = attend_forward(cross_queries, cross_keys, cross_values, patch_valid)
    cross_sum = row_sum(rows_term(cross_mixed, w_cross_out, "ilc,cd->ild"), local_items)
    second_norm, second_normed, second_inverse = norm_forward(
        first_low.astype(jnp.float32) + cross_sum + bias_rows[1], norm_gain[1], norm_shift[1]
    )
    second_low = second_norm.astype(jnp.bfloat16)
    group_second = group_gather(second_low)
    hidden_pre = (
        jnp.einsum("ild,df->ilf", group_second, w_hidden, preferred_element_type=jnp.float32)
        + hidden_bias
    )
    hidden_act, gelu_pull = jax.vjp(
        lambda pre_act: jax.nn.gelu(pre_act, approximate=False), hidden_pre
    )
    hidden_low = hidden_act.astype(jnp.bfloat16)
    ffn_sum = row_sum(rows_term(hidden_low, w_output, "ilf,fd->ild"), local_items)
    final_norm, final_normed, final_inverse = norm_forward(
        second_low.astype(jnp.float32) + ffn_sum + bias_rows[2], norm_gain[2], norm_shift[2]
    )
    grad_third, gain_third, shift_third = norm_backward(
        cotangent.astype(jnp.float32), final_normed, final_inverse, norm_gain[2]
    )
    group_ffn_grad = group_gather(grad_third.astype(jnp.bfloat16))
    grad_output = jnp.einsum(
        "ilf,ild->fd", hidden_low, group_ffn_grad, preferred_element_type=jnp.float32
    )
    grad_act = jnp.einsum(
        "ild,fd->ilf", group_ffn_grad, w_output, preferred_element_type=jnp.float32
    )
    grad_pre = gelu_pull(grad_act)[0].astype(jnp.bfloat16)
    grad_hidden_bias = jnp.sum(grad_pre, axis=(0, 1), dtype=jnp.float32)
    grad_hidden = jnp.einsum(
        "ild,ilf->df", group_second, grad_pre, preferred_element_type=jnp.float32
    )
    back_second = row_sum(rows_term(grad_pre, w_hidden, "ilf,df->ild"), local_items)
    grad_second, gain_second, shift_second = norm_backward(
        grad_third + back_second, second_normed, second_inverse, norm_gain[1]
    )
    group_cross_grad = group_gather(grad_second.astype(jnp.bfloat16))
    grad_cross_out = jnp.einsum(
        "ilc,ild->cd", cross_mixed, group_cross_grad, preferred_element_type=jnp.float32
    )
    cross_mixed_grad = jnp.einsum(
        "ild,cd->ilc", group_cross_grad, w_cross_out, preferred_element_type=jnp.float32
    ).astype(jnp.bfloat16)
    cross_q_grad, cross_k_grad, cross_v_grad = attend_backward(
        cross_queries, cross_keys, cross_values, patch_valid, cross_total, cross_mixed_grad
    )
    grad_query = jnp.einsum(
        "ild,ilc->dc", group_first, cross_q_grad, preferred_element_type=jnp.float32
    )
    query_bias_grad = jnp.sum(cross_q_grad, axis=(0, 1), dtype=jnp.float32)
    back_first = row_sum(rows_term(cross_q_grad, w_query, "ilc,dc->ild"), local_items)
    kv_grad = jnp.stack([cross_k_grad, cross_v_grad], 0)
    grad_patch = jnp.einsum(
        "ipc,tiph->tch", group_patches, kv_grad, preferred_element_type=jnp.float32
    )
    value_bias_grad = jnp.sum(cross_v_grad, axis=(0, 1), dtype=jnp.float32)
    patch_grad = lax.psum_scatter(
        jnp.einsum("tiph,tch->ipc", kv_grad, w_patch, preferred_element_type=jnp.float32),
        "mp",
        scatter_dimension=0,
        tiled=True,
    )
    grad_cross_bias = jnp.stack([query_bias_grad, value_bias_grad])
    grad_first, gain_first, shift_first = norm_backward(
        grad_second + back_first, first_normed, first_inverse, norm_gain[0]
    )
    group_self_grad = group_gather(grad_first.astype(jnp.bfloat16))
    grad_attn_out = jnp.einsum(
        "ilc,ild->cd", self_mixed, group_self_grad, preferred_element_type=jnp.float32
    )
    self_mixed_grad = jnp.einsum(
        "ild,cd->ilc", group_self_grad, w_attn_out, preferred_element_type=jnp.float32
    ).astype(jnp.bfloat16)
    self_q_grad, self_k_grad, self_v_grad = attend_backward(
        queries, key_part, values, None, self_total, self_mixed_grad
    )
    proj_grad = jnp.stack([self_q_grad, self_k_grad, self_v_grad], 2)
    grad_attn = jnp.einsum(
        "ild,iltc->tdc", group_text, proj_grad, preferred_element_type=jnp.float32
    )
    grad_attn_bias = jnp.stack(
        [
            jnp.sum(self_q_grad, axis=(0, 1), dtype=jnp.float32),
            jnp.sum(self_v_grad, axis=(0, 1), dtype=jnp.float32),
        ]
    )
    back_text = row_sum(rows_term(proj_grad, w_attn, "iltc,tdc->ild"), local_items)
    text_grad = grad_first + back_text
    bias_grads = jnp.stack(
        [
            jnp.sum(grad_first, axis=(0, 1)),
            jnp.sum(grad_second, axis=(0, 1)),
            jnp.sum(grad_third, axis=(0, 1)),
        ]
    )
    gain_grads = jnp.stack([gain_first, gain_second, gain_third])
    shift_grads = jnp.stack([shift_first, shift_second, shift_third])
    (
        grad_attn,
        grad_attn_bias,
        grad_attn_out,
        grad_query,
        grad_patch,
        grad_cross_bias,
        grad_cross_out,
        grad_hidden,
        grad_hidden_bias,
        grad_output,
    ) = lax.psum(
        (
            grad_attn,
            grad_attn_bias,
            grad_attn_out,
            grad_query,
            grad_patch,
            grad_cross_bias,
            grad_cross_out,
            grad_hidden,
            grad_hidden_bias,
            grad_output,
        ),
        "dp",
    )
    grad_out_bias, grad_gain, grad_shift = lax.psum(
        (bias_grads, gain_grads, shift_grads), ("dp", "mp")
    )
    return (
        final_norm,
        text_grad,
        patch_grad,
        grad_attn,
        grad_attn_bias,
        grad_attn_out,
        grad_query,
        grad_patch,
        grad_cross_bias,
        grad_cross_out,
        grad_hidden,
        grad_hidden_bias,
        grad_output,
        grad_out_bias,
        grad_gain,
        grad_shift,
    )


def solution(mesh):
    return jax.shard_map(
        per_device,
        mesh=mesh,
        in_specs=(
            P(("dp", "mp"), None, None),
            P(("dp", "mp"), None, None),
            P("dp"),
            P(("dp", "mp"), None, None),
            P(None, None, "mp"),
            P(None, "mp"),
            P("mp", None),
            P(None, "mp"),
            P(None, None, "mp"),
            P(None, "mp"),
            P("mp", None),
            P(None, "mp"),
            P("mp"),
            P("mp", None),
            P(),
            P(),
            P(),
        ),
        out_specs=(
            P(("dp", "mp"), None, None),
            P(("dp", "mp"), None, None),
            P(("dp", "mp"), None, None),
            P(None, None, "mp"),
            P(None, "mp"),
            P("mp", None),
            P(None, "mp"),
            P(None, None, "mp"),
            P(None, "mp"),
            P("mp", None),
            P(None, "mp"),
            P("mp"),
            P("mp", None),
            P(),
            P(),
            P(),
        ),
        check_vma=False,
    )
```

profile of v0, /device:TPU:0, one launch (start us, length us, event | category | flops | bytes accessed | tf_op | source)
XLA Modules:
  0.0 897.4 jit_solution(16877745695997397641)
XLA Ops:
  7.2 23.8 %all_gather.21 = bf16[16,40,768]{2,1,0:T(8,128)(2,1)S(1)} all-gather(bf16[4,40,768]{2,1,0:T(8,128)(2,1)} %param.17), channel_id=1, replica_groups=mesh['dp'=8,'mp'=4] {'mp'}, dimensions={0}, use_global_device_ids=true | all-gather | bytes 1228800 | tf_op jit(solution)/shard_map/all_gather | solution.py:15
  31.1 2.5 convolution_bitcast_fusion.4
  38.1 1.6 squeeze.6
  41.5 2.8 fusion.68
  44.4 1.4 copy.90
  47.4 38.4 %reduce-scatter.8.cloned.1.call-done = f32[4,40,768]{2,1,0:T(8,128)} async-done(((f32[16,40,768]{2,1,0:T(8,128)}), f32[4,40,768]{2,1,0:T(8,128)}) %reduce-scatter.8.cloned.1.call-update) | async-done | bytes 491536 | tf_op jit(solution)/shard_map/reduce_scatter | solution.py:19
  85.8 1.2 fusion.87
  87.9 29.5 %all_gather.23 = bf16[16,40,768]{2,1,0:T(8,128)(2,1)S(1)} all-gather(bf16[4,40,768]{2,1,0:T(8,128)(2,1)S(1)} %add_convert_fusion.7), channel_id=1, replica_groups=mesh['dp'=8,'mp'=4] {'mp'}, dimensions={0}, use_global_device_ids=true | all-gather | bytes 1228800 | tf_op jit(solution)/shard_map/all_gather | solution.py:15
  119.8 68.5 %all-gather.2.cloned.1.call-done = bf16[16,145,1024]{2,1,0:T(8,128)(2,1)} async-done(((bf16[4,145,1024]{2,1,0:T(8,128)(2,1)}), bf16[16,145,1024]{2,1,0:T(8,128)(2,1)}) %all-gather.2.cloned.1.call-update) | async-done | bytes 4751376 | tf_op jit(solution)/shard_map/all_gather | solution.py:160
  188.3 4.7 fusion.4
  193.2 1.7 slice.81
  194.8 1.7 copy.92
  196.5 3.6 copy.91
  200.1 2.4 fusion.90
  205.0 1.6 convert_element_type.354
  206.6 2.8 fusion.62
  210.3 40.3 %reduce-scatter.10.cloned.1.call-done = f32[4,40,768]{2,1,0:T(8,128)} async-done(((f32[16,40,768]{2,1,0:T(8,128)}), f32[4,40,768]{2,1,0:T(8,128)}) %reduce-scatter.10.cloned.1.call-update) | async-done | bytes 491536 | tf_op jit(solution)/shard_map/reduce_scatter | solution.py:19
  250.6 1.5 fusion.86
  253.1 20.2 %all_gather.24 = bf16[16,40,768]{2,1,0:T(8,128)(2,1)S(1)} all-gather(bf16[4,40,768]{2,1,0:T(8,128)(2,1)S(1)} %add_convert_fusion.6), channel_id=1, replica_groups=mesh['dp'=8,'mp'=4] {'mp'}, dimensions={0}, use_global_device_ids=true | all-gather | bytes 1228800 | tf_op jit(solution)/shard_map/all_gather | solution.py:15
  273.3 1.3 fusion.34
  274.6 5.3 multiply_convert_fusion.2
  280.9 2.2 fusion.25
  283.2 41.2 %reduce-scatter.12.cloned.1.call-done = f32[4,40,768]{2,1,0:T(8,128)} async-done(((f32[16,40,768]{2,1,0:T(8,128)}), f32[4,40,768]{2,1,0:T(8,128)}) %reduce-scatter.12.cloned.1.call-update) | async-done | bytes 491536 | tf_op jit(solution)/shard_map/reduce_scatter | solution.py:19
  324.4 1.6 fusion.84
  327.0 20.2 %all_gather.25 = bf16[16,40,768]{2,1,0:T(8,128)(2,1)S(1)} all-gather(bf16[4,40,768]{2,1,0:T(8,128)(2,1)S(1)} %fusion.80), channel_id=1, replica_groups=mesh['dp'=8,'mp'=4] {'mp'}, dimensions={0}, use_global_device_ids=true | all-gather | bytes 1228800 | tf_op jit(solution)/shard_map/all_gather | solution.py:15
  347.2 3.8 convert_reduce_fusion.1
  351.9 2.3 fusion.27
  354.2 41.2 %reduce-scatter.14.cloned.1.call-done = f32[4,40,768]{2,1,0:T(8,128)} async-done(((f32[16,40,768]{2,1,0:T(8,128)}), f32[4,40,768]{2,1,0:T(8,128)}) %reduce-scatter.14.cloned.1.call-update) | async-done | bytes 491536 | tf_op jit(solution)/shard_map/reduce_scatter | solution.py:19
  395.5 2.3 fusion.47
  398.1 20.3 %all_gather.26 = bf16[16,40,768]{2,1,0:T(8,128)(2,1)S(1)} all-gather(bf16[4,40,768]{2,1,0:T(8,128)(2,1)S(1)} %convert_element_type.370), channel_id=1, replica_groups=mesh['dp'=8,'mp'=4] {'mp'}, dimensions={0}, use_global_device_ids=true | all-gather | bytes 1228800 | tf_op jit(solution)/shard_map/all_gather | solution.py:15
  420.8 3.2 multiply_reduce_fusion
  427.7 1.6 convert_element_type.375
  429.3 2.7 fusion.64
  432.3 41.0 %reduce-scatter.16.cloned.1.call-done = f32[4,40,768]{2,1,0:T(8,128)} async-done(((f32[16,40,768]{2,1,0:T(8,128)}), f32[4,40,768]{2,1,0:T(8,128)}) %reduce-scatter.16.cloned.1.call-update) | async-done | bytes 491536 | tf_op jit(solution)/shard_map/reduce_scatter | solution.py:19
  473.3 1.3 multiply_reduce_fusion.3
  475.7 20.3 %all_gather.27 = bf16[16,40,768]{2,1,0:T(8,128)(2,1)S(1)} all-gather(bf16[4,40,768]{2,1,0:T(8,128)(2,1)S(1)} %convert_element_type.376), channel_id=1, replica_groups=mesh['dp'=8,'mp'=4] {'mp'}, dimensions={0}, use_global_device_ids=true | all-gather | bytes 1228800 | tf_op jit(solution)/shard_map/all_gather | solution.py:15
  497.0 1.2 convolution_convert_fusion.4
  498.2 2.2 reshape.314
  500.4 1.8 multiply_reduce_fusion.1
  502.2 1.2 convert_reduce_fusion.3
  503.7 1.2 fusion.20
  506.8 1.3 copy.103
  510.6 3.7 convolution_bitcast_fusion.3
  515.5 2.9 multiply_convert_fusion
  518.3 2.7 copy.111
  521.1 2.0 convert_reduce_fusion
  523.0 2.8 copy.112
  525.8 7.2 convolution_bitcast_fusion
  534.2 3.9 convolution_bitcast_fusion.1
  538.1 2.5 convolution_bitcast_fusion.2
  540.7 1.3 convolution_bitcast_fusion.7
  541.9 1.2 convolution_bitcast_fusion.6
  543.3 3.7 fusion.14
  547.0 1.2 convolution_bitcast_fusion.8
  548.7 2.2 convolution_bitcast_fusion.5
  552.0 13.0 %all-reduce.1 = (f32[2,192]{1,0:T(2,128)}, f32[2,192]{1,0:T(2,128)}, f32[768]{0:T(1024)}) all-reduce(f32[2,192]{1,0:T(2,128)S(1)} %pad_maximum_fusion.11, f32[2,192]{1,0:T(2,128)S(1)} %pad_maximum_fusion.12, f32[768]{0:T(1024)S(1)} %copy-done.79), channel_id=1, replica_groups=mesh['dp'=8,'mp'=4] {'dp'}, use_global_device_ids=true, to_apply=%region_28.29 | all-reduce | flops 1536 | bytes 12288 | tf_op jit(solution)/shard_map/psum | solution.py:278
  565.0 44.8 %all-reduce = (f32[3,768]{1,0:T(4,128)}, f32[3,768]{1,0:T(4,128)}, f32[3,768]{1,0:T(4,128)}) all-reduce(f32[3,768]{1,0:T(4,128)S(1)} %pad_maximum_fusion.8, f32[3,768]{1,0:T(4,128)S(1)} %pad_maximum_fusion.9, f32[3,768]{1,0:T(4,128)S(1)} %pad_maximum_fusion.10), channel_id=1, replica_groups=mesh['dp'=8,'mp'=4] {'dp','mp'}, use_global_device_ids=true, to_apply=%region_43.44 | all-reduce | flops 6912 | bytes 55296 | tf_op jit(solution)/shard_map/psum | solution.py:293
  609.8 1.9 add.230
  611.7 116.1 %reduce-scatter.20.cloned.1.call-done = f32[4,145,1024]{2,1,0:T(8,128)} async-done(((f32[16,145,1024]{2,1,0:T(8,128)}), f32[4,145,1024]{2,1,0:T(8,128)}) %reduce-scatter.20.cloned.1.call-update) | async-done | bytes 2375696 | tf_op jit(solution)/shard_map/reduce_scatter | solution.py:226
  727.8 4.6 copy.113
  732.4 147.0 %all-reduce.5.cloned.1.call-done = (f32[3,768,192]{1,2,0:T(8,128)}, f32[192,768]{1,0:T(8,128)}, f32[768,192]{0,1:T(8,128)}, f32[2,1024,192]{1,2,0:T(8,128)}, f32...) async-done(((f32[3,768,192]{1,2,0:T(8,128)}, f32[192,768]{1,0:T(8,128)}, f32[768,192]{0,1:T(8,128)}, f32[2,1024,192]{1,2,0:T(8,128)}, f32[192,768]{1,0:T(8,128)}, ...) | async-done | bytes 9830416 | tf_op jit(solution)/shard_map/psum | solution.py:278
  879.5 2.9 copy.171
  886.5 1.4 copy.176
  889.0 1.4 copy.177
  (285 shorter events, 40.9 us)
Async XLA Ops:
  7.2 266.1 %copy-start = (bf16[768,768]{1,0:T(8,128)(2,1)S(1)}, bf16[768,768]{1,0:T(8,128)(2,1)}, u32[]{:S(2)}) copy-start(bf16[768,768]{1,0:T(8,128)(2,1)} %param.28) | copy-start | bytes 3538948
  7.2 78.6 %reduce-scatter.8.cloned.1.call-start = ((), (), s32[]{:S(2)}) async-start(), calls=%async_computation.7 | async-start | bytes 2457600 | tf_op jit(solution)/shard_map/reduce_scatter | solution.py:19
  31.1 2.5 copy-start.43
  37.7 2.2 copy-start.2
  41.4 2.9 copy-start.35
  41.4 3.0 copy-start.41
  44.3 3.0 copy-start.81
  44.4 41.4 %copy-start.42 = (bf16[4,40,768]{2,1,0:T(8,128)(2,1)S(1)}, bf16[4,40,768]{2,1,0:T(8,128)(2,1)}, u32[]{:S(2)}) copy-start(bf16[4,40,768]{2,1,0:T(8,128)(2,1)} %param.17) | copy-start | bytes 737284
  44.4 143.9 %all-gather.2.cloned.1.call-start = ((), (), s32[]{:S(2)}) async-start(), calls=%async_computation.8 | async-start | bytes 6225920 | tf_op jit(solution)/shard_map/all_gather | solution.py:160
  45.8 72.5 %copy-start.62 = (bf16[768,192]{0,1:T(8,128)(2,1)S(1)}, bf16[768,192]{0,1:T(8,128)(2,1)}, u32[]{:S(2)}) copy-start(bf16[768,192]{0,1:T(8,128)(2,1)} %param.24) | copy-start | bytes 884740
  45.9 204.7 %reduce-scatter.10.cloned.1.call-start = ((), (), s32[]{:S(2)}) async-start(), calls=%async_computation.9 | async-start | bytes 2457600 | tf_op jit(solution)/shard_map/reduce_scatter | solution.py:19
  46.0 157.2 %copy-start.68 = (f32[3,64]{1,0:T(4,128)}, f32[3,64]{1,0:T(4,128)S(1)}, u32[]{:S(2)}) copy-start(f32[3,64]{1,0:T(4,128)S(1)} %reshape.319) | copy-start | bytes 2308
  46.7 72.1 %copy-start.67 = (f32[768]{0:T(1024)}, f32[768]{0:T(1024)S(1)}, u32[]{:S(2)}) copy-start(f32[768]{0:T(1024)S(1)} %get-tuple-element.86) | copy-start | bytes 9220
  87.2 32.7 %copy-start.64 = (f32[4,40]{1,0:T(4,128)}, f32[4,40]{1,0:T(4,128)S(1)}, u32[]{:S(2)}) copy-start(f32[4,40]{1,0:T(4,128)S(1)} %add_rsqrt_fusion.2) | copy-start | bytes 1924
  87.9 100.4 %copy-start.83 = (bf16[2,1024,192]{1,2,0:T(8,128)(2,1)S(1)}, bf16[2,1024,192]{1,2,0:T(8,128)(2,1)}, u32[]{:S(2)}) copy-start(bf16[2,1024,192]{1,2,0:T(8,128)(2,1)} %param.25) | copy-start | bytes 2359300
  200.1 3.1 copy-start.4
  206.6 2.8 copy-start.37
  209.4 115.0 %reduce-scatter.12.cloned.1.call-start = ((), (), s32[]{:S(2)}) async-start(), calls=%async_computation.10 | async-start | bytes 2457600 | tf_op jit(solution)/shard_map/reduce_scatter | solution.py:19
  209.6 43.3 %copy-start.66 = (f32[768]{0:T(1024)S(1)}, f32[768]{0:T(1024)}, u32[]{:S(2)}) copy-start(f32[768]{0:T(1024)} %get-tuple-element.87) | copy-start | bytes 9220
  210.3 64.2 %copy-start.72 = (f32[768]{0:T(1024)}, f32[768]{0:T(1024)S(1)}, u32[]{:S(2)}) copy-start(f32[768]{0:T(1024)S(1)} %convert_element_type.361) | copy-start | bytes 9220
  274.5 5.4 copy-start.30
  274.6 6.3 copy-start.82
  283.1 41.3 %copy-start.71 = (f32[768]{0:T(1024)S(1)}, f32[768]{0:T(1024)}, u32[]{:S(2)}) copy-start(f32[768]{0:T(1024)} %get-tuple-element.79) | copy-start | bytes 9220
  283.1 43.2 %copy-start.27 = (bf16[4,40,768]{2,1,0:T(8,128)(2,1)S(1)}, bf16[4,40,768]{2,1,0:T(8,128)(2,1)}, u32[]{:S(2)}) copy-start(bf16[4,40,768]{2,1,0:T(8,128)(2,1)} %param.20) | copy-start | bytes 737284
  283.1 112.4 %reduce-scatter.14.cloned.1.call-start = ((), (), s32[]{:S(2)}) async-start(), calls=%async_computation.11 | async-start | bytes 2457600 | tf_op jit(solution)/shard_map/reduce_scatter | solution.py:19
  324.4 22.8 %copy-start.32 = (f32[16,40,768]{2,1,0:T(8,128)S(1)}, f32[16,40,768]{2,1,0:T(8,128)}, u32[]{:S(2)}) copy-start(f32[16,40,768]{2,1,0:T(8,128)} %get-tuple-element.112) | copy-start | bytes 5898244
  326.0 21.2 %copy-start.31 = (f32[16,40,768]{2,1,0:T(8,128)S(1)}, f32[16,40,768]{2,1,0:T(8,128)}, u32[]{:S(2)}) copy-start(f32[16,40,768]{2,1,0:T(8,128)} %copy-done.30) | copy-start | bytes 5898244
  326.0 21.2 %copy-start.73 = (f32[768]{0:T(1024)S(1)}, f32[768]{0:T(1024)}, u32[]{:S(2)}) copy-start(f32[768]{0:T(1024)} %copy-done.72) | copy-start | bytes 9220
  347.2 3.8 copy-start.47
  354.2 41.3 %copy-start.8 = (f32[4,40,768]{2,1,0:T(8,128)S(1)}, f32[4,40,768]{2,1,0:T(8,128)}, u32[]{:S(2)}) copy-start(f32[4,40,768]{2,1,0:T(8,128)} %copy-done.7) | copy-start | bytes 1474564
  354.2 41.3 %copy-start.11 = (f32[4,40,768]{2,1,0:T(8,128)S(1)}, f32[4,40,768]{2,1,0:T(8,128)}, u32[]{:S(2)}) copy-start(f32[4,40,768]{2,1,0:T(8,128)} %copy-done.10) | copy-start | bytes 1474564
  354.2 41.3 %copy-start.70 = (f32[768]{0:T(1024)S(1)}, f32[768]{0:T(1024)}, u32[]{:S(2)}) copy-start(f32[768]{0:T(1024)} %get-tuple-element.85) | copy-start | bytes 9220
  354.2 119.1 %reduce-scatter.16.cloned.1.call-start = ((), (), s32[]{:S(2)}) async-start(), calls=%async_computation.12 | async-start | bytes 2457600 | tf_op jit(solution)/shard_map/reduce_scatter | solution.py:19
  397.8 21.6 %copy-start.61 = (bf16[192,768]{1,0:T(8,128)(2,1)S(1)}, bf16[192,768]{1,0:T(8,128)(2,1)}, u32[]{:S(2)}) copy-start(bf16[192,768]{1,0:T(8,128)(2,1)} %param.27) | copy-start | bytes 884740
  398.0 22.8 %copy-start.16 = (f32[4,40,768]{2,1,0:T(8,128)}, f32[4,40,768]{2,1,0:T(8,128)S(1)}, u32[]{:S(2)}) copy-start(f32[4,40,768]{2,1,0:T(8,128)S(1)} %get-tuple-element.106) | copy-start | bytes 1474564
  398.1 22.8 %copy-start.69 = (f32[3,64]{1,0:T(4,128)S(1)}, f32[3,64]{1,0:T(4,128)}, u32[]{:S(2)}) copy-start(f32[3,64]{1,0:T(4,128)} %copy-done.68) | copy-start | bytes 2308
  425.4 2.2 copy-start.12
  429.3 44.0 %copy-start.6 = (f32[4,40,768]{2,1,0:T(8,128)S(1)}, f32[4,40,768]{2,1,0:T(8,128)}, u32[]{:S(2)}) copy-start(f32[4,40,768]{2,1,0:T(8,128)} %copy-done.5) | copy-start | bytes 1474564
  429.3 44.0 %copy-start.17 = (f32[4,40,768]{2,1,0:T(8,128)S(1)}, f32[4,40,768]{2,1,0:T(8,128)}, u32[]{:S(2)}) copy-start(f32[4,40,768]{2,1,0:T(8,128)} %copy-done.16) | copy-start | bytes 1474564
  429.3 44.0 %copy-start.65 = (f32[4,40]{1,0:T(4,128)S(1)}, f32[4,40]{1,0:T(4,128)}, u32[]{:S(2)}) copy-start(f32[4,40]{1,0:T(4,128)} %copy-done.64) | copy-start | bytes 1924
  432.1 177.8 %reduce-scatter.18.cloned.1.call-start = ((), (), s32[]{:S(2)}) async-start(), calls=%async_computation.13 | async-start | bytes 2457600 | tf_op jit(solution)/shard_map/reduce_scatter | solution.py:19
  474.6 22.4 %copy-start.63 = (bf16[192,768]{1,0:T(8,128)(2,1)S(1)}, bf16[192,768]{1,0:T(8,128)(2,1)}, u32[]{:S(2)}) copy-start(bf16[192,768]{1,0:T(8,128)(2,1)} %param.23) | copy-start | bytes 884740
  475.7 24.7 %copy-start.3 = (f32[16,3,40,40]{2,3,1,0:T(8,128)S(1)}, f32[16,3,40,40]{2,3,1,0:T(8,128)}, u32[]{:S(2)}) copy-start(f32[16,3,40,40]{2,3,1,0:T(8,128)} %copy-done.2) | copy-start | bytes 921604
  505.4 3.8 copy-start.33
  514.3 213.5 %reduce-scatter.20.cloned.1.call-start = ((), (), s32[]{:S(2)}) async-start(), calls=%async_computation.14 | async-start | bytes 12451840 | tf_op jit(solution)/shard_map/reduce_scatter | solution.py:226
  518.3 2.7 copy-start.21
  523.0 2.8 copy-start.39
  523.0 2.8 copy-start.84
  533.0 346.4 %all-reduce.5.cloned.1.call-start = ((), (), s32[]{:S(2)}) async-start(), calls=%async_computation.15 | async-start | bytes 19660800 | tf_op jit(solution)/shard_map/psum | solution.py:278
  534.2 3.9 copy-start.46
  534.2 3.9 copy-start.86
  534.2 9.0 %slice-start = ((s8[4980736]{0:T(1024)(128)(4,1)}), s8[4194304]{0:T(1024)(128)(4,1)S(1)}, s32[]{:S(2)}) async-start(s8[4980736]{0:T(1024)(128)(4,1)} %bitcast.158), calls=%async_computation.16 | async-start | bytes 8388608
  538.1 2.6 copy-start.24
  538.1 3.8 copy-start.38
  538.1 3.8 copy-start.50
  538.1 5.1 slice-start.1
  543.3 3.7 copy-start.36
  543.3 3.7 copy-start.52
  550.9 58.9 %copy-start.15 = (f32[4,40,768]{2,1,0:T(8,128)S(1)}, f32[4,40,768]{2,1,0:T(8,128)}, u32[]{:S(2)}) copy-start(f32[4,40,768]{2,1,0:T(8,128)} %copy-done.14) | copy-start | bytes 1474564
  879.5 2.9 copy-start.56
  879.5 3.7 copy-start.55
  884.0 2.5 copy-start.26
  886.5 2.5 copy-start.25
  886.5 3.9 copy-start.1
  (34 other events, 40.9 us)
Sparse Core Ops, SparseCore 0:
  44.4 41.2 reduce-scatter.7
  87.9 100.3 all-gather.1
  209.5 41.0 reduce-scatter.9
  283.2 41.1 reduce-scatter.11
  354.3 41.1 reduce-scatter.13
  432.2 41.0 reduce-scatter.15
  514.4 41.0 reduce-scatter.17
  557.9 169.8 reduce-scatter.19
  733.9 145.5 all-reduce.4
where the time goes:
time: 907 us; the launch traced here: 897 us
  waiting for transfers between devices  534 us (59%)
  blocking collectives  192 us (21%)
  matrix products  71.8 us (8%)
  local copies, waits for them, and re-layouts  62.4 us (7%)
  other arithmetic  20.9 us (2%)
  between operations  15.3 us (2%)
    reduce_scatter x6, waiting for transfers between devices, row_sum(): lax.psum_scatter(term_fn(jnp.int32(0), local_count * lax.axis_size('mp'))...  202 us
    psum x1, waiting for transfers between devices, per_device(): lax.psum((grad_attn, grad_attn_bias, grad_attn_out, grad_query, grad_patc...  147 us
    all_gather x6, blocking collectives, group_gather(): return lax.all_gather(local_rows, 'mp', axis=0, tiled=True)  134 us
    reduce_scatter x1, waiting for transfers between devices, per_device(): lax.psum_scatter(jnp.einsum('tiph,tch->ipc', kv_grad, w_patch, preferred_...  116 us
    all_gather x1, waiting for transfers between devices, per_device(): group_patches = lax.all_gather(patch_states, 'mp', axis=0, tiled=True)  68.5 us
    psum x1, blocking collectives, per_device(): lax.psum((bias_grads, gain_grads, shift_grads), ('dp', 'mp'))  44.8 us
    unnamed x187, local copies, waits for them, and re-layouts  30.1 us
  transfers between devices with their start and end apart: 9, of which 8 were waited for; matrix products, arithmetic and copies ran while one was open for 5% of the time, Pallas kernels for 0%

commit v1 on v0

v1 whole, which is shorter than its diff:
```python
import math
import functools
import jax, jax.numpy as jnp
from jax import lax
from jax.experimental import pallas as pl
from jax.experimental.pallas import tpu as pltpu

from jax.sharding import PartitionSpec as P

MESH = pl.DeviceIdType.MESH

def bit_of(d, b):
    return lax.rem(lax.div(d, jnp.int32(2 ** b)), jnp.int32(2))

def flip(d, b):
    return d + (1 - 2 * bit_of(d, b)) * (2 ** b)

def when(cond, fn):
    if cond is True:
        fn()
    else:
        pl.when(cond)(fn)

class Gather:
    def __init__(self, src, dst, row0, rows, order, d, z, nz, sems, base):
        self.src, self.dst, self.row0, self.order = src, dst, row0, order
        self.d, self.z, self.nz = d, z, nz
        self.piece = rows // (2 ** len(order))
        self.zs, self.zr, self.ps, self.pr = sems
        self.base = base
        self.k = len(order)

    def win(self, s):
        w = jnp.int32(0)
        for i, b in enumerate(self.order):
            if i >= s:
                w = w + bit_of(self.d, b) * (2 ** i)
        size = self.piece * 2 ** s
        start = self.row0 + w * self.piece
        return pl.ds(pl.multiple_of(start, 16), size)

    def shard(self, dr, j):
        return self.z - j if dr == 0 else self.z + j

    def has(self, dr, j):
        return self.z >= j if dr == 0 else self.z + j < self.nz

    def zcopy(self, dr, j):
        t = self.shard(dr, j)
        rows = self.win(0)
        src = self.src.at[rows] if j == 0 else self.dst.at[t, rows]
        to = self.z + 1 if dr == 0 else self.z - 1
        return pltpu.make_async_remote_copy(src, self.dst.at[t, rows], self.zs.at[self.base, dr, j], self.zr.at[self.base, dr, j], device_id=(self.d, to), device_id_type=MESH)

    def zcan(self, dr, j):
        ahead = self.z + 1 < self.nz if dr == 0 else self.z >= 1
        return ahead if j == 0 else jnp.logical_and(ahead, self.has(dr, j))

    def pcopy(self, s, dr, j):
        t = self.shard(dr, j)
        rows = self.win(s)
        b = self.order[s]
        return pltpu.make_async_remote_copy(self.dst.at[t, rows], self.dst.at[t, rows], self.ps.at[self.base, s, dr, j - 1], self.pr.at[self.base, s, dr, j - 1], device_id=(flip(self.d, b), self.z), device_id_type=MESH)

    def events(self):
        return self.nz + self.k

    def event(self, e):
        nz, k = self.nz, self.k
        if e == 0:
            for dr in (0, 1):
                when(self.zcan(dr, 0), lambda: self.zcopy(dr, 0).start())
            return
        for s in range(k, -1, -1):
            j = e - s
            if not 1 <= j <= nz - 1:
                continue
            for dr in (0, 1):
                def go(dr=dr, j=j, s=s):
                    if s == 0:
                        self.zcopy(dr, j - 1).wait_recv()
                        if j <= nz - 2:
                            when(self.zcan(dr, j), lambda: self.zcopy(dr, j).start())
                    else:
                        self.pcopy(s - 1, dr, j).wait_recv()
                    if s < k:
                        self.pcopy(s, dr, j).start()
                when(self.has(dr, j), go)

    def finish(self):
        nz, k = self.nz, self.k
        for dr in (0, 1):
            for j in range(nz - 1):
                when(self.zcan(dr, j), lambda dr=dr, j=j: self.zcopy(dr, j).wait_send())
            for s in range(k):
                for j in range(1, nz):
                    when(self.has(dr, j), lambda dr=dr, j=j, s=s: self.pcopy(s, dr, j).wait_send())

def enter(d, z, nd, nz, bits):
    bar = pltpu.get_barrier_semaphore()
    for b in bits:
        pl.semaphore_signal(bar, inc=1, device_id=(flip(d, b), z), device_id_type=MESH)
    @pl.when(z + 1 < nz)
    def _():
        pl.semaphore_signal(bar, inc=1, device_id=(d, z + 1), device_id_type=MESH)
    @pl.when(z >= 1)
    def _():
        pl.semaphore_signal(bar, inc=1, device_id=(d, z - 1), device_id_type=MESH)
    last = nz - 1
    pl.semaphore_wait(bar, len(bits) + lax.div(z + last, jnp.int32(nz)) + lax.div(last - z + last, jnp.int32(nz)))

def gather_kernel(plan, nd, nz, bits, *refs):
    n = max(p[0] for p in plan) + 1
    ins, outs = refs[:n], refs[n:2 * n]
    own = refs[2 * n:3 * n]
    zs, zr, ps, pr, lsem = refs[3 * n:]
    d, z = lax.axis_index("dp"), lax.axis_index("mp")
    loads = [pltpu.make_async_copy(ins[i], own[i], lsem.at[i]) for i in range(n)]
    enter(d, z, nd, nz, bits)
    for c in loads:
        c.start()
    chunks = [Gather(ins[i], outs[i], r0, rows, order, d, z, nz, (zs, zr, ps, pr), c) for c, (i, r0, rows, order, _) in enumerate(plan)]
    last = max(g.events() + p[4] for g, p in zip(chunks, plan))
    for t in range(last):
        for g, p in zip(chunks, plan):
            if 0 <= t - p[4] < g.events():
                g.event(t - p[4])
        if t == 2:
            for c in loads:
                c.wait()
            stores = [pltpu.make_async_copy(own[i], outs[i].at[z], lsem.at[i]) for i in range(n)]
            for c in stores:
                c.start()
    for c in stores:
        c.wait()
    for g in chunks:
        g.finish()

def gather_weights(shards, plan, nd, nz, bits):
    n = len(shards)
    nc = len(plan)
    sem = pltpu.SemaphoreType.DMA
    return pl.pallas_call(
        functools.partial(gather_kernel, plan, nd, nz, bits),
        out_shape=tuple(jax.ShapeDtypeStruct((nz,) + a.shape, a.dtype) for a in shards),
        in_specs=[pl.BlockSpec(memory_space=pl.ANY)] * n,
        out_specs=tuple([pl.BlockSpec(memory_space=pl.ANY)] * n),
        scratch_shapes=[pltpu.VMEM(a.shape, a.dtype) for a in shards]
        + [sem((nc, 2, nz - 1)), sem((nc, 2, nz - 1)), sem((nc, 3, 2, nz - 1)), sem((nc, 3, 2, nz - 1)), sem((n,))],
        compiler_params=pltpu.CompilerParams(collective_id=0, has_side_effects=True),
    )(*shards)

class Reduce:
    def __init__(self, part, keep, halves, recvs, ups, downs, extra, result, row0, rows, order, d, z, nz, bits, sems, base):
        self.part, self.keep, self.core_in = part, keep, halves
        self.recvs, self.ups, self.downs, self.extra, self.result = recvs, ups, downs, extra, result
        self.row0, self.rows, self.order = row0, rows, order
        self.d, self.z, self.nz = d, z, nz
        self.bits = bits
        self.ss, self.rs = sems
        self.base = base
        self.slot = 0
        self.pending = []
        self.steps = []
        self.build()

    def remote(self, src, dst, to, cond=True):
        s = self.slot
        self.slot += 1
        copy = lambda: pltpu.make_async_remote_copy(src, dst, self.ss.at[self.base, s], self.rs.at[self.base, s], device_id=to, device_id_type=MESH)
        self.pending.append((cond, copy))
        return copy

    def build(self):
        d, z, nz = self.d, self.z, self.nz
        half = self.rows // 2
        cb = self.bits[0]
        mine = bit_of(d, cb)
        lo = pl.multiple_of(self.row0 + mine * half, 16)
        ot = pl.multiple_of(self.row0 + (1 - mine) * half, 16)
        send = self.remote(self.part.at[:, pl.ds(ot, half), :], self.core_in, (flip(d, cb), z))
        load = lambda: pltpu.make_async_copy(self.part.at[:, pl.ds(lo, half), :], self.keep, self.ss.at[self.base, self.slots_max - 1])
        def first():
            send().start()
            load().start()
        def arrive():
            load().wait()
            send().wait_recv()
            add_rows(self.keep, self.core_in, nz, half)
        self.steps.append(first)
        prev = arrive
        start, size, whole = jnp.int32(0), half, True
        taken = []
        for op in self.order:
            if op == "z":
                for h in range(nz):
                    self.steps.append(functools.partial(self.zhop, h, start, size, prev if h == 0 else None))
                self.zbase = self.slot
                self.slot += 2 * nz
                prev = None
                whole = False
                zprep = self.zcopies(start, size)
                self.zc = zprep
            else:
                size //= 2
                m = bit_of(d, op)
                keep0 = pl.multiple_of(start + m * size, 16)
                send0 = pl.multiple_of(start + (1 - m) * size, 16)
                buf = self.recvs[op]
                if whole:
                    src = self.keep.at[:, pl.ds(send0, size), :]
                    dst = buf
                else:
                    src = self.keep.at[z, pl.ds(send0, size), :]
                    dst = buf.at[0]
                cp = self.remote(src, dst, (flip(d, op), z))
                def step(prev=prev, cp=cp):
                    if prev is not None:
                        prev()
                    cp().start()
                self.steps.append(step)
                def prev(cp=cp, keep0=keep0, size=size, whole=whole, buf=buf):
                    cp().wait_recv()
                    if whole:
                        add_rows(self.keep.at[:, pl.ds(keep0, size), :], buf, nz, size)
                    else:
                        add_plain(self.keep.at[z, pl.ds(keep0, size), :], buf.at[0], size)
                taken.append(op)
                start = keep0
        for e, b in enumerate(self.bits[3:]):
            cp = self.remote(self.keep.at[z, pl.ds(start, size), :], self.extra.at[e], (flip(d, b), z))
            def step(prev=prev, cp=cp):
                if prev is not None:
                    prev()
                cp().start()
            self.steps.append(step)
            def prev(cp=cp, e=e, start=start, size=size):
                cp().wait_recv()
                cp().wait_send()
                add_plain(self.keep.at[z, pl.ds(start, size), :], self.extra.at[e], size)
            self.pending.pop()
        pos = pl.multiple_of(mine * half + start, 16)
        def place(prev=prev, pos=pos, start=start, size=size):
            if prev is not None:
                prev()
            copy_plain(self.result.at[pl.ds(pos, size), :], self.keep.at[z, pl.ds(start, size), :], size)
        prev = place
        for op in list(reversed(taken)) + [cb]:
            m = bit_of(d, op)
            win = self.result.at[pl.ds(pos, size), :]
            cp = self.remote(win, win, (flip(d, op), z))
            def step(prev=prev, cp=cp):
                prev()
                cp().start()
            self.steps.append(step)
            prev = lambda cp=cp: cp().wait_recv()
            pos = pl.multiple_of(pos - m * size, 16)
            size *= 2
        self.steps.append(prev)

    slots_max = 24

    def zcopies(self, start, size):
        out = {}
        d, z, nz = self.d, self.z, self.nz
        rows = pl.ds(start, size)
        for t in range(nz):
            su, sd = self.zbase + t, self.zbase + nz + t
            if t >= 1:
                out["u", t] = lambda t=t, s=su: pltpu.make_async_remote_copy(self.keep.at[t, rows, :], self.ups.at[t - 1], self.ss.at[self.base, s], self.rs.at[self.base, s], device_id=(d, z + 1), device_id_type=MESH)
                self.pending.append((z < t, out["u", t]))
            if t <= nz - 2:
                out["d", t] = lambda t=t, s=sd: pltpu.make_async_remote_copy(self.keep.at[t, rows, :], self.downs.at[t], self.ss.at[self.base, s], self.rs.at[self.base, s], device_id=(d, z - 1), device_id_type=MESH)
                self.pending.append((z > t, out["d", t]))
        return out

    def zhop(self, h, start, size, prev):
        z, nz = self.z, self.nz
        if prev is not None:
            prev()
        rows = pl.ds(start, size)
        @pl.when(z == h)
        def _():
            for t in range(nz - 1, h - 1, -1):
                if t == 0:
                    continue
                if h > 0:
                    self.zc["u", t]().wait_recv()
                    add_plain(self.keep.at[t, rows, :], self.ups.at[t - 1], size)
                if t > h:
                    self.zc["u", t]().start()
        me = nz - 1 - h
        @pl.when(z == me)
        def _():
            for t in range(0, me + 1):
                if t == nz - 1:
                    continue
                if h > 0:
                    self.zc["d", t]().wait_recv()
                    add_plain(self.keep.at[t, rows, :], self.downs.at[t], size)
                if t < me:
                    self.zc["d", t]().start()

    def finish(self):
        for cond, cp in self.pending:
            when(cond, lambda: cp().wait_send())

def add_plain(dst, src, rows):
    step = 16
    def body(i, c):
        r = pl.ds(pl.multiple_of(i * step, step), step)
        dst[r, :] = dst[r, :] + src[r, :]
        return c
    lax.fori_loop(0, rows // step, body, 0, unroll=min(4, rows // step))

def copy_plain(dst, src, rows):
    dst[...] = src[...]

def add_rows(dst, src, nz, rows):
    for t in range(nz):
        add_plain(dst.at[t], src.at[t], rows)

def reduce_kernel(plan, shapes, nz, bits, *refs):
    n = len(shapes)
    nc = len(plan)
    ins, outs = refs[:n], refs[n:2 * n]
    it = iter(refs[2 * n:])
    results = [next(it) for _ in range(n)]
    d, z = lax.axis_index("dp"), lax.axis_index("mp")
    bufs = []
    for _ in plan:
        keep, core_in = next(it), next(it)
        recvs = {b: next(it) for b in bits[1:3]}
        ups, downs = next(it), next(it)
        extra = next(it) if len(bits) > 3 else None
        bufs.append((keep, core_in, recvs, ups, downs, extra))
    ss, rs, lsem = it
    enter(d, z, None, nz, bits)
    chunks = []
    for c, (i, r0, rows, order, _) in enumerate(plan):
        chunks.append(Reduce(ins[i], *bufs[c], results[i].at[pl.ds(r0, rows), :], r0, rows, order, d, z, nz, bits, (ss, rs), c))
    last = max(len(c.steps) + p[4] for c, p in zip(chunks, plan))
    for t in range(last):
        for c, p in zip(chunks, plan):
            if 0 <= t - p[4] < len(c.steps):
                c.steps[t - p[4]]()
    stores = [pltpu.make_async_copy(results[i], outs[i], lsem.at[i]) for i in range(n)]
    for s in stores:
        s.start()
    for c in chunks:
        c.finish()
    for s in stores:
        s.wait()

def window_rows(rows, order, op):
    size = rows // 2
    for o in order:
        if o == "z":
            if op == "z":
                return size
        else:
            size //= 2
            if o == op:
                return size
    return size

def reduce_grads(parts, plan, nz, bits):
    sem = pltpu.SemaphoreType.DMA
    n, nc = len(parts), len(plan)
    shapes = [a.shape[1:] for a in parts]
    dt = parts[0].dtype
    scratch = [pltpu.VMEM(s, dt) for s in shapes]
    for i, r0, rows, order, _ in plan:
        C = shapes[i][1]
        scratch += [pltpu.VMEM((nz, rows // 2, C), dt)] * 2
        for b in bits[1:3]:
            lead = nz if order.index(b) < order.index("z") else 1
            scratch.append(pltpu.VMEM((lead, window_rows(rows, order, b), C), dt))
        scratch += [pltpu.VMEM((nz - 1, window_rows(rows, order, "z"), C), dt)] * 2
        if len(bits) > 3:
            scratch.append(pltpu.VMEM((len(bits) - 3, window_rows(rows, order, None), C), dt))
    return pl.pallas_call(
        functools.partial(reduce_kernel, plan, shapes, nz, bits),
        out_shape=tuple(jax.ShapeDtypeStruct(s, dt) for s in shapes),
        in_specs=[pl.BlockSpec(memory_space=pl.ANY)] * n,
        out_specs=tuple([pl.BlockSpec(memory_space=pl.ANY)] * n),
        scratch_shapes=scratch + [sem((nc, Reduce.slots_max)), sem((nc, Reduce.slots_max)), sem((n,))],
        compiler_params=pltpu.CompilerParams(collective_id=1, has_side_effects=True, vmem_limit_bytes=60 << 20),
    )(*parts)

HEAD = 64
epsilon = 1e-06

def norm_forward(hidden_sum, gain, shift):
    row_mean = jnp.mean(hidden_sum, -1, keepdims=True)
    centred = hidden_sum - row_mean
    inverse = lax.rsqrt(jnp.mean(centred * centred, -1, keepdims=True) + epsilon)
    normed = centred * inverse
    return (normed * gain.astype(jnp.float32) + shift.astype(jnp.float32), normed, inverse)

def norm_backward(grad_out, normed, inverse, gain):
    scaled = grad_out * gain.astype(jnp.float32)
    grad_in = inverse * (scaled - jnp.mean(scaled, -1, keepdims=True) - normed * jnp.mean(scaled * normed, -1, keepdims=True))
    return (grad_in, jnp.sum(grad_out * normed, axis=(0, 1)), jnp.sum(grad_out, axis=(0, 1)))

def heads(flat):
    return flat.reshape(flat.shape[:-1] + (flat.shape[-1] // HEAD, HEAD))

def ein(form, *ops):
    return jnp.einsum(form, *ops, preferred_element_type=jnp.float32)

score_scale = 1.0 / math.sqrt(HEAD)

def probabilities(q, k, valid):
    scores = ein("ziqhe,zikhe->zihqk", heads(q), heads(k)) * score_scale
    if valid is not None:
        scores = jnp.where(valid, scores, -1e30)
    highest = jnp.max(scores, -1, keepdims=True)
    log_total = highest + jnp.log(jnp.sum(jnp.exp(scores - highest), -1, keepdims=True))
    return jnp.exp(scores - log_total)

def attend(prob, v, shape):
    mixed = ein("zihqk,zikhe->ziqhe", prob.astype(jnp.bfloat16), heads(v))
    return mixed.reshape(shape).astype(jnp.bfloat16)

def attend_backward(q, k, v, prob, grad_mixed):
    gm = heads(grad_mixed)
    grad_v = ein("zihqk,ziqhe->zikhe", prob.astype(jnp.bfloat16), gm)
    grad_prob = ein("ziqhe,zikhe->zihqk", gm, heads(v))
    delta = jnp.sum(prob * grad_prob, -1, keepdims=True)
    gs = (prob * (grad_prob - delta)).astype(jnp.bfloat16)
    gq = ein("zihqk,zikhe->ziqhe", gs, heads(k)) * score_scale
    gk = ein("zihqk,ziqhe->zikhe", gs, heads(q)) * score_scale
    return (gq.reshape(q.shape).astype(jnp.bfloat16), gk.reshape(k.shape).astype(jnp.bfloat16), grad_v.reshape(v.shape).astype(jnp.bfloat16))

def plane_bits(nd):
    return tuple(range(nd.bit_length() - 1))

def per_device(nd, nz, text_states, patch_states, patch_rows, cotangent, w_attn, attn_bias, w_attn_out, w_query, w_patch, cross_bias, w_cross_out, w_hidden, hidden_bias, w_output, out_bias, norm_gain, norm_shift):
    bf, f32 = jnp.bfloat16, jnp.float32
    bits = plane_bits(nd)
    z = lax.axis_index("mp")
    ni = text_states.shape[0]
    hw = w_query.shape[1]
    W_A = jnp.concatenate([w_attn[0], w_attn[1], w_attn[2], w_query], 1)
    W_B = jnp.concatenate([w_patch[0], w_patch[1]], 1)
    W_O = jnp.concatenate([w_attn_out, w_cross_out], 0)
    shards = (W_A, W_B, W_O, w_hidden, w_output)
    GA, GB, GO, GH, GW = gather_weights(shards, gather_plan(shards, bits), nd, nz, bits[:3])
    full_bias = lax.all_gather(jnp.concatenate([attn_bias.reshape(-1), cross_bias.reshape(-1), hidden_bias]).astype(f32), "mp", axis=0)
    ab = full_bias[:, :2 * hw].reshape(nz, 2, 1, 1, hw)
    cb = full_bias[:, 2 * hw:4 * hw].reshape(nz, 2, 1, 1, hw)
    hb = full_bias[:, 4 * hw:].reshape(nz, 1, 1, -1)
    bias_rows = out_bias.astype(f32)
    x = text_states
    proj = ein("ild,zdc->zilc", x, GA[..., :3 * hw])
    q = (proj[..., :hw] + ab[:, 0]).astype(bf)
    k = proj[..., hw:2 * hw].astype(bf)
    v = (proj[..., 2 * hw:] + ab[:, 1]).astype(bf)
    self_prob = probabilities(q, k, None)
    self_mixed = attend(self_prob, v, q.shape)
    self_sum = ein("zilc,zcd->ild", self_mixed, GO[:, :hw])
    first_norm, n0, i0 = norm_forward(x.astype(f32) + self_sum + bias_rows[0], norm_gain[0], norm_shift[0])
    first = first_norm.astype(bf)
    cq = (ein("ild,zdc->zilc", first, GA[..., 3 * hw:]) + cb[:, 0]).astype(bf)
    kv = ein("ipc,zcd->zipd", patch_states, GB)
    ck = kv[..., :hw].astype(bf)
    cv = (kv[..., hw:] + cb[:, 1]).astype(bf)
    rows = lax.dynamic_slice_in_dim(patch_rows, z * ni, ni)
    positions = lax.broadcasted_iota(jnp.int32, (ni, patch_states.shape[1]), 1)
    valid = (positions < rows[:, None])[None, :, None, None, :]
    cross_prob = probabilities(cq, ck, valid)
    cross_mixed = attend(cross_prob, cv, cq.shape)
    cross_sum = ein("zilc,zcd->ild", cross_mixed, GO[:, hw:])
    second_norm, n1, i1 = norm_forward(first.astype(f32) + cross_sum + bias_rows[1], norm_gain[1], norm_shift[1])
    second = second_norm.astype(bf)
    pre = ein("ild,zdf->zilf", second, GH) + hb
    act, pull = jax.vjp(lambda p: jax.nn.gelu(p, approximate=False), pre)
    hid = act.astype(bf)
    ffn_sum = ein("zilf,zfd->ild", hid, GW)
    layer_out, n2, i2 = norm_forward(second.astype(f32) + ffn_sum + bias_rows[2], norm_gain[2], norm_shift[2])
    grad_third, gain2, shift2 = norm_backward(cotangent.astype(f32), n2, i2, norm_gain[2])
    g3 = grad_third.astype(bf)
    dW = ein("zilf,ild->zfd", hid, g3).astype(bf)
    dpre = pull(ein("ild,zfd->zilf", g3, GW))[0].astype(bf)
    dH = ein("ild,zilf->zdf", second, dpre).astype(bf)
    dhb = jnp.sum(dpre, axis=(1, 2), dtype=f32)
    grad_second, gain1, shift1 = norm_backward(grad_third + ein("zilf,zdf->ild", dpre, GH), n1, i1, norm_gain[1])
    g2 = grad_second.astype(bf)
    dO2 = ein("zilc,ild->zcd", cross_mixed, g2).astype(bf)
    cmg = ein("ild,zcd->zilc", g2, GO[:, hw:]).astype(bf)
    dcq, dck, dcv = attend_backward(cq, ck, cv, cross_prob, cmg)
    dkv = jnp.concatenate([dck, dcv], -1)
    dB = ein("ipc,ziph->zch", patch_states, dkv).astype(bf)
    dcqb = jnp.sum(dcq, axis=(1, 2), dtype=f32)
    dcvb = jnp.sum(dcv, axis=(1, 2), dtype=f32)
    patch_grad = ein("ziph,zch->ipc", dkv, GB)
    grad_first, gain0, shift0 = norm_backward(grad_second + ein("zilc,zdc->ild", dcq, GA[..., 3 * hw:]), n0, i0, norm_gain[0])
    g1 = grad_first.astype(bf)
    dO1 = ein("zilc,ild->zcd", self_mixed, g1).astype(bf)
    smg = ein("ild,zcd->zilc", g1, GO[:, :hw]).astype(bf)
    dq, dk, dv = attend_backward(q, k, v, self_prob, smg)
    dqkv = jnp.concatenate([dq, dk, dv], -1)
    dA = jnp.concatenate([ein("ild,zilc->zdc", x, dqkv).astype(bf), ein("ild,zilc->zdc", first, dcq).astype(bf)], -1)
    dO = jnp.concatenate([dO1, dO2], 1)
    text_grad = grad_first + ein("zilc,zdc->ild", dqkv, GA[..., :3 * hw])
    small = jnp.concatenate([
        jnp.sum(grad_first, axis=(0, 1)), jnp.sum(grad_second, axis=(0, 1)), jnp.sum(grad_third, axis=(0, 1)),
        gain0, gain1, gain2, shift0, shift1, shift2,
        jnp.concatenate([jnp.sum(dq, axis=(1, 2), dtype=f32), jnp.sum(dv, axis=(1, 2), dtype=f32), dcqb, dcvb, dhb], 1).reshape(-1)])
    small = lax.psum(small, ("dp", "mp"))
    D = x.shape[-1]
    grads = (dA, dB, dO, dH, dW)
    RA, RB, RO, RH, RW = reduce_grads(grads, reduce_plan(shards, bits), nz, bits)
    RA, RB, RO, RH, RW = (r.astype(f32) for r in (RA, RB, RO, RH, RW))
    rep = small[:9 * D].reshape(3, 3, D)
    own = lax.dynamic_index_in_dim(small[9 * D:].reshape(nz, -1), z, 0, False)
    return (
        layer_out, text_grad, patch_grad,
        jnp.stack([RA[:, t * hw:(t + 1) * hw] for t in range(3)]),
        own[:2 * hw].reshape(2, hw), RO[:hw], RA[:, 3 * hw:],
        jnp.stack([RB[:, :hw], RB[:, hw:]]),
        own[2 * hw:4 * hw].reshape(2, hw), RO[hw:], RH, own[4 * hw:], RW,
        rep[0], rep[1], rep[2],
    )

def gather_plan(shards, bits):
    c, x, y = bits[:3]
    a, b, o, h, w = (s.shape[0] for s in shards)
    return ((0, 0, a, (x, y, c), 0), (1, 0, b, (y, x, c), 0), (2, 0, o, (x, c), 0), (3, 0, h, (y, x, c), 0), (4, 0, w, (y, c), 0))

def reduce_plan(shards, bits):
    c, x, y = bits[:3]
    a, b, o, h, w = (s.shape[0] for s in shards)
    return ((4, 0, w, (y, x, "z"), 0), (3, 0, h, (x, y, "z"), 1), (2, 0, o, ("z", x, y), 2), (1, 0, b, (y, x, "z"), 3), (0, 0, a, (x, y, "z"), 4))

def solution(mesh):
    nd, nz = mesh.shape["dp"], mesh.shape["mp"]
    rows = P(("dp", "mp"), None, None)
    return jax.shard_map(
        functools.partial(per_device, nd, nz),
        mesh=mesh,
        in_specs=(rows, rows, P("dp"), rows, P(None, None, "mp"), P(None, "mp"), P("mp", None), P(None, "mp"), P(None, None, "mp"), P(None, "mp"), P("mp", None), P(None, "mp"), P("mp"), P("mp", None), P(), P(), P()),
        out_specs=(rows, rows, rows, P(None, None, "mp"), P(None, "mp"), P("mp", None), P(None, "mp"), P(None, None, "mp"), P(None, "mp"), P("mp", None), P(None, "mp"), P("mp"), P("mp", None), P(), P(), P()),
        check_vma=False,
    )
```

time: 907 us -> 510 us (0.56)
  waiting for transfers between devices: 534 us -> 0 us
  Pallas kernels: 0 us -> 270 us
  blocking collectives: 192 us -> 63.5 us
  between operations: 15.3 us -> 2.04 us
    reduce_scatter x7 -> x0, waiting for transfers between devices: 318 us -> none  [the longest x6 202 us: row_sum(): lax.psum_scatter(term_fn(jnp.int32(0), local_count * lax.axis_size('mp'))...]
    pallas_call x0 -> x2, Pallas kernels: none -> 270 us  [the longest x1 193 us: reduce_grads(): pl.pallas_call(functools.partial(reduce_kernel, plan, shapes, nz, bits),...]
    psum x1 -> x0, waiting for transfers between devices: 147 us -> none  [per_device(): lax.psum((grad_attn, grad_attn_bias, grad_attn_out, grad_query, grad_patc...]
    all_gather x6 -> x1, blocking collectives: 134 us -> 14.8 us  [per_device(): lax.all_gather(jnp.concatenate([attn_bias.reshape(-1), cross_bias.reshape...]
    all_gather x1 -> x0, waiting for transfers between devices: 68.5 us -> none  [per_device(): group_patches = lax.all_gather(patch_states, 'mp', axis=0, tiled=True)]
    unnamed x187 -> x168, local copies, waits for them, and re-layouts: 30.1 us -> 15.1 us
    convert_element_type x18 -> x17, local copies, waits for them, and re-layouts: 17.1 us -> 27.5 us  [the longest x1 6.32 us: per_device(): ein('ild,zilc->zdc', x, dqkv).astype(bf)]
    concatenate x0 -> x5, other arithmetic: none -> 10.4 us  [the longest x1 5.28 us: per_device(): jnp.concatenate([ein('ild,zilc->zdc', x, dqkv).astype(bf), ein('ild,zilc-...]
  transfers between devices with their start and end apart: 9 -> 0, of which waited for: 8 -> 0; matrix products, arithmetic and copies ran while one was open for 5% -> 0% of each run, Pallas kernels for 0% -> 0%
where the time goes in v1:
time: 510 us; the launch traced here: 503 us
  Pallas kernels  270 us (53%)
  matrix products  77.7 us (15%)
  local copies, waits for them, and re-layouts  64.5 us (13%)
  blocking collectives  63.5 us (12%)
  other arithmetic  25.9 us (5%)
    pallas_call x1, Pallas kernels, reduce_grads(): pl.pallas_call(functools.partial(reduce_kernel, plan, shapes, nz, bits),...  193 us
    dot_general x33, matrix products, ein(): return jnp.einsum(form, *ops, preferred_element_type=jnp.float32)  77.7 us
    pallas_call x1, Pallas kernels, gather_weights(): pl.pallas_call(functools.partial(gather_kernel, plan, nd, nz, bits), out_...  76.4 us
    psum x1, blocking collectives, per_device(): small = lax.psum(small, ('dp', 'mp'))  48.7 us
    unnamed x168, local copies, waits for them, and re-layouts  15.1 us
    all_gather x1, blocking collectives, per_device(): lax.all_gather(jnp.concatenate([attn_bias.reshape(-1), cross_bias.reshape...  14.8 us

profile of v1, /device:TPU:0, one launch (start us, length us, event | category | flops | bytes accessed | tf_op | source)
XLA Modules:
  0.0 503.3 jit_solution(8635942921899307895)
XLA Ops:
  4.2 14.8 %all-gather = f32[4,1,1536]{2,1,0:T(1,128)S(1)} all-gather(f32[1,1,1536]{2,1,0:T(1,128)S(1)} %fusion.166), channel_id=1, replica_groups=mesh['dp'=8,'mp'=4] {'mp'}, dimensions={0}, use_global_device_ids=true | all-gather | bytes 30720 | tf_op jit(solution)/shard_map/all_gather | solution.py:450
  19.0 1.1 copy.184
  20.1 1.2 fusion.177
  21.9 1.5 pad_maximum_fusion.5.refs_0_
  23.9 1.2 pad_maximum_fusion.9.refs_1_
  25.9 76.4 %shard_map.288 = (bf16[4,768,768]{2,1,0:T(8,128)(2,1)}, bf16[4,1024,384]{2,1,0:T(8,128)(2,1)}, bf16[4,384,768]{2,1,0:T(8,128)(2,1)}, bf16[4,768,768]{2,1,0:T(8,128)(2,1)}, bf16[4,768,768]{2,1,0:T(8,128)(2,1)}) custom-call(bf16[768,768]{1,0:T(8,128)(2,1)} %pad_maximum_fusion.5.refs_0_, bf16[1024,384]{1,0:T(8,128)(2,1)} %pad_maximum_fusion.9.refs_1_, ...), custom_call_target="tpu_custom_call" | custom-call | tf_op jit(solution)/shard_map/pallas_call | solution.py:143
  102.3 5.9 %fusion.21 = f32[4,4,145,384]{3,2,1,0:T(8,128)} fusion(bf16[4,1024,384]{2,1,0:T(8,128)(2,1)} %get-tuple-element.28, bf16[4,145,1024]{2,0,1:T(4,128)(2,1)S(1)} %copy-done.62), kind=kOutput, calls=%fused_computation.37 | convolution fusion | flops 1824522240 | bytes 7897088 | tf_op jit(solution)/shard_map/ipc,zcd->zipd/dot_general | solution.py:410
  108.3 2.4 fusion.20
  110.8 2.2 copy.194
  113.0 1.8 slice.341
  114.8 1.7 copy.196
  116.5 2.9 fusion.53
  120.9 1.8 reshape.336
  124.6 1.9 fusion.185
  127.7 2.2 fusion.105
  131.1 2.2 fusion.186
  135.4 1.1 copy.198
  136.5 1.6 convert_element_type.322
  138.1 1.9 fusion.187
  140.5 7.1 %fusion.33 = (bf16[4,4,40,768]{3,2,1,0:T(8,128)(2,1)S(1)}, f32[4,4,40,768]{3,2,1,0:T(8,128)S(1)}, f32[4,768,4,40]{1,3,2,0:T(8,128)S(1)}) fusion(f32[4,768]{1,0:T(4,128)S(1)} %slice.254, bf16[4,40,768]{2,1,0:T(8,128)(2,1)S(1)} %add_convert_fusion, bf16[4,768,768]{2,1,0:T(8,128)(2,1)} %get-tuple-element.29), kind=kOutput, calls=%fused_computation.54 | convolution fusion | flops 787415040 | bytes 9891840 | tf_op jit(solution)/shard_map/ild,zdf->zilf/dot_general | solution.py:410
  147.7 1.1 fusion.188
  149.3 2.7 convert_reduce_fusion.1
  152.0 2.4 multiply_reduce_fusion.2
  154.5 1.8 fusion.129
  157.1 1.2 fusion.108
  158.4 2.2 reshape.342
  160.6 2.6 multiply_reduce_fusion
  165.5 1.1 copy.200
  166.6 2.2 convert_element_type.343
  168.9 3.4 multiply_reduce_fusion.3
  173.9 1.2 fusion.109
  175.1 2.2 reshape.343
  177.3 1.5 convert_reduce_fusion.3
  178.8 1.1 copy.257
  179.9 2.4 reshape.389
  182.3 1.7 multiply_reduce_fusion.1
  186.2 1.1 reshape.388
  187.3 1.8 convert_reduce_fusion.4
  189.4 1.1 reshape.387
  190.5 4.7 fusion.89
  195.2 2.0 convert_reduce_fusion
  197.3 2.7 copy.218
  200.0 1.7 multiply_convert_fusion
  201.7 1.6 copy.217
  203.4 4.8 fusion.46
  208.2 2.9 copy.224
  211.1 1.5 bitcast_convert_fusion.6
  212.7 1.7 copy.220
  214.5 3.2 bitcast_convert_fusion.2
  217.7 6.3 %copy.219 = bf16[4,576,768]{1,2,0:T(8,128)(2,1)} copy(bf16[4,576,768]{2,1,0:T(8,128)(2,1)} %bitcast_convert_fusion.2) | data formatting | bytes 7077888 | tf_op jit(solution)/shard_map/convert_element_type | solution.py:504
  224.1 5.3 %pad_maximum_fusion.refs_0_ = bf16[4,768,768]{2,1,0:T(8,128)(2,1)} fusion(bf16[4,768,192]{2,1,0:T(8,128)(2,1)S(1)} %bitcast.382, bf16[4,768,576]{2,1,0:T(8,128)(2,1)} %bitcast.377), kind=kLoop, calls=%fused_computation.5 | loop fusion | flops 9437184 | bytes 9437184 | tf_op jit(solution)/shard_map/concatenate | solution.py:504
  229.4 4.7 fusion.15.refs_1_
  235.8 1.6 pad_maximum_fusion.1.refs_2_
  237.5 3.6 fusion.refs_3_
  241.1 3.8 bitcast_convert_fusion.refs_4_
  244.9 193.3 %shard_map.289 = (bf16[768,768]{1,0:T(8,128)(2,1)}, bf16[1024,384]{1,0:T(8,128)(2,1)}, bf16[384,768]{1,0:T(8,128)(2,1)}, bf16[768,768]{1,0:T(8,128)(2,1)}, bf16[768,768]{1,0:T(8,128)(2,1)}) custom-call(bf16[4,768,768]{2,1,0:T(8,128)(2,1)} %pad_maximum_fusion.refs_0_, bf16[4,1024,384]{2,1,0:T(8,128)(2,1)} %fusion.15.refs_1_, ...), custom_call_target="tpu_custom_call" | custom-call | tf_op jit(solution)/shard_map/pallas_call | solution.py:382
  438.2 1.4 convert_element_type.374
  440.2 1.8 copy.225
  442.6 48.7 %psum.7 = f32[13056]{0:T(1024)S(1)} all-reduce(f32[13056]{0:T(1024)S(1)} %constant_dynamic-update-slice_fusion), channel_id=1, replica_groups=mesh['dp'=8,'mp'=4] {'dp','mp'}, use_global_device_ids=true, to_apply=%region_32.33 | all-reduce | flops 13056 | bytes 104448 | tf_op jit(solution)/shard_map/psum | solution.py:511
  492.2 1.1 fusion.179
  493.4 1.1 copy.226
  495.1 1.7 copy.227
  497.5 1.6 convert_element_type.382
  499.7 1.6 convert_element_type.383
  (248 shorter events, 28.6 us)
Async XLA Ops:
  21.5 1.9 copy-start.26
  23.4 1.6 copy-start.41
  23.4 1.6 copy-start.42
  25.9 76.4 %copy-start.62 = (bf16[4,145,1024]{2,0,1:T(4,128)(2,1)S(1)}, bf16[4,145,1024]{2,0,1:T(4,128)(2,1)}, u32[]{:S(2)}) copy-start(bf16[4,145,1024]{2,0,1:T(4,128)(2,1)} %param.18) | copy-start | bytes 3563524
  114.8 1.7 copy-start.64
  120.5 2.9 copy-start.8
  120.9 2.5 copy-start.16
  122.7 1.2 copy-start.6
  123.4 1.2 copy-start.65
  124.2 2.3 copy-start.48
  124.2 3.0 copy-start.49
  124.6 3.0 copy-start.32
  127.7 3.3 copy-start.43
  127.7 3.3 copy-start.67
  133.3 1.4 copy-start.1
  135.4 2.7 copy-start.59
  138.1 9.5 %copy-start.34 = (bf16[4,4,40,192]{3,2,1,0:T(8,128)(2,1)}, bf16[4,4,40,192]{3,2,1,0:T(8,128)(2,1)S(1)}, u32[]{:S(2)}) copy-start(bf16[4,4,40,192]{3,2,1,0:T(8,128)(2,1)S(1)} %convert_element_type.322) | copy-start | bytes 737284
  138.1 9.5 %slice-start = ((s8[4718592]{0:T(1024)(128)(4,1)}), s8[4194304]{0:T(1024)(128)(4,1)S(1)}, s32[]{:S(2)}) async-start(s8[4718592]{0:T(1024)(128)(4,1)} %bitcast.385), calls=%async_computation | async-start | bytes 8388608
  140.4 7.2 %copy-start.14 = (bf16[4,40,768]{2,1,0:T(8,128)(2,1)}, bf16[4,40,768]{2,1,0:T(8,128)(2,1)S(1)}, u32[]{:S(2)}) copy-start(bf16[4,40,768]{2,1,0:T(8,128)(2,1)S(1)} %add_convert_fusion) | copy-start | bytes 737284
  140.4 7.2 %slice-start.1 = ((s8[4718592]{0:T(1024)(128)(4,1)}), s8[524288]{0:T(1024)(128)(4,1)S(1)}, s32[]{:S(2)}) async-start(s8[4718592]{0:T(1024)(128)(4,1)} %bitcast.385), calls=%async_computation.1 | async-start | bytes 1048576
  147.6 1.2 copy-start.22
  147.6 1.4 copy-start.24
  147.7 4.4 slice-start.2
  149.3 5.2 %copy-start.51 = (f32[4,40]{1,0:T(4,128)}, f32[4,40]{1,0:T(4,128)S(1)}, u32[]{:S(2)}) copy-start(f32[4,40]{1,0:T(4,128)S(1)} %broadcast_multiply_fusion.4) | copy-start | bytes 1924
  149.3 5.2 %copy-start.53 = (f32[4,40]{1,0:T(4,128)}, f32[4,40]{1,0:T(4,128)S(1)}, u32[]{:S(2)}) copy-start(f32[4,40]{1,0:T(4,128)S(1)} %broadcast_multiply_fusion.5) | copy-start | bytes 1924
  149.3 2.8 slice-start.3
  152.0 2.4 copy-start.10
  152.0 2.5 copy-start.47
  154.5 2.7 copy-start.60
  163.2 1.4 copy-start
  168.8 3.4 copy-start.5
  168.9 5.0 copy-start.61
  187.3 3.2 copy-start.37
  190.5 4.7 copy-start.9
  197.3 2.7 copy-start.3
  208.2 3.0 copy-start.36
  208.2 3.0 copy-start.44
  212.7 1.8 copy-start.38
  212.7 1.8 copy-start.39
  212.7 1.8 copy-start.40
  212.7 1.8 copy-start.66
  224.0 5.3 %copy-start.18 = (bf16[4,4,145,192]{3,2,0,1:T(8,128)(2,1)S(1)}, bf16[4,4,145,192]{3,2,0,1:T(8,128)(2,1)}, u32[]{:S(2)}) copy-start(bf16[4,4,145,192]{3,2,0,1:T(8,128)(2,1)} %copy.218) | copy-start | bytes 2672644
  224.0 5.3 %copy-start.19 = (bf16[4,4,145,192]{3,2,0,1:T(8,128)(2,1)S(1)}, bf16[4,4,145,192]{3,2,0,1:T(8,128)(2,1)}, u32[]{:S(2)}) copy-start(bf16[4,4,145,192]{3,2,0,1:T(8,128)(2,1)} %copy.217) | copy-start | bytes 2672644
  224.1 5.3 %copy-start.63 = (bf16[4,145,1024]{2,0,1:T(4,128)(2,1)S(1)}, bf16[4,145,1024]{2,0,1:T(4,128)(2,1)}, u32[]{:S(2)}) copy-start(bf16[4,145,1024]{2,0,1:T(4,128)(2,1)} %param.18) | copy-start | bytes 3563524
  229.4 4.7 copy-start.29
  229.4 4.7 copy-start.35
  235.8 1.6 copy-start.11
  235.8 1.7 copy-start.15
  237.5 3.6 copy-start.23
  237.5 3.6 copy-start.25
  237.5 3.6 copy-start.52
  237.5 3.6 copy-start.54
  440.1 1.9 copy-start.46
  440.1 1.9 copy-start.45
  440.1 1.9 copy-start.58
  440.1 1.9 copy-start.56
  440.1 2.0 copy-start.57
  440.1 2.0 copy-start.55
  440.2 2.3 copy-start.50
  440.2 52.0 %copy-start.13 = (bf16[384,768]{1,0:T(8,128)(2,1)S(1)}, bf16[384,768]{1,0:T(8,128)(2,1)}, u32[]{:S(2)}) copy-start(bf16[384,768]{1,0:T(8,128)(2,1)} %get-tuple-element.32) | copy-start | bytes 1769476
  442.0 51.3 %copy-start.12 = (bf16[768,768]{1,0:T(8,128)(2,1)S(1)}, bf16[768,768]{1,0:T(8,128)(2,1)}, u32[]{:S(2)}) copy-start(bf16[768,768]{1,0:T(8,128)(2,1)} %get-tuple-element.31) | copy-start | bytes 3538948
  493.2 1.3 copy-start.27
  495.1 2.4 copy-start.21
  496.8 2.9 copy-start.20
  (8 other events, 7.5 us)

commit v2 on v1

v2 whole, which is shorter than its diff:
```python
import functools
import math

import jax
import jax.numpy as jnp
from jax import lax
from jax.experimental import pallas as pl
from jax.experimental.pallas import tpu as pltpu
from jax.sharding import PartitionSpec as P

MESH = pl.DeviceIdType.MESH
HEAD = 64
LANES = 128
epsilon = 1e-06
score_scale = 1.0 / math.sqrt(HEAD)
bf16, f32 = jnp.bfloat16, jnp.float32


def bit_of(d, b):
    return lax.rem(lax.div(d, jnp.int32(2 ** b)), jnp.int32(2))


def flip(d, b):
    return d + (1 - 2 * bit_of(d, b)) * (2 ** b)


def when(cond, fn):
    if cond is True:
        fn()
    else:
        pl.when(cond)(fn)


class Gather:
    def __init__(self, src, dst, row0, rows, order, d, z, nz, sems, base):
        self.src, self.dst, self.row0, self.order = src, dst, row0, order
        self.d, self.z, self.nz = d, z, nz
        self.piece = rows // (2 ** len(order))
        self.zs, self.zr, self.ps, self.pr = sems
        self.base = base
        self.k = len(order)

    def win(self, s):
        w = jnp.int32(0)
        for i, b in enumerate(self.order):
            if i >= s:
                w = w + bit_of(self.d, b) * (2 ** i)
        size = self.piece * 2 ** s
        start = self.row0 + w * self.piece
        return pl.ds(pl.multiple_of(start, 16), size)

    def shard(self, dr, j):
        return self.z - j if dr == 0 else self.z + j

    def has(self, dr, j):
        return self.z >= j if dr == 0 else self.z + j < self.nz

    def zcopy(self, dr, j):
        t = self.shard(dr, j)
        rows = self.win(0)
        src = self.src.at[rows] if j == 0 else self.dst.at[t, rows]
        to = self.z + 1 if dr == 0 else self.z - 1
        return pltpu.make_async_remote_copy(src, self.dst.at[t, rows], self.zs.at[self.base, dr, j], self.zr.at[self.base, dr, j], device_id=(self.d, to), device_id_type=MESH)

    def zcan(self, dr, j):
        ahead = self.z + 1 < self.nz if dr == 0 else self.z >= 1
        return ahead if j == 0 else jnp.logical_and(ahead, self.has(dr, j))

    def pcopy(self, s, dr, j):
        t = self.shard(dr, j)
        rows = self.win(s)
        b = self.order[s]
        return pltpu.make_async_remote_copy(self.dst.at[t, rows], self.dst.at[t, rows], self.ps.at[self.base, s, dr, j - 1], self.pr.at[self.base, s, dr, j - 1], device_id=(flip(self.d, b), self.z), device_id_type=MESH)

    def events(self):
        return self.nz + self.k

    def event(self, e):
        nz, k = self.nz, self.k
        if e == 0:
            for dr in (0, 1):
                when(self.zcan(dr, 0), lambda: self.zcopy(dr, 0).start())
            return
        for s in range(k, -1, -1):
            j = e - s
            if not 1 <= j <= nz - 1:
                continue
            for dr in (0, 1):
                def go(dr=dr, j=j, s=s):
                    if s == 0:
                        self.zcopy(dr, j - 1).wait_recv()
                        if j <= nz - 2:
                            when(self.zcan(dr, j), lambda: self.zcopy(dr, j).start())
                    else:
                        self.pcopy(s - 1, dr, j).wait_recv()
                    if s < k:
                        self.pcopy(s, dr, j).start()
                when(self.has(dr, j), go)

    def finish(self):
        nz, k = self.nz, self.k
        for dr in (0, 1):
            for j in range(nz - 1):
                when(self.zcan(dr, j), lambda dr=dr, j=j: self.zcopy(dr, j).wait_send())
            for s in range(k):
                for j in range(1, nz):
                    when(self.has(dr, j), lambda dr=dr, j=j, s=s: self.pcopy(s, dr, j).wait_send())


def add_into(dst, src, rows):
    step = 32 if rows % 32 == 0 else 16

    def body(i, c):
        r = pl.ds(pl.multiple_of(i * step, step), step)
        dst[r, :] = dst[r, :] + src[r, :]
        return c
    lax.fori_loop(0, rows // step, body, 0)


def add_all(dst, src, count, rows):
    def body(t, c):
        add_into(dst.at[t], src.at[t], rows)
        return c
    lax.fori_loop(0, count, body, 0)


def op_rows(half, order, op):
    size = half
    for o in order:
        if o == "z":
            if op == "z":
                return size
        else:
            size //= 2
            if o == op:
                return size
    return size


class Reduce:
    slots_max = 20

    def __init__(self, keep, bufs, result, pos, half, order, d, z, nz, bits, sems, base):
        self.keep = keep
        self.recvs, self.ups, self.downs, self.extra = bufs
        self.result, self.pos, self.half, self.order = result, pos, half, order
        self.d, self.z, self.nz, self.bits = d, z, nz, bits
        self.ss, self.rs, self.ls = sems
        self.base = base
        self.slot = 0
        self.pending = []
        self.steps = []
        self.build()

    def copy(self, s, src, dst, to):
        return lambda: pltpu.make_async_remote_copy(src, dst, self.ss.at[self.base, s], self.rs.at[self.base, s], device_id=to, device_id_type=MESH)

    def remote(self, src, dst, to, keep=True):
        cp = self.copy(self.slot, src, dst, to)
        self.slot += 1
        if keep:
            self.pending.append((True, cp))
        return cp

    def build(self):
        d, z, nz = self.d, self.z, self.nz
        prev = None
        start, size, whole = jnp.int32(0), self.half, True
        taken = []

        def then(prev, cp):
            def step():
                if prev is not None:
                    prev()
                cp().start()
            self.steps.append(step)

        for op in self.order:
            if op == "z":
                self.zbase = self.slot
                self.slot += 2 * nz
                self.zc = self.zcopies(start, size)
                for h in range(nz):
                    self.steps.append(functools.partial(self.zhop, h, start, size, prev if h == 0 else None))
                prev, whole = None, False
                continue
            size //= 2
            m = bit_of(d, op)
            keep0 = pl.multiple_of(start + m * size, 16)
            send0 = pl.multiple_of(start + (1 - m) * size, 16)
            buf = self.recvs[op]
            if whole:
                cp = self.remote(self.keep.at[:, pl.ds(send0, size), :], buf, (flip(d, op), z))
            else:
                cp = self.remote(self.keep.at[z, pl.ds(send0, size), :], buf.at[0], (flip(d, op), z))
            then(prev, cp)

            def prev(cp=cp, keep0=keep0, size=size, whole=whole, buf=buf):
                cp().wait_recv()
                if whole:
                    add_all(self.keep.at[:, pl.ds(keep0, size), :], buf, nz, size)
                else:
                    add_into(self.keep.at[z, pl.ds(keep0, size), :], buf.at[0], size)
            taken.append(op)
            start = keep0
        for e, b in enumerate(self.bits[3:]):
            cp = self.remote(self.keep.at[z, pl.ds(start, size), :], self.extra.at[e], (flip(d, b), z), False)
            then(prev, cp)

            def prev(cp=cp, e=e, start=start, size=size):
                cp().wait_recv()
                cp().wait_send()
                add_into(self.keep.at[z, pl.ds(start, size), :], self.extra.at[e], size)
        pos = pl.multiple_of(self.pos + start, 16)
        own = lambda pos=pos, size=size: pltpu.make_async_copy(self.keep.at[z, pl.ds(start, size), :], self.result.at[pl.ds(pos, size), :], self.ls.at[self.base])

        def place(prev=prev, own=own):
            if prev is not None:
                prev()
            own().start()
        first = True
        for op in list(reversed(taken)) + [self.bits[0]]:
            win = self.result.at[pl.ds(pos, size), :]
            if first:
                cp = self.remote(self.keep.at[z, pl.ds(start, size), :], win, (flip(d, op), z))
            else:
                cp = self.remote(win, win, (flip(d, op), z))
            if first:
                def step(cp=cp):
                    place()
                    cp().start()
                self.steps.append(step)

                def prev(cp=cp):
                    cp().wait_recv()
                    own().wait()
                first = False
            else:
                then(prev, cp)
                prev = lambda cp=cp: cp().wait_recv()
            if op != self.bits[0]:
                pos = pl.multiple_of(pos - bit_of(d, op) * size, 16)
                size *= 2
        self.steps.append(prev)

    def zcopies(self, start, size):
        out = {}
        d, z, nz = self.d, self.z, self.nz
        rows = pl.ds(start, size)
        for t in range(nz):
            src = self.keep.at[t, rows, :]
            if t >= 1:
                out["u", t] = self.copy(self.zbase + t, src, self.ups.at[t - 1], (d, z + 1))
                self.pending.append((z < t, out["u", t]))
            if t <= nz - 2:
                out["d", t] = self.copy(self.zbase + nz + t, src, self.downs.at[t], (d, z - 1))
                self.pending.append((z > t, out["d", t]))
        return out

    def zhop(self, h, start, size, prev):
        z, nz = self.z, self.nz
        if prev is not None:
            prev()
        rows = pl.ds(start, size)

        @pl.when(z == h)
        def _():
            for t in range(nz - 1, max(h, 1) - 1, -1):
                if h > 0:
                    self.zc["u", t]().wait_recv()
                    add_into(self.keep.at[t, rows, :], self.ups.at[t - 1], size)
                if t > h:
                    self.zc["u", t]().start()
        me = nz - 1 - h

        @pl.when(z == me)
        def _():
            for t in range(0, min(me, nz - 2) + 1):
                if h > 0:
                    self.zc["d", t]().wait_recv()
                    add_into(self.keep.at[t, rows, :], self.downs.at[t], size)
                if t < me:
                    self.zc["d", t]().start()

    def finish(self):
        for cond, cp in self.pending:
            when(cond, lambda: cp().wait_send())


def enter(d, z, nz, bits):
    bar = pltpu.get_barrier_semaphore()
    for b in bits:
        pl.semaphore_signal(bar, inc=1, device_id=(flip(d, b), z), device_id_type=MESH)
    for o in range(1, nz):
        pl.semaphore_signal(bar, inc=1, device_id=(d, lax.rem(z + o, jnp.int32(nz))), device_id_type=MESH)
    pl.semaphore_wait(bar, len(bits) + nz - 1)


def dot(a, b):
    return lax.dot_general(a, b, (((1,), (0,)), ((), ())), preferred_element_type=f32)


def dot_nt(a, b):
    return lax.dot_general(a, b, (((1,), (1,)), ((), ())), preferred_element_type=f32)


def dot_tn(a, b):
    return lax.dot_general(a, b, (((0,), (0,)), ((), ())), preferred_element_type=f32)


def norm_forward(h, gain, shift):
    centred = h - jnp.mean(h, -1, keepdims=True)
    inverse = lax.rsqrt(jnp.mean(centred * centred, -1, keepdims=True) + epsilon)
    normed = centred * inverse
    return normed * gain + shift, normed, inverse


def norm_backward(grad, normed, inverse, gain):
    scaled = grad * gain
    return inverse * (scaled - jnp.mean(scaled, -1, keepdims=True) - normed * jnp.mean(scaled * normed, -1, keepdims=True))


def col_sum(v):
    return jnp.sum(v, axis=0, keepdims=True)


class Dims:
    pass


def layer_kernel(m, *refs):
    n_in, n_out = len(m.inputs), len(m.outputs)
    R = dict(zip(m.inputs + m.outputs + m.scratch, refs))
    g = Dims()
    for k, v in R.items():
        setattr(g, k, v)
    ni, L, T, D, nz, hp, nh, KP, NP = m.ni, m.L, m.T, m.D, m.nz, m.hp, m.nh, m.KP, m.NP
    d, z = lax.axis_index("dp"), lax.axis_index("mp")
    core = bit_of(d, m.bits[0])
    partner = flip(d, m.bits[0])

    def shard(o):
        t = z
        for b in range(nz.bit_length() - 1):
            t = t + lax.rem(lax.div(o, jnp.int32(2 ** b)), jnp.int32(2)) * (1 - 2 * bit_of(z, b)) * (2 ** b)
        return t

    g.DCQ = g.HD.at[:, :, 0:hp]
    g.DQ = g.DP.at[:, :, 0:m.QW]

    g.VG[z] = g.vown[...]
    enter(d, z, nz, m.bits)
    gsem = (g.zs, g.zr, g.ps, g.pr)
    own = {"A": g.A, "B": g.B, "O": g.O, "H": g.H, "W": g.W, "V": g.vown}
    far = {"A": g.GA, "B": g.GB, "O": g.GO, "H": g.GH, "W": g.GW, "V": g.VG}
    gathers = [Gather(own[k], far[k], r0, rows, order, d, z, nz, gsem, c) for c, (k, r0, rows, order, _) in enumerate(m.gather_plan)]
    queue = []
    for tick in range(64):
        for c, p in enumerate(m.gather_plan):
            e = tick - p[4]
            if 0 <= e < gathers[c].events():
                queue.append((c, e))

    def advance(stop):
        names = stop if isinstance(stop, str) else ""
        while queue:
            if names:
                if not any(m.gather_plan[c][0] in names for c, e in queue):
                    return
            c, e = queue.pop(0)
            gathers[c].event(e)

    def gather_some(k):
        for _ in range(k):
            if queue:
                c, e = queue.pop(0)
                gathers[c].event(e)

    pair_slot = [0]

    def pair(ref, rows):
        s = pair_slot[0]
        pair_slot[0] += 1
        return pltpu.make_async_remote_copy(ref.at[pl.ds(0, rows)], ref.at[pl.ds(rows, rows)], g.cs.at[s], g.cr.at[s], device_id=(partner, z), device_id_type=MESH)

    def fetch(buf, sem, slot, key, rows, o):
        dst = buf.at[slot, pl.ds(0, rows[1])] if buf.shape[1] != rows[1] else buf.at[slot]
        src = pl.ds(rows[0], rows[1])

        @pl.when(o == 0)
        def _():
            pltpu.make_async_copy(own[key].at[src], dst, sem.at[slot]).start()

        @pl.when(o != 0)
        def _():
            pltpu.make_async_copy(far[key].at[shard(o), src], dst, sem.at[slot]).start()

    def arrived(buf, sem, slot, key, rows):
        dst = buf.at[slot, pl.ds(0, rows[1])] if buf.shape[1] != rows[1] else buf.at[slot]
        pltpu.make_async_copy(own[key].at[pl.ds(rows[0], rows[1])], dst, sem.at[slot]).wait()

    def stream(blocks, body, between=None):
        for buf, sem, key, rows in blocks:
            fetch(buf, sem, 0, key, rows, 0)

        def step(o, c):
            slot = lax.rem(o, jnp.int32(2))

            @pl.when(o + 1 < nz)
            def _():
                for buf, sem, key, rows in blocks:
                    fetch(buf, sem, 1 - slot, key, rows, o + 1)
            for buf, sem, key, rows in blocks:
                arrived(buf, sem, slot, key, rows)
            body(o, slot)
            if between is not None:
                between(o)
            return c
        lax.fori_loop(0, nz, step, 0)

    lane = lax.broadcasted_iota(jnp.int32, (L, hp), 1)
    low = [lane // HEAD == h for h in range(nh)]
    high = [lane // HEAD == h + 1 for h in range(nh)]

    def stack(v, masks):
        return jnp.concatenate([jnp.where(k, v, 0.0) for k in masks], axis=0).astype(bf16)

    def unstack(v, masks):
        out = jnp.where(masks[0], v[0:L], 0.0)
        for h in range(1, nh):
            out = out + jnp.where(masks[h], v[h * L:(h + 1) * L], 0.0)
        return out

    def softmax(s):
        e = jnp.exp(s - jnp.max(s, -1, keepdims=True))
        return e / jnp.sum(e, -1, keepdims=True)

    for c, p in enumerate(m.gather_plan):
        if p[4] == 0:
            gathers[c].event(0)
    queue[:] = [q for q in queue if not (q[1] == 0 and m.gather_plan[q[0]][4] == 0)]
    for i in range(ni):
        g.XF[i * L:(i + 1) * L] = g.x[i].astype(f32)
        g.PT[i * KP:i * KP + NP] = g.patches[i]
        g.PT[i * KP + NP // 16 * 16:(i + 1) * KP] = jnp.concatenate([g.patches[i, NP // 16 * 16:NP].astype(f32), jnp.zeros((KP - NP, m.PW), f32)], 0).astype(bf16)
    g.X[0:T] = g.XF[...].astype(bf16)
    swaps = [pair(g.X, T), pair(g.PT, ni * KP)]
    for s in swaps:
        s.start()

    advance("AVO")
    g.ACC[...] = jnp.zeros((T, D), f32)

    def self_forward(o, slot):
        t = shard(o)
        bias = g.VG[t].astype(f32)[0:1, LANES:]
        qkv = (dot(g.X[0:T], g.SA[slot, :, LANES:]) + bias).astype(bf16)
        g.QKV[o] = qkv
        qf = qkv.astype(f32)
        outs = []
        for i in range(ni):
            r = slice(i * L, (i + 1) * L)
            qs = stack(qf[r, 0:hp], high)
            k_i = qf[r, 3 * LANES:3 * LANES + hp].astype(bf16)
            v_i = qf[r, 2 * LANES:2 * LANES + hp].astype(bf16)
            p = softmax(dot_nt(qs, k_i) * score_scale)
            g.PS[o * ni + i] = p
            outs.append(unstack(dot(p.astype(bf16), v_i), low))
        mixed = jnp.concatenate(outs, 0).astype(bf16)
        g.MX[0, o, 0:T] = mixed
        g.ACC[...] += dot(mixed, g.SO[slot])

    self_blocks = [(g.SA, g.sa, "A", (0, D)), (g.SO, g.so, "O", (0, hp))]
    stream(self_blocks, self_forward)

    def out_row(j):
        return g.ob[j:j + 1, :], g.gain[j:j + 1, :], g.shift[j:j + 1, :]

    ob, gn, sh = out_row(0)
    first, normed, inv = norm_forward(g.XF[...] + g.ACC[...] + ob, gn, sh)
    g.NM[0] = normed
    g.INV[0] = jnp.broadcast_to(inv, (T, LANES))
    g.F[0:T] = first.astype(bf16)
    advance("B")
    g.ACC[...] = jnp.zeros((T, D), f32)

    key_pos = lax.broadcasted_iota(jnp.int32, (nh * L, KP), 1)

    def cross_forward(o, slot):
        t = shard(o)
        vb = g.VG[t].astype(f32)
        cq = (dot(g.F[0:T], g.SA[slot, :, 0:hp]) + vb[0:1, 0:hp]).astype(bf16)
        g.CQ[o] = cq
        cqf = cq.astype(f32)
        kv = (dot(g.PT[0:ni * KP], g.SB[slot]) + vb[1:2, 0:m.BW]).astype(bf16)
        g.KV[o] = kv
        outs = []
        for i in range(ni):
            qs = stack(cqf[i * L:(i + 1) * L], low)
            kvi = g.KV[o, i * KP:(i + 1) * KP]
            s = dot_nt(qs, kvi[:, 0:hp]) * score_scale
            s = jnp.where(key_pos < g.rows[z * ni + i], s, -1e30)
            p = softmax(s)
            g.PC[o * ni + i] = p
            outs.append(unstack(dot(p.astype(bf16), kvi[:, LANES:LANES + hp]), high))
        mixed = jnp.concatenate(outs, 0).astype(bf16)
        g.MX[1, o, 0:T] = mixed
        g.ACC[...] += dot(mixed, g.SO[slot])

    cross_out = (g.SO, g.so, "O", (LANES, hp))
    cross_blocks = [(g.SA, g.sa, "A", (0, D)), (g.SB, g.sb, "B", (0, m.PW)), cross_out]
    stream(cross_blocks, cross_forward)
    ob, gn, sh = out_row(1)
    second, normed, inv = norm_forward(g.F[0:T].astype(f32) + g.ACC[...] + ob, gn, sh)
    g.NM[1] = normed
    g.INV[1] = jnp.broadcast_to(inv, (T, LANES))
    g.S2[0:T] = second.astype(bf16)
    advance("H")
    other = g.MX.at[1 - core]
    mix_swap = pltpu.make_async_remote_copy(other.at[:, pl.ds(0, T)], other.at[:, pl.ds(T, T)], g.cs.at[m.swaps - 1], g.cr.at[m.swaps - 1], device_id=(partner, z), device_id_type=MESH)
    mix_swap.start()
    swaps += [pair(g.F, T), pair(g.S2, T)]
    for s in swaps[2:4]:
        s.start()

    def hidden_forward(o, slot):
        t = shard(o)
        pre = dot(g.S2[0:T], g.SA[slot]) + g.VG[t].astype(f32)[2:3, :]
        cdf = 0.5 * (1.0 + lax.erf(pre * math.sqrt(0.5)))
        g.GP[o] = cdf + pre * jnp.exp(-0.5 * pre * pre) * (1.0 / math.sqrt(2.0 * math.pi))
        g.HD[o, 0:T] = (pre * cdf).astype(bf16)

    stream([(g.SA, g.sa, "H", (0, D))], hidden_forward)
    hid_swaps = [pair(g.HD.at[o], T) for o in range(nz)]
    for s in hid_swaps:
        s.start()
    advance("W")
    g.ACC[...] = jnp.zeros((T, D), f32)

    def output_forward(o, slot):
        g.ACC[...] += dot(g.HD[o, 0:T], g.SA[slot])

    stream([(g.SA, g.sa, "W", (0, m.FZ))], output_forward)
    ob, gn, sh = out_row(2)
    final, normed, inv = norm_forward(g.S2[0:T].astype(f32) + g.ACC[...] + ob, gn, sh)
    g.layer_out[...] = final.reshape(ni, L, D)

    for i in range(ni):
        g.ACC[i * L:(i + 1) * L] = g.cot[i].astype(f32)
    cot = g.ACC[...]
    g.SM[...] = jnp.zeros(g.SM.shape, f32)

    def record(j, grad_in, grad_out, normed):
        g.SM[j:j + 1] = col_sum(grad_in)
        g.SM[3 + j:4 + j] = col_sum(grad_out * normed)
        g.SM[6 + j:7 + j] = col_sum(grad_out)

    third = norm_backward(cot, normed, inv, gn)
    record(2, third, cot, normed)
    g.G3[0:T] = third.astype(bf16)
    swap3 = pair(g.G3, T)
    swap3.start()

    rsem = (g.ss, g.rs, g.ls)
    results = {"A": g.RA, "B": g.RB, "O": g.RO, "H": g.RH, "W": g.RW}
    chunks = []
    for c, (k, h0, half, order) in enumerate(m.reduce_plan):
        recvs = {b: R[f"rv{c}_{b}"] for b in m.bits[1:3]}
        bufs = (recvs, R[f"up{c}"], R[f"dn{c}"], R.get(f"ex{c}"))
        whole = m.rows[k] // 2
        chunks.append(Reduce(R[f"kp{c}"], bufs, results[k], core * whole + h0, half, order, d, z, nz, m.bits, rsem, c))
    active = []

    def launch(k):
        for c, p in enumerate(m.reduce_plan):
            if p[0] == k:
                active.append(list(chunks[c].steps))
        pump(1)

    def pump(times):
        for _ in range(times):
            for steps in active:
                if steps:
                    steps.pop(0)()

    def plan_of(k):
        return [(c, p[1], p[2]) for c, p in enumerate(m.reduce_plan) if p[0] == k]

    def half_columns(whole, h0, half):
        return pl.ds(pl.multiple_of(core * whole + h0, LANES), half)

    swap3.wait_recv()
    for s in hid_swaps:
        s.wait_recv()

    def job_w(o, c):
        t = shard(o)
        for ch, h0, half in plan_of("W"):
            R[f"kp{ch}"][t] = dot_tn(g.HD[o, :, half_columns(m.FZ // 2, h0, half)], g.G3[...]).astype(bf16)
        return c
    lax.fori_loop(0, nz, job_w, 0)
    for s in hid_swaps:
        s.wait_send()
    launch("W")

    g.ACC[...] = third

    def hidden_backward(o, slot):
        t = shard(o)
        pre = (dot_nt(g.G3[0:T], g.SA[slot]) * g.GP[o]).astype(bf16)
        g.DP[o, 0:T] = pre
        g.SM[pl.ds(9 + t, 1)] = col_sum(pre.astype(f32))
        pltpu.make_async_remote_copy(g.DP.at[o, pl.ds(0, T)], g.DP.at[o, pl.ds(T, T)], g.ds.at[0, o], g.dr.at[0, o], device_id=(partner, z), device_id_type=MESH).start()
        g.ACC[...] += dot_nt(pre, g.SH[slot])

    stream([(g.SA, g.sa, "W", (0, m.FZ)), (g.SH, g.sh, "H", (0, D))], hidden_backward)

    def loop_wait(ref, rows, kind):
        for o in range(nz):
            cp = pltpu.make_async_remote_copy(ref.at[o, pl.ds(0, rows)], ref.at[o, pl.ds(rows, rows)], g.ds.at[kind, o], g.dr.at[kind, o], device_id=(partner, z), device_id_type=MESH)
            cp.wait()

    def loop_send(ref, rows, kind, o):
        pltpu.make_async_remote_copy(ref.at[o, pl.ds(0, rows)], ref.at[o, pl.ds(rows, rows)], g.ds.at[kind, o], g.dr.at[kind, o], device_id=(partner, z), device_id_type=MESH).start()

    gn = g.gain[1:2, :]
    normed, inv = g.NM[1], g.INV[1][:, 0:1]
    grad = g.ACC[...]
    secondg = norm_backward(grad, normed, inv, gn)
    record(1, secondg, grad, normed)
    g.G12[1, 0:T] = secondg.astype(bf16)
    swap2 = pair(g.G12.at[1], T)
    swap2.start()
    pump(1)
    loop_wait(g.DP, T, 0)
    swaps[3].wait_recv()

    def job_h(o, c):
        t = shard(o)
        for ch, h0, half in plan_of("H"):
            R[f"kp{ch}"][t] = dot_tn(g.S2[:, half_columns(D // 2, h0, half)], g.DP[o]).astype(bf16)
        return c
    lax.fori_loop(0, nz, job_h, 0)
    launch("H")

    g.ACC[...] = secondg
    g.patch_grad[...] = jnp.zeros(g.patch_grad.shape, f32)

    def backward_unit(qs, k_i, v_i, p, ms, masks):
        grad_v = dot_tn(p.astype(bf16), ms)
        grad_p = dot_nt(ms, v_i)
        gs = (p * (grad_p - jnp.sum(p * grad_p, -1, keepdims=True))).astype(bf16)
        grad_q = unstack(dot(gs, k_i), masks) * score_scale
        grad_k = dot_tn(gs, qs) * score_scale
        return grad_q, grad_k.astype(bf16).astype(f32), grad_v.astype(bf16).astype(f32)

    def cross_backward(o, slot):
        t = shard(o)
        gm = dot_nt(g.G12[1, 0:T], g.SO[slot]).astype(bf16).astype(f32)
        cqf = g.CQ[o].astype(f32)
        grads = []
        for i in range(ni):
            r = slice(i * L, (i + 1) * L)
            kvi = g.KV[o, i * KP:(i + 1) * KP]
            gq, gk, gv = backward_unit(stack(cqf[r], low), kvi[:, 0:hp], kvi[:, LANES:LANES + hp], g.PC[o * ni + i], stack(gm[r], high), low)
            grads.append(gq)
            g.DKV[o, i * KP:(i + 1) * KP] = jnp.concatenate([gk[:, 0:LANES], gk[:, LANES:] + gv[:, 0:LANES], gv[:, LANES:]], 1).astype(bf16)
        dcq = jnp.concatenate(grads, 0).astype(bf16)
        g.DCQ[o, 0:T] = dcq
        loop_send(g.DCQ, T, 1, o)
        loop_send(g.DKV, ni * KP, 2, o)
        dkv = g.DKV[o, 0:ni * KP]
        g.SM[pl.ds(9 + nz + t, 1), 0:hp] = col_sum(dcq.astype(f32))
        g.SM[pl.ds(9 + 2 * nz + t, 1), 0:m.BW] = col_sum(dkv.astype(f32))
        g.ACC[...] += dot_nt(dcq, g.SA[slot, :, 0:hp])
        for i in range(ni):
            g.patch_grad[i] += dot_nt(g.DKV[o, i * KP:(i + 1) * KP], g.SB[slot])[0:NP]

    def between(o):
        @pl.when(o == 1)
        def _():
            pump(1)

        @pl.when(o == 3)
        def _():
            pump(1)
    stream(cross_blocks, cross_backward, between)
    gn = g.gain[0:1, :]
    normed, inv = g.NM[0], g.INV[0][:, 0:1]
    grad = g.ACC[...]
    firstg = norm_backward(grad, normed, inv, gn)
    record(0, firstg, grad, normed)
    g.G12[0, 0:T] = firstg.astype(bf16)
    swap1 = pair(g.G12.at[0], T)
    swap1.start()
    pump(1)
    loop_wait(g.DCQ, T, 1)
    loop_wait(g.DKV, ni * KP, 2)
    swaps[1].wait_recv()

    def job_b(o, c):
        t = shard(o)
        for ch, h0, half in plan_of("B"):
            R[f"kp{ch}"][t] = dot_tn(g.PT[:, half_columns(m.PW // 2, h0, half)], g.DKV[o]).astype(bf16)
        return c
    lax.fori_loop(0, nz, job_b, 0)
    launch("B")

    g.ACC[...] = firstg

    def self_backward(o, slot):
        t = shard(o)
        gm = dot_nt(g.G12[0, 0:T], g.SO[slot]).astype(bf16).astype(f32)
        qf = g.QKV[o].astype(f32)
        gqs, gks, gvs = [], [], []
        for i in range(ni):
            r = slice(i * L, (i + 1) * L)
            k_i = qf[r, 3 * LANES:3 * LANES + hp].astype(bf16)
            v_i = qf[r, 2 * LANES:2 * LANES + hp].astype(bf16)
            gq, gk, gv = backward_unit(stack(qf[r, 0:hp], high), k_i, v_i, g.PS[o * ni + i], stack(gm[r], low), high)
            gqs.append(gq)
            gks.append(gk)
            gvs.append(gv)
        gq, gk, gv = (jnp.concatenate(v, 0) for v in (gqs, gks, gvs))
        dq = jnp.concatenate([gq, gv[:, 0:LANES], gv[:, LANES:] + gk[:, 0:LANES], gk[:, LANES:]], 1).astype(bf16)
        g.DQ[o, 0:T] = dq
        loop_send(g.DQ, T, 3, o)
        g.SM[pl.ds(9 + 3 * nz + t, 1), 0:m.QW] = col_sum(dq.astype(f32))
        g.ACC[...] += dot_nt(dq, g.SA[slot, :, LANES:])

    stream(self_blocks, self_backward, between)
    g.text_grad[...] = g.ACC[...].reshape(ni, L, D)
    pump(1)
    loop_wait(g.DQ, T, 3)
    swap1.wait_recv()
    swap2.wait_recv()
    for s in swaps[0:1] + swaps[2:3] + [mix_swap]:
        s.wait_recv()

    def job_o(o, c):
        t = shard(o)
        g.TMP[...] = dot_tn(g.MX[core, o], g.G12[core])
        for ch, h0, half in plan_of("O"):
            R[f"kp{ch}"][t] = g.TMP[pl.ds(pl.multiple_of(core * HEAD + h0, 16), half)].astype(bf16)
        return c
    lax.fori_loop(0, nz, job_o, 0)
    launch("O")

    def job_a(o, c):
        t = shard(o)
        for ch, h0, half in plan_of("A"):
            cols = half_columns(D // 2, h0, half)
            kp = R[f"kp{ch}"]
            left = dot_tn(g.F[:, cols], g.DCQ[o])
            right = dot_tn(g.X[:, cols], g.DQ[o])
            kp[t, :, 0:LANES] = left[:, 0:LANES].astype(bf16)
            kp[t, :, LANES:hp] = (left[:, LANES:] + right[:, 0:LANES]).astype(bf16)
            kp[t, :, hp:] = right[:, LANES:].astype(bf16)
        return c
    lax.fori_loop(0, nz, job_a, 0)
    launch("A")

    sends = []
    for i, b in enumerate(m.bits):
        cp = pltpu.make_async_remote_copy(g.SM, g.SR.at[i], g.ms.at[i], g.mr.at[i], device_id=(flip(d, b), z), device_id_type=MESH)
        cp.start()
        pump(1)
        cp.wait()
        g.SM[...] += g.SR[i]
    g.SZ[z] = g.SM[...]
    nb = len(m.bits)
    for o in range(1, nz):
        to = lax.rem(z + o, jnp.int32(nz))
        cp = pltpu.make_async_remote_copy(g.SM, g.SZ.at[z], g.ms.at[nb + o], g.zm.at[z], device_id=(d, to), device_id_type=MESH)
        cp.start()
        sends.append(cp)
    pump(1)
    for o in range(1, nz):
        frm = lax.rem(z + o, jnp.int32(nz))
        pltpu.make_async_remote_copy(g.SM, g.SZ.at[frm], g.ms.at[nb + o], g.zm.at[frm], device_id=(d, frm), device_id_type=MESH).wait_recv()
    total = g.SZ[0]
    for t in range(1, nz):
        total = total + g.SZ[t]
    g.small[...] = total
    while any(active):
        pump(1)

    for cp in sends + swaps + [swap1, swap2, swap3, mix_swap]:
        cp.wait_send()
    for q in gathers:
        q.finish()
    for c in chunks:
        c.finish()


def gather_plan(rows, bits):
    c, x, y = bits[:3]
    a, b, o, h, w = (rows[k] for k in "ABOHW")
    return (
        ("V", 0, 16, (), 0), ("A", 0, a, (x, y, c), 0), ("O", 0, o, (x, c), 1), ("B", 0, b, (y, x, c), 1), ("H", 0, h, (y, x, c), 2), ("W", 0, w, (y, c), 2),
    )


def reduce_plan(rows, bits):
    c, x, y = bits[:3]
    plan = []
    for k in "WHBOA":
        half = rows[k] // 2
        orders = [(y, x, "z"), (x, "z", y), ("z", y, x)]
        unit = 64 if k == "O" else LANES
        n = half // unit
        cuts = [n * (i + 1) // 3 - n * i // 3 for i in range(3)]
        h0 = 0
        for cut, order in zip(cuts, orders):
            plan.append((k, h0, cut * unit, order))
            h0 += cut * unit
    return tuple(plan)


def run_layer(m, nd, shards, vown, x, patches, rows, cot, ob, gain, shift):
    nz = m.nz
    ni, L, D = x.shape
    T = ni * L
    m.ni, m.L, m.D, m.T = ni, L, D, T
    m.NP, m.PW = patches.shape[1:]
    m.KP = (m.NP + 15) // 16 * 16
    hw = D // nz
    m.nh = hw // HEAD
    m.hp = (hw + HEAD + LANES - 1) // LANES * LANES
    hp, KP, PW = m.hp, m.KP, m.PW
    A, B, O, H, W = shards
    m.BW, m.QW, m.FZ = B.shape[1], D - LANES, W.shape[0]
    FZ = m.FZ
    m.rows = {k: s.shape[0] for k, s in zip("ABOHW", shards)}
    lanes = {k: s.shape[1] for k, s in zip("ABOHW", shards)}
    m.gather_plan = gather_plan(m.rows, m.bits)
    m.reduce_plan = reduce_plan(m.rows, m.bits)
    m.swaps = nz + 9
    V, sem = pltpu.VMEM, pltpu.SemaphoreType.DMA
    nc, ng = len(m.reduce_plan), len(m.gather_plan)
    nb = len(m.bits)
    sums = (9 + 4 * nz + 7) // 8 * 8
    scratch = dict(
        VG=V((nz, 16, D), bf16), XF=V((T, D), f32), X=V((2 * T, D), bf16), PT=V((2 * ni * KP, PW), bf16),
        SA=V((2, D, D), bf16), SH=V((2, D, D), bf16), SB=V((2, PW, m.BW), bf16), SO=V((2, hp, D), bf16),
        ACC=V((T, D), f32), QKV=V((nz, T, m.QW), bf16), PS=V((nz * ni, m.nh * L, L), f32), MX=V((2, nz, 2 * T, hp), bf16),
        NM=V((2, T, D), f32), INV=V((2, T, LANES), f32), F=V((2 * T, D), bf16), S2=V((2 * T, D), bf16),
        CQ=V((nz, T, hp), bf16), KV=V((nz, ni * KP, m.BW), bf16), PC=V((nz * ni, m.nh * L, KP), f32),
        GP=V((nz, T, FZ), f32), HD=V((nz, 2 * T, FZ), bf16), SM=V((sums, D), f32), G3=V((2 * T, D), bf16), DP=V((nz, 2 * T, FZ), bf16),
        G12=V((2, 2 * T, D), bf16), DKV=V((nz, 2 * ni * KP, m.BW), bf16),
        TMP=V((hp, D), f32), SR=V((nb, sums, D), f32), SZ=V((nz, sums, D), f32),
        zs=sem((ng, 2, nz)), zr=sem((ng, 2, nz)), ps=sem((ng, 3, 2, nz)), pr=sem((ng, 3, 2, nz)),
        cs=sem((m.swaps,)), cr=sem((m.swaps,)), ds=sem((4, nz)), dr=sem((4, nz)),
        sa=sem((2,)), sh=sem((2,)), sb=sem((2,)), so=sem((2,)),
        ss=sem((nc, Reduce.slots_max)), rs=sem((nc, Reduce.slots_max)), ls=sem((nc,)), ms=sem((nb + nz,)), mr=sem((nb,)), zm=sem((nz,)),
    )
    for c, (k, h0, half, order) in enumerate(m.reduce_plan):
        C = lanes[k]
        scratch[f"kp{c}"] = V((nz, half, C), bf16)
        for b in m.bits[1:3]:
            lead = nz if order.index(b) < order.index("z") else 1
            scratch[f"rv{c}_{b}"] = V((lead, op_rows(half, order, b), C), bf16)
        for n in ("up", "dn"):
            scratch[f"{n}{c}"] = V((nz - 1, op_rows(half, order, "z"), C), bf16)
        if nb > 3:
            scratch[f"ex{c}"] = V((nb - 3, half // 4, C), bf16)
    S = jax.ShapeDtypeStruct
    hbm, vm, sm = (pl.BlockSpec(memory_space=s) for s in (pl.ANY, pltpu.VMEM, pltpu.SMEM))
    outs = dict(
        layer_out=(S((ni, L, D), f32), vm), text_grad=(S((ni, L, D), f32), vm), patch_grad=(S((ni, m.NP, PW), f32), vm), small=(S((sums, D), f32), vm),
        **{"R" + k: (S(s.shape, bf16), hbm) for k, s in zip("ABOHW", shards)},
        **{"G" + k: (S((nz,) + s.shape, bf16), hbm) for k, s in zip("ABOHW", shards)},
    )
    ins = dict(x=(x, vm), patches=(patches, vm), rows=(rows, sm), cot=(cot, vm), A=(A, hbm), B=(B, hbm), O=(O, hbm), H=(H, hbm), W=(W, hbm),
               vown=(vown, vm), ob=(ob, vm), gain=(gain, vm), shift=(shift, vm))
    m.inputs, m.outputs, m.scratch = list(ins), list(outs), list(scratch)
    res = pl.pallas_call(
        functools.partial(layer_kernel, m),
        out_shape=tuple(o[0] for o in outs.values()),
        in_specs=[i[1] for i in ins.values()],
        out_specs=tuple(o[1] for o in outs.values()),
        scratch_shapes=list(scratch.values()),
        compiler_params=pltpu.CompilerParams(collective_id=0, has_side_effects=True, vmem_limit_bytes=67043328),
        name="layer",
    )(*[i[0] for i in ins.values()])
    return dict(zip(outs, res))


def per_device(nd, nz, text_states, patch_states, patch_rows, cotangent, w_attn, attn_bias, w_attn_out, w_query, w_patch, cross_bias, w_cross_out, w_hidden, hidden_bias, w_output, out_bias, norm_gain, norm_shift):
    m = Dims()
    m.nz, m.bits = nz, tuple(range(nd.bit_length() - 1))
    z = lax.axis_index("mp")
    hw = w_query.shape[1]
    D = text_states.shape[-1]
    A = jnp.concatenate([w_query, w_attn[0], w_attn[2], w_attn[1]], 1)
    B = jnp.concatenate([w_patch[0], w_patch[1]], 1)
    O = jnp.concatenate([w_attn_out, w_cross_out], 0)
    zero = jnp.zeros((hw,), bf16)
    vown = jnp.stack([
        jnp.concatenate([cross_bias[0], attn_bias[0], attn_bias[1], zero]),
        jnp.pad(jnp.concatenate([zero, cross_bias[1]]), (0, D - 2 * hw)), hidden_bias])
    vown = jnp.pad(vown, ((0, 13), (0, 0)))
    r = run_layer(m, nd, (A, B, O, w_hidden, w_output), vown, text_states, patch_states, patch_rows, cotangent, out_bias.astype(f32), norm_gain.astype(f32), norm_shift.astype(f32))
    RA, RB, RO, RH, RW = (r["R" + k].astype(f32) for k in "ABOHW")
    small = r["small"]
    pick = lambda base: lax.dynamic_slice_in_dim(small, base + z, 1, 0)[0]
    cq, kv, qv = pick(9 + nz), pick(9 + 2 * nz), pick(9 + 3 * nz)
    at = hw - LANES
    part = lambda a, i: a[:, i * hw:(i + 1) * hw]
    return (
        r["layer_out"], r["text_grad"], r["patch_grad"],
        jnp.stack([part(RA, 1), part(RA, 3), part(RA, 2)]),
        jnp.stack([qv[at:at + hw], qv[at + hw:at + 2 * hw]]),
        RO[:hw], part(RA, 0), jnp.stack([part(RB, 0), part(RB, 1)]),
        jnp.stack([cq[:hw], kv[hw:2 * hw]]), RO[hw:], RH, pick(9), RW,
        small[0:3], small[3:6], small[6:9],
    )


def solution(mesh):
    nd, nz = mesh.shape["dp"], mesh.shape["mp"]
    rows = P(("dp", "mp"), None, None)
    return jax.shard_map(
        functools.partial(per_device, nd, nz),
        mesh=mesh,
        in_specs=(rows, rows, P("dp"), rows, P(None, None, "mp"), P(None, "mp"), P("mp", None), P(None, "mp"), P(None, None, "mp"), P(None, "mp"), P("mp", None), P(None, "mp"), P("mp"), P("mp", None), P(), P(), P()),
        out_specs=(rows, rows, rows, P(None, None, "mp"), P(None, "mp"), P("mp", None), P(None, "mp"), P(None, None, "mp"), P(None, "mp"), P("mp", None), P(None, "mp"), P("mp"), P("mp", None), P(), P(), P()),
        check_vma=False,
    )
```

time: 510 us -> 293 us (0.57); the launches traced: 503 us -> 292 us
  matrix products: 77.7 us -> 0 us
  blocking collectives: 63.5 us -> 0 us
  local copies, waits for them, and re-layouts: 64.5 us -> 21.3 us
  other arithmetic: 25.9 us -> 12.2 us
  Pallas kernels: 270 us -> 258 us
    dot_general x33 -> x0, matrix products: 77.7 us -> none  [ein(): return jnp.einsum(form, *ops, preferred_element_type=jnp.float32)]
    psum x1 -> x0, blocking collectives: 48.7 us -> none  [per_device(): small = lax.psum(small, ('dp', 'mp'))]
    convert_element_type x17 -> x0, local copies, waits for them, and re-layouts: 27.5 us -> none  [the longest x1 6.32 us: per_device(): ein('ild,zilc->zdc', x, dqkv).astype(bf)]
    all_gather x1 -> x0, blocking collectives: 14.8 us -> none  [per_device(): lax.all_gather(jnp.concatenate([attn_bias.reshape(-1), cross_bias.reshape...]
    pallas_call x2 -> x1, Pallas kernels: 270 us -> 258 us  [run_layer(): pl.pallas_call(functools.partial(layer_kernel, m), out_shape=tuple((o[0]...]
    reshape x12 -> x0, local copies, waits for them, and re-layouts: 9.12 us -> none  [the longest x6 7.6 us: heads(): return flat.reshape(flat.shape[:-1] + (flat.shape[-1] // HEAD, HEAD))]
    concatenate x5 -> x4, other arithmetic: 10.4 us -> 3.63 us  [the longest x1 1.5 us: per_device(): A = jnp.concatenate([w_query, w_attn[0], w_attn[2], w_attn[1]], 1)]
    convert_element_type x13 -> x7, other arithmetic: 10.7 us -> 6.5 us  [the longest x4 4.69 us: per_device(): RA, RB, RO, RH, RW = (r['R' + k].astype(f32) for k in 'ABOHW')]
where the time goes in v2:
time: 293 us; the launch traced here: 292 us
  Pallas kernels  258 us (88%)
  local copies, waits for them, and re-layouts  21.3 us (7%)
  other arithmetic  12.2 us (4%)
    pallas_call x1, Pallas kernels, run_layer(): pl.pallas_call(functools.partial(layer_kernel, m), out_shape=tuple((o[0]...  258 us
    unnamed x43, local copies, waits for them, and re-layouts  11.7 us

profile of v2, /device:TPU:0, one launch (start us, length us, event | category | flops | bytes accessed | tf_op | source)
XLA Modules:
  0.0 292.4 jit_solution(3509515549309487834)
XLA Ops:
  0.6 0.0 copy-start.9
  0.7 0.8 slice_reduce_fusion.2
  1.5 0.1 pad_maximum_fusion.5
  1.6 0.1 pad.35
  1.6 0.7 stack.45
  2.3 0.6 fusion.4.refs_9_
  2.9 1.2 fusion.5
  4.1 0.2 copy.44
  4.3 0.2 copy.45
  4.5 0.0 copy-start.5
  4.5 0.2 copy.46
  4.7 0.0 copy-done.9
  4.7 0.2 copy.36
  4.9 1.5 pad_maximum_fusion.2.refs_4_
  6.4 0.0 copy-done.5
  6.4 0.1 fusion.6
  6.4 0.0 copy-start.2
  6.4 0.2 copy.47
  6.6 0.2 copy.48
  6.9 0.0 copy-start.10
  6.9 0.0 copy-start.11
  6.9 1.2 pad_maximum_fusion.3.refs_5_
  8.1 0.0 copy-done.2
  8.1 1.4 copy.39.refs_1_
  9.5 0.0 copy-done.10
  9.5 0.0 copy-done.11
  9.5 0.9 pad_maximum_fusion.4.refs_6_
  10.3 0.0 copy-done.12
  10.3 0.6 convert_element_type.28.refs_10_
  10.9 0.0 copy-done.13
  10.9 0.6 convert_element_type.29.refs_11_
  11.6 0.0 copy-done.14
  11.6 0.6 convert_element_type.30.refs_12_
  12.2 258.1 %layer.1 = (f32[4,40,768]{2,1,0:T(8,128)}, f32[4,40,768]{2,1,0:T(8,128)}, f32[4,145,1024]{2,1,0:T(8,128)}, f32[32,768]{1,0:T(8,128)}, bf16[768,768]{1,0:T(8,128)...) custom-call(bf16[4,40,768]{2,1,0:T(8,128)(2,1)} %refs_0_.1, ...), custom_call_target="tpu_custom_call" | custom-call | tf_op jit(solution)/shard_map/layer/pallas_call | solution.py:877
  270.3 0.9 constant_dynamic-slice_fusion
  271.2 0.6 pad_maximum_fusion.7
  271.8 0.6 pad_maximum_fusion.6
  272.4 1.4 convert_element_type.31
  273.8 0.5 slice_bitcast_fusion.4
  274.3 0.2 pad_maximum_fusion
  274.4 0.0 copy-start.6
  274.4 1.8 copy.41
  276.3 0.0 copy-done.6
  276.3 0.1 convert_element_type.33
  276.4 0.3 slice_bitcast_fusion.1
  276.7 0.1 pad_maximum_fusion.1
  276.9 0.0 copy-start
  276.9 1.7 copy.43
  278.6 1.3 dynamic-slice_reduce_fusion
  279.9 1.5 fusion.8
  281.4 0.0 copy-done
  281.4 0.1 slice.104
  281.5 0.0 copy-start.1
  281.5 1.1 copy.42
  282.5 2.1 fusion.7
  284.7 2.9 %copy.40 = f32[4,145,1024]{2,0,1:T(4,128)} copy(f32[4,145,1024]{2,1,0:T(8,128)S(1)} %copy-done.1) | data formatting | bytes 4751360
  287.6 0.0 copy-done.4
  287.6 1.6 convert_element_type.34
  289.2 0.1 copy-done.3
  289.3 1.6 convert_element_type.35
  290.9 0.0 copy-done.8
  290.9 0.8 copy.51
  291.7 0.0 copy-done.7
  291.7 0.8 copy.52
  (11 shorter events, 0.0 us)
Async XLA Ops:
  0.6 4.0 %copy-start.9 = (bf16[768,192]{0,1:T(8,128)(2,1)S(1)}, bf16[768,192]{0,1:T(8,128)(2,1)}, u32[]{:S(2)}) copy-start(bf16[768,192]{0,1:T(8,128)(2,1)} %param.24) | copy-start | bytes 884740
  4.5 1.9 copy-start.5
  6.4 1.6 copy-start.2
  6.9 2.6 copy-start.10
  6.9 2.6 copy-start.11
  8.1 2.3 copy-start.12
  8.1 2.9 copy-start.13
  8.1 3.5 %copy-start.14 = (bf16[3,768]{1,0:T(4,128)(2,1)S(1)}, bf16[3,768]{1,0:T(4,128)(2,1)}, u32[]{:S(2)}) copy-start(bf16[3,768]{1,0:T(4,128)(2,1)} %param.33) | copy-start | bytes 13828
  274.4 1.8 copy-start.6
  276.9 4.5 %copy-start = (bf16[768,768]{1,0:T(8,128)(2,1)S(1)}, bf16[768,768]{1,0:T(8,128)(2,1)}, u32[]{:S(2)}) copy-start(bf16[768,768]{1,0:T(8,128)(2,1)} %get-tuple-element.28) | copy-start | bytes 3538948
  281.5 3.2 %copy-start.1 = (f32[4,145,1024]{2,1,0:T(8,128)S(1)}, f32[4,145,1024]{2,1,0:T(8,128)}, u32[]{:S(2)}) copy-start(f32[4,145,1024]{2,1,0:T(8,128)} %get-tuple-element.36) | copy-start | bytes 7127044
  284.7 2.9 %copy-start.4 = (bf16[768,768]{1,0:T(8,128)(2,1)S(1)}, bf16[768,768]{1,0:T(8,128)(2,1)}, u32[]{:S(2)}) copy-start(bf16[768,768]{1,0:T(8,128)(2,1)} %get-tuple-element.32) | copy-start | bytes 3538948
  287.6 1.7 copy-start.3
  289.2 1.7 copy-start.8
  289.3 2.4 copy-start.7

commit v3 on v2

v3 whole, which is shorter than its diff:
```python
import functools
import math

import jax
import jax.numpy as jnp
from jax import lax
from jax.experimental import pallas as pl
from jax.experimental.pallas import tpu as pltpu
from jax.sharding import PartitionSpec as P

MESH = pl.DeviceIdType.MESH
HEAD = 64
LANES = 128
epsilon = 1e-06
DEV = set()
score_scale = 1.0 / math.sqrt(HEAD)
bf16, f32 = jnp.bfloat16, jnp.float32


def bit_of(d, b):
    return lax.rem(lax.div(d, jnp.int32(2 ** b)), jnp.int32(2))


def flip(d, b):
    return d + (1 - 2 * bit_of(d, b)) * (2 ** b)


def when(cond, fn):
    if cond is True:
        fn()
    else:
        pl.when(cond)(fn)


class Gather:
    def __init__(self, src, dst, row0, rows, order, pos, sems, base):
        self.src, self.dst, self.row0, self.order, self.pos = src, dst, row0, order, pos
        self.piece = rows // (2 ** len(order))
        self.zs, self.zr, self.ps, self.pr = sems
        self.base = base
        self.k = len(order)

    def win(self, s):
        w = jnp.int32(0)
        for i, b in enumerate(self.order):
            if i >= s:
                w = w + bit_of(self.pos.d, b) * (2 ** i)
        return pl.ds(pl.multiple_of(self.row0 + w * self.piece, 16), self.piece * 2 ** s)

    def shard(self, dr, j):
        return self.pos.z + j * (2 * dr - 1) * self.pos.sign

    def zcopy(self, dr, j):
        p = self.pos
        t, rows = self.shard(dr, j), self.win(0)
        src = self.src.at[rows] if j == 0 else self.dst.at[t, rows]
        real = dr + p.upper - 2 * dr * p.upper
        return pltpu.make_async_remote_copy(src, self.dst.at[t, rows], self.zs.at[self.base, real, j], self.zr.at[self.base, real, j], device_id=(p.d, p.z + (1 - 2 * dr) * p.sign), device_id_type=MESH)

    def pcopy(self, s, dr, j):
        p = self.pos
        part = self.dst.at[self.shard(dr, j), self.win(s)]
        return pltpu.make_async_remote_copy(part, part, self.ps.at[self.base, s, dr, j - 1], self.pr.at[self.base, s, dr, j - 1], device_id=(flip(p.d, self.order[s]), p.z), device_id_type=MESH)

    @staticmethod
    def has(cls, nz, dr, j):
        return cls >= j if dr == 0 else cls + j < nz

    @staticmethod
    def ahead(cls, dr):
        return dr == 0 or cls >= 1

    def item(self, cls, nz, st, dr, j):
        if st == -1:
            self.zcopy(dr, 0).start()
            return
        if st == 0:
            self.zcopy(dr, j - 1).wait_recv()
            if j <= nz - 2 and self.ahead(cls, dr):
                self.zcopy(dr, j).start()
        else:
            self.pcopy(st - 1, dr, j).wait_recv()
        if st < self.k:
            self.pcopy(st, dr, j).start()

    def finish(self, cls, nz):
        for dr in (0, 1):
            for j in range(nz - 1):
                if self.ahead(cls, dr) and self.has(cls, nz, dr, j):
                    self.zcopy(dr, j).wait_send()
            for s in range(self.k):
                for j in range(1, nz):
                    if self.has(cls, nz, dr, j):
                        self.pcopy(s, dr, j).wait_send()


def add_into(dst, src, rows):
    step = 32 if rows % 32 == 0 else 16

    def body(i, c):
        r = pl.ds(pl.multiple_of(i * step, step), step)
        dst[r, :] = dst[r, :] + src[r, :]
        return c
    lax.fori_loop(0, rows // step, body, 0)


def add_all(dst, src, count, rows):
    def body(t, c):
        add_into(dst.at[t], src.at[t], rows)
        return c
    lax.fori_loop(0, count, body, 0)


def op_rows(half, order, op):
    size = half
    for o in order:
        if o == "z":
            if op == "z":
                return size
        else:
            size //= 2
            if o == op:
                return size
    return size


class Reduce:
    def __init__(self, keep, recvs, line, extra, result, row, half, order, pos, nz, bits, sems, base):
        self.keep, self.recvs, self.line, self.extra = keep, recvs, line, extra
        self.result, self.row, self.half, self.order = result, row, half, order
        self.pos, self.nz, self.bits = pos, nz, bits
        self.ss, self.rs, self.ls = sems
        self.base = base
        self.slot = 2 * nz
        self.pending = []
        self.steps = []
        self.build()

    def copy(self, s, src, dst, to):
        return lambda: pltpu.make_async_remote_copy(src, dst, self.ss.at[self.base, s], self.rs.at[self.base, s], device_id=to, device_id_type=MESH)

    def remote(self, src, dst, b, keep=True):
        cp = self.copy(self.slot, src, dst, (flip(self.pos.d, b), self.pos.z))
        self.slot += 1
        if keep:
            self.pending.append(cp)
        return cp

    def build(self):
        d, z, nz = self.pos.d, self.pos.z, self.nz
        prev = lambda: None
        start, size, whole = jnp.int32(0), self.half, True
        taken = []

        def then(prev, cp):
            def step():
                prev()
                cp().start()
            self.steps.append(step)

        for op in self.order:
            if op == "z":
                self.rows = pl.ds(start, size)
                self.size = size
                self.steps.append(prev)
                prev, whole = (lambda: None), False
                continue
            size //= 2
            m = bit_of(d, op)
            keep0 = pl.multiple_of(start + m * size, 16)
            send0 = pl.multiple_of(start + (1 - m) * size, 16)
            buf = self.recvs[op]
            if whole:
                cp = self.remote(self.keep.at[:, pl.ds(send0, size), :], buf, op)
            else:
                cp = self.remote(self.keep.at[z, pl.ds(send0, size), :], buf.at[0], op)
            then(prev, cp)

            def prev(cp=cp, keep0=keep0, size=size, whole=whole, buf=buf):
                cp().wait_recv()
                if whole:
                    add_all(self.keep.at[:, pl.ds(keep0, size), :], buf, nz, size)
                else:
                    add_into(self.keep.at[z, pl.ds(keep0, size), :], buf.at[0], size)
            taken.append(op)
            start = keep0
        for e, b in enumerate(self.bits[3:]):
            cp = self.remote(self.keep.at[z, pl.ds(start, size), :], self.extra.at[e], b, False)

            def prev(before=prev, cp=cp, e=e, start=start, size=size):
                before()
                cp().start()
                cp().wait()
                add_into(self.keep.at[z, pl.ds(start, size), :], self.extra.at[e], size)
        at = pl.multiple_of(self.row + start, 16)
        total = self.keep.at[z, pl.ds(start, size), :]
        win = self.result.at[pl.ds(at, size), :]
        own = lambda win=win: pltpu.make_async_copy(total, win, self.ls.at[self.base])
        op = taken[-1]
        cp = self.remote(total, win, op)

        def step(prev=prev, cp=cp):
            prev()
            own().start()
            cp().start()
        self.steps.append(step)

        def prev(cp=cp):
            cp().wait_recv()
            own().wait()
        for nxt in taken[-2::-1] + [self.bits[0]]:
            at = pl.multiple_of(at - bit_of(d, op) * size, 16)
            size *= 2
            op = nxt
            win = self.result.at[pl.ds(at, size), :]
            cp = self.remote(win, win, op)
            then(prev, cp)
            prev = lambda cp=cp: cp().wait_recv()
        self.steps.append(prev)

    def hop(self, kind, i):
        p, nz = self.pos, self.nz
        far, near = nz - 1 - i, i
        if kind == 1:
            t = far * (1 - p.upper) + near * p.upper
            flow, to = p.upper, p.z + p.sign
        else:
            t = near * (1 - p.upper) + far * p.upper
            flow, to = 1 - p.upper, p.z - p.sign
        cell = self.keep.at[t, self.rows, :]
        land = self.line.at[flow, nz - 2 - i]
        s = flow * nz + i
        cp = lambda: pltpu.make_async_remote_copy(cell, land, self.ss.at[self.base, s], self.rs.at[self.base, s], device_id=(p.d, to), device_id_type=MESH)
        return cp, cell, land

    def sends(self, cls, kind):
        return self.nz - 1 - cls if kind == 1 else cls

    def along(self, cls, kind, i):
        if kind == 1 and cls == 0:
            for k in range(self.nz - 1):
                self.hop(1, k)[0]().start()
            return
        cp, cell, land = self.hop(kind, i)
        cp().wait_recv()
        add_into(cell, land, self.size)
        if i < self.sends(cls, kind):
            cp().start()

    def finish(self, cls):
        for cp in self.pending:
            cp().wait_send()
        for kind in (1, 2):
            for i in range(self.sends(cls, kind)):
                self.hop(kind, i)[0]().wait_send()


def enter(d, z, nz, bits):
    bar = pltpu.get_barrier_semaphore()
    for b in bits:
        pl.semaphore_signal(bar, inc=1, device_id=(flip(d, b), z), device_id_type=MESH)
    for o in range(1, nz):
        pl.semaphore_signal(bar, inc=1, device_id=(d, lax.rem(z + o, jnp.int32(nz))), device_id_type=MESH)
    pl.semaphore_wait(bar, len(bits) + nz - 1)


def dot(a, b):
    return lax.dot_general(a, b, (((1,), (0,)), ((), ())), preferred_element_type=f32)


def dot_nt(a, b):
    return lax.dot_general(a, b, (((1,), (1,)), ((), ())), preferred_element_type=f32)


def dot_tn(a, b):
    return lax.dot_general(a, b, (((0,), (0,)), ((), ())), preferred_element_type=f32)


def norm_forward(h, gain, shift):
    centred = h - jnp.mean(h, -1, keepdims=True)
    inverse = lax.rsqrt(jnp.mean(centred * centred, -1, keepdims=True) + epsilon)
    normed = centred * inverse
    return normed * gain + shift, normed, inverse


def norm_backward(grad, normed, inverse, gain):
    scaled = grad * gain
    return inverse * (scaled - jnp.mean(scaled, -1, keepdims=True) - normed * jnp.mean(scaled * normed, -1, keepdims=True))


def col_sum(v):
    return jnp.sum(v, axis=0, keepdims=True)


class Dims:
    pass


def layer_kernel(m, *refs):
    n_in, n_out = len(m.inputs), len(m.outputs)
    R = dict(zip(m.inputs + m.outputs + m.scratch, refs))
    g = Dims()
    for k, v in R.items():
        setattr(g, k, v)
    ni, L, T, D, nz, hp, nh, KP, NP = m.ni, m.L, m.T, m.D, m.nz, m.hp, m.nh, m.KP, m.NP
    d, z = lax.axis_index("dp"), lax.axis_index("mp")
    core = bit_of(d, m.bits[0])
    partner = flip(d, m.bits[0])

    def shard(o):
        t = z
        for b in range(nz.bit_length() - 1):
            t = t + lax.rem(lax.div(o, jnp.int32(2 ** b)), jnp.int32(2)) * (1 - 2 * bit_of(z, b)) * (2 ** b)
        return t

    g.DCQ = g.HD.at[:, :, 0:hp]
    g.DQ = g.DP.at[:, :, 0:m.QW]

    pos = Dims()
    pos.d, pos.z = d, z
    pos.upper = lax.div(2 * z, jnp.int32(nz))
    pos.sign = 1 - 2 * pos.upper
    kind = z * (1 - pos.upper) + (nz - 1 - z) * pos.upper
    classes = range(nz // 2)

    g.VG[z] = g.vown[...]
    enter(d, z, nz, m.bits)
    gsem = (g.zs, g.zr, g.ps, g.pr)
    own = {"A": g.A, "B": g.B, "O": g.O, "H": g.H, "W": g.W, "V": g.vown}
    far = {"A": g.GA, "B": g.GB, "O": g.GO, "H": g.GH, "W": g.GW, "V": g.VG}
    gathers = [Gather(own[k], far[k], r0, rows, order, pos, gsem, c) for c, (k, r0, rows, order) in enumerate(m.gather_plan)]
    calls = [0, 0]

    def gather_steps():
        at = calls[0]
        calls[0] += 1
        if "nog" in DEV:
            return
        for cls in classes:
            todo = m.gather_steps[cls][at]
            if todo:
                @pl.when(kind == cls)
                def _():
                    for c, st, dr, j in todo:
                        gathers[c].item(cls, nz, st, dr, j)

    def reduce_steps():
        at = calls[1]
        calls[1] += 1
        if "nor" in DEV:
            return
        for cls in classes:
            todo = m.reduce_steps[cls][at]
            if todo:
                @pl.when(kind == cls)
                def _():
                    for c, what in todo:
                        i = progress[cls, c, what]
                        progress[cls, c, what] += 1
                        if what == 0:
                            chunks[c].steps[i]()
                        else:
                            chunks[c].along(cls, what, i)

    def after_each(steps):
        def between(o):
            for q in range(nz - 1):
                pl.when(o == q)(lambda: steps())
        return between

    def finish_gather():
        if "nog" not in DEV:
            for cls in classes:
                @pl.when(kind == cls)
                def _():
                    for q in gathers:
                        q.finish(cls, nz)

    pair_slot = [0]

    def pair(ref, rows):
        s = pair_slot[0]
        pair_slot[0] += 1
        return pltpu.make_async_remote_copy(ref.at[pl.ds(0, rows)], ref.at[pl.ds(rows, rows)], g.cs.at[s], g.cr.at[s], device_id=(partner, z), device_id_type=MESH)

    def place(block, slot):
        buf, sem, key, rows, cols = block
        return buf.at[slot, pl.ds(0, rows[1]), pl.ds(*cols)], sem.at[slot]

    def fetch(block, slot, o):
        buf, sem, key, rows, cols = block
        dst, done = place(block, slot)
        r, c = pl.ds(*rows), pl.ds(*cols)

        def mine():
            pltpu.make_async_copy(own[key].at[r, c], dst, done).start()

        def other():
            pltpu.make_async_copy(far[key].at[shard(o), r, c], dst, done).start()
        if isinstance(o, int):
            mine()
        else:
            pl.when(o == 0)(mine)
            pl.when(o != 0)(other)

    def arrived(block, slot):
        buf, sem, key, rows, cols = block
        dst, done = place(block, slot)
        pltpu.make_async_copy(own[key].at[pl.ds(*rows), pl.ds(*cols)], dst, done).wait()

    def stream(blocks, body, between, ahead):
        def step(o, c):
            slot = lax.rem(o, jnp.int32(2))

            @pl.when(o + 1 < nz)
            def _():
                for b in blocks:
                    fetch(b, 1 - slot, o + 1)

            @pl.when(o + 1 == nz)
            def _():
                for b in ahead:
                    fetch(b, 0, 0)
            for b in blocks:
                arrived(b, slot)
            body(o, slot)
            between(o)
            return c
        lax.fori_loop(0, nz, step, 0)

    FZ, PW, BW = m.FZ, m.PW, m.BW
    self_blocks = [(g.SA, g.sa, "A", (0, D), (LANES, D - LANES)), (g.SO, g.so, "O", (0, hp), (0, D))]
    cross_blocks = [(g.SA, g.sa, "A", (0, D), (0, hp)), (g.SB, g.sb, "B", (0, PW), (0, BW)), (g.SO, g.so, "O", (LANES, hp), (0, D))]
    hidden_blocks = [(g.SA, g.sa, "H", (0, D), (0, FZ))]
    output_blocks = [(g.SA, g.sa, "W", (0, FZ), (0, D))]
    back_blocks = output_blocks + [(g.SH, g.sh, "H", (0, D), (0, FZ))]
    self_back = [(g.SA, g.sa, "A", (0, D), (LANES, D - LANES)), (g.SO, g.so, "O", (0, hp), (0, D))]
    for b in self_blocks:
        fetch(b, 0, 0)

    lane = lax.broadcasted_iota(jnp.int32, (L, hp), 1)
    low = [lane // HEAD == h for h in range(nh)]
    high = [lane // HEAD == h + 1 for h in range(nh)]

    def stack(v, masks):
        return jnp.concatenate([jnp.where(k, v, 0.0) for k in masks], axis=0).astype(bf16)

    def unstack(v, masks):
        out = jnp.where(masks[0], v[0:L], 0.0)
        for h in range(1, nh):
            out = out + jnp.where(masks[h], v[h * L:(h + 1) * L], 0.0)
        return out

    def softmax(s):
        e = jnp.exp(s - jnp.max(s, -1, keepdims=True))
        return e / jnp.sum(e, -1, keepdims=True)

    for i in range(ni):
        g.XF[i * L:(i + 1) * L] = g.x[i].astype(f32)
        g.PT[i * KP:i * KP + NP] = g.patches[i]
        g.PT[i * KP + NP // 16 * 16:(i + 1) * KP] = jnp.concatenate([g.patches[i, NP // 16 * 16:NP].astype(f32), jnp.zeros((KP - NP, m.PW), f32)], 0).astype(bf16)
    g.X[0:T] = g.XF[...].astype(bf16)
    swaps = [pair(g.X, T), pair(g.PT, ni * KP)]
    for s in swaps:
        s.start()

    g.ACC[...] = jnp.zeros((T, D), f32)
    gather_steps()

    def self_forward(o, slot):
        t = shard(o)
        bias = g.VG[t].astype(f32)[0:1, LANES:]
        qkv = (dot(g.X[0:T], g.SA[slot, :, LANES:]) + bias).astype(bf16)
        g.QKV[o] = qkv
        qf = qkv.astype(f32)
        outs = []
        for i in range(ni):
            r = slice(i * L, (i + 1) * L)
            qs = stack(qf[r, 0:hp], high)
            k_i = qf[r, 3 * LANES:3 * LANES + hp].astype(bf16)
            v_i = qf[r, 2 * LANES:2 * LANES + hp].astype(bf16)
            p = softmax(dot_nt(qs, k_i) * score_scale)
            g.PS[o * ni + i] = p
            outs.append(unstack(dot(p.astype(bf16), v_i), low))
        mixed = jnp.concatenate(outs, 0).astype(bf16)
        g.MX[0, o, 0:T] = mixed
        g.ACC[...] += dot(mixed, g.SO[slot])

    stream(self_blocks, self_forward, after_each(gather_steps), cross_blocks)

    def out_row(j):
        return g.ob[j:j + 1, :], g.gain[j:j + 1, :], g.shift[j:j + 1, :]

    ob, gn, sh = out_row(0)
    first, normed, inv = norm_forward(g.XF[...] + g.ACC[...] + ob, gn, sh)
    g.NM[0] = normed
    g.INV[0] = jnp.broadcast_to(inv, (T, LANES))
    g.F[0:T] = first.astype(bf16)
    g.ACC[...] = jnp.zeros((T, D), f32)
    gather_steps()

    key_pos = lax.broadcasted_iota(jnp.int32, (nh * L, KP), 1)

    def cross_forward(o, slot):
        t = shard(o)
        vb = g.VG[t].astype(f32)
        cq = (dot(g.F[0:T], g.SA[slot, :, 0:hp]) + vb[0:1, 0:hp]).astype(bf16)
        g.CQ[o] = cq
        cqf = cq.astype(f32)
        kv = (dot(g.PT[0:ni * KP], g.SB[slot]) + vb[1:2, 0:m.BW]).astype(bf16)
        g.KV[o] = kv
        outs = []
        for i in range(ni):
            qs = stack(cqf[i * L:(i + 1) * L], low)
            kvi = g.KV[o, i * KP:(i + 1) * KP]
            s = dot_nt(qs, kvi[:, 0:hp]) * score_scale
            s = jnp.where(key_pos < g.rows[z * ni + i], s, -1e30)
            p = softmax(s)
            g.PC[o * ni + i] = p
            outs.append(unstack(dot(p.astype(bf16), kvi[:, LANES:LANES + hp]), high))
        mixed = jnp.concatenate(outs, 0).astype(bf16)
        g.MX[1, o, 0:T] = mixed
        g.ACC[...] += dot(mixed, g.SO[slot])

    stream(cross_blocks, cross_forward, after_each(gather_steps), hidden_blocks)
    ob, gn, sh = out_row(1)
    second, normed, inv = norm_forward(g.F[0:T].astype(f32) + g.ACC[...] + ob, gn, sh)
    g.NM[1] = normed
    g.INV[1] = jnp.broadcast_to(inv, (T, LANES))
    g.S2[0:T] = second.astype(bf16)
    gather_steps()
    other = g.MX.at[1 - core]
    mix_swap = pltpu.make_async_remote_copy(other.at[:, pl.ds(0, T)], other.at[:, pl.ds(T, T)], g.cs.at[m.swaps - 1], g.cr.at[m.swaps - 1], device_id=(partner, z), device_id_type=MESH)
    mix_swap.start()
    swaps += [pair(g.F, T), pair(g.S2, T)]
    for s in swaps[2:4]:
        s.start()

    def hidden_forward(o, slot):
        t = shard(o)
        pre = dot(g.S2[0:T], g.SA[slot]) + g.VG[t].astype(f32)[2:3, :]
        cdf = 0.5 * (1.0 + lax.erf(pre * math.sqrt(0.5)))
        g.GP[o] = cdf + pre * jnp.exp(-0.5 * pre * pre) * (1.0 / math.sqrt(2.0 * math.pi))
        g.HD[o, 0:T] = (pre * cdf).astype(bf16)

    stream(hidden_blocks, hidden_forward, after_each(gather_steps), output_blocks)
    hid_swaps = [pair(g.HD.at[o], T) for o in range(nz)]
    for s in hid_swaps:
        s.start()
    g.ACC[...] = jnp.zeros((T, D), f32)
    gather_steps()

    def output_forward(o, slot):
        g.ACC[...] += dot(g.HD[o, 0:T], g.SA[slot])

    stream(output_blocks, output_forward, after_each(gather_steps), back_blocks)
    gather_steps()
    ob, gn, sh = out_row(2)
    final, normed, inv = norm_forward(g.S2[0:T].astype(f32) + g.ACC[...] + ob, gn, sh)
    g.layer_out[...] = final.reshape(ni, L, D)

    if "fwd" in DEV:
        for cp in swaps + hid_swaps + [mix_swap]:
            cp.wait()
        finish_gather()
        return
    for i in range(ni):
        g.ACC[i * L:(i + 1) * L] = g.cot[i].astype(f32)
    cot = g.ACC[...]
    g.SM[...] = jnp.zeros(g.SM.shape, f32)

    def record(j, grad_in, grad_out, normed):
        g.SM[j:j + 1] = col_sum(grad_in)
        g.SM[3 + j:4 + j] = col_sum(grad_out * normed)
        g.SM[6 + j:7 + j] = col_sum(grad_out)

    third = norm_backward(cot, normed, inv, gn)
    record(2, third, cot, normed)
    g.G3[0:T] = third.astype(bf16)
    swap3 = pair(g.G3, T)
    swap3.start()

    rsem = (g.ss, g.rs, g.ls)
    results = {"A": g.RA, "B": g.RB, "O": g.RO, "H": g.RH, "W": g.RW}
    chunks = []
    progress = {}
    for c, (k, h0, half, order) in enumerate(m.reduce_plan):
        recvs = {b: R[f"rv{c}_{b}"] for b in m.bits[1:3]}
        whole = m.rows[k] // 2
        chunks.append(Reduce(R[f"kp{c}"], recvs, R[f"ln{c}"], R.get(f"ex{c}"), results[k], core * whole + h0, half, order, pos, nz, m.bits, rsem, c))
        for cls in classes:
            for what in range(3):
                progress[cls, c, what] = 0

    def half_columns(whole):
        return pl.ds(pl.multiple_of(core * whole, LANES), whole)

    def deal(k, t, value):
        for c, p in enumerate(m.reduce_plan):
            if p[0] == k:
                R[f"kp{c}"][t] = value[p[1]:p[1] + p[2]].astype(bf16)

    reduce_steps()

    swap3.wait_recv()
    for s in hid_swaps:
        s.wait_recv()
    reduce_steps()

    def job_w(o, c):
        t = shard(o)
        deal("W", t, dot_tn(g.HD[o, :, half_columns(m.FZ // 2)], g.G3[...]))
        return c
    if "skip_job_w" not in DEV:
        lax.fori_loop(0, nz, job_w, 0)
    for s in hid_swaps:
        s.wait_send()
    reduce_steps()
    g.ACC[...] = third

    def loop_send(ref, rows, kind, o):
        pltpu.make_async_remote_copy(ref.at[o, pl.ds(0, rows)], ref.at[o, pl.ds(rows, rows)], g.ds.at[kind, o], g.dr.at[kind, o], device_id=(partner, z), device_id_type=MESH).start()

    def hidden_backward(o, slot):
        t = shard(o)
        pre = (dot_nt(g.G3[0:T], g.SA[slot]) * g.GP[o]).astype(bf16)
        g.DP[o, 0:T] = pre
        g.SM[pl.ds(9 + t, 1)] = col_sum(pre.astype(f32))
        loop_send(g.DP, T, 0, o)
        g.ACC[...] += dot_nt(pre, g.SH[slot])

    stream(back_blocks, hidden_backward, after_each(reduce_steps), cross_blocks)
    reduce_steps()

    def loop_wait(ref, rows, kind):
        for o in range(nz):
            cp = pltpu.make_async_remote_copy(ref.at[o, pl.ds(0, rows)], ref.at[o, pl.ds(rows, rows)], g.ds.at[kind, o], g.dr.at[kind, o], device_id=(partner, z), device_id_type=MESH)
            cp.wait()

    gn = g.gain[1:2, :]
    normed, inv = g.NM[1], g.INV[1][:, 0:1]
    grad = g.ACC[...]
    secondg = norm_backward(grad, normed, inv, gn)
    record(1, secondg, grad, normed)
    g.G12[1, 0:T] = secondg.astype(bf16)
    swap2 = pair(g.G12.at[1], T)
    swap2.start()
    reduce_steps()
    loop_wait(g.DP, T, 0)
    swaps[3].wait_recv()

    def job_h(o, c):
        t = shard(o)
        deal("H", t, dot_tn(g.S2[:, half_columns(D // 2)], g.DP[o]))
        return c
    if "skip_job_h" not in DEV:
        lax.fori_loop(0, nz, job_h, 0)
    reduce_steps()

    g.ACC[...] = secondg
    g.patch_grad[...] = jnp.zeros(g.patch_grad.shape, f32)

    def backward_unit(qs, k_i, v_i, p, ms, masks):
        grad_v = dot_tn(p.astype(bf16), ms)
        grad_p = dot_nt(ms, v_i)
        gs = (p * (grad_p - jnp.sum(p * grad_p, -1, keepdims=True))).astype(bf16)
        grad_q = unstack(dot(gs, k_i), masks) * score_scale
        grad_k = dot_tn(gs, qs) * score_scale
        return grad_q, grad_k.astype(bf16).astype(f32), grad_v.astype(bf16).astype(f32)

    def cross_backward(o, slot):
        t = shard(o)
        gm = dot_nt(g.G12[1, 0:T], g.SO[slot]).astype(bf16).astype(f32)
        cqf = g.CQ[o].astype(f32)
        grads = []
        for i in range(ni):
            r = slice(i * L, (i + 1) * L)
            kvi = g.KV[o, i * KP:(i + 1) * KP]
            gq, gk, gv = backward_unit(stack(cqf[r], low), kvi[:, 0:hp], kvi[:, LANES:LANES + hp], g.PC[o * ni + i], stack(gm[r], high), low)
            grads.append(gq)
            g.DKV[o, i * KP:(i + 1) * KP] = jnp.concatenate([gk[:, 0:LANES], gk[:, LANES:] + gv[:, 0:LANES], gv[:, LANES:]], 1).astype(bf16)
        dcq = jnp.concatenate(grads, 0).astype(bf16)
        g.DCQ[o, 0:T] = dcq
        loop_send(g.DCQ, T, 1, o)
        loop_send(g.DKV, ni * KP, 2, o)
        dkv = g.DKV[o, 0:ni * KP]
        g.SM[pl.ds(9 + nz + t, 1), 0:hp] = col_sum(dcq.astype(f32))
        g.SM[pl.ds(9 + 2 * nz + t, 1), 0:m.BW] = col_sum(dkv.astype(f32))
        g.ACC[...] += dot_nt(dcq, g.SA[slot, :, 0:hp])
        for i in range(ni):
            g.patch_grad[i] += dot_nt(g.DKV[o, i * KP:(i + 1) * KP], g.SB[slot])[0:NP]

    stream(cross_blocks, cross_backward, after_each(reduce_steps), self_blocks)
    reduce_steps()
    gn = g.gain[0:1, :]
    normed, inv = g.NM[0], g.INV[0][:, 0:1]
    grad = g.ACC[...]
    firstg = norm_backward(grad, normed, inv, gn)
    record(0, firstg, grad, normed)
    g.G12[0, 0:T] = firstg.astype(bf16)
    swap1 = pair(g.G12.at[0], T)
    swap1.start()
    reduce_steps()
    loop_wait(g.DCQ, T, 1)
    loop_wait(g.DKV, ni * KP, 2)
    swaps[1].wait_recv()

    def job_b(o, c):
        t = shard(o)
        deal("B", t, dot_tn(g.PT[:, half_columns(m.PW // 2)], g.DKV[o]))
        return c
    if "skip_job_b" not in DEV:
        lax.fori_loop(0, nz, job_b, 0)
    reduce_steps()

    g.ACC[...] = firstg

    def self_backward(o, slot):
        t = shard(o)
        gm = dot_nt(g.G12[0, 0:T], g.SO[slot]).astype(bf16).astype(f32)
        qf = g.QKV[o].astype(f32)
        gqs, gks, gvs = [], [], []
        for i in range(ni):
            r = slice(i * L, (i + 1) * L)
            k_i = qf[r, 3 * LANES:3 * LANES + hp].astype(bf16)
            v_i = qf[r, 2 * LANES:2 * LANES + hp].astype(bf16)
            gq, gk, gv = backward_unit(stack(qf[r, 0:hp], high), k_i, v_i, g.PS[o * ni + i], stack(gm[r], low), high)
            gqs.append(gq)
            gks.append(gk)
            gvs.append(gv)
        gq, gk, gv = (jnp.concatenate(v, 0) for v in (gqs, gks, gvs))
        dq = jnp.concatenate([gq, gv[:, 0:LANES], gv[:, LANES:] + gk[:, 0:LANES], gk[:, LANES:]], 1).astype(bf16)
        g.DQ[o, 0:T] = dq
        loop_send(g.DQ, T, 3, o)
        g.SM[pl.ds(9 + 3 * nz + t, 1), 0:m.QW] = col_sum(dq.astype(f32))
        g.ACC[...] += dot_nt(dq, g.SA[slot, :, LANES:])

    stream(self_blocks, self_backward, after_each(reduce_steps), [])
    g.text_grad[...] = g.ACC[...].reshape(ni, L, D)
    reduce_steps()
    loop_wait(g.DQ, T, 3)
    swap1.wait_recv()
    swap2.wait_recv()
    for s in swaps[0:1] + swaps[2:3] + [mix_swap]:
        s.wait_recv()

    def job_o(o, c):
        t = shard(o)
        g.TMP[...] = dot_tn(g.MX[core, o], g.G12[core])
        deal("O", t, g.TMP[pl.ds(pl.multiple_of(core * HEAD, 16), m.rows["O"] // 2)])
        return c
    if "skip_job_o" not in DEV:
        lax.fori_loop(0, nz, job_o, 0)
    reduce_steps()

    def job_a(o, c):
        t = shard(o)
        cols = half_columns(D // 2)
        left = dot_tn(g.F[:, cols], g.DCQ[o])
        right = dot_tn(g.X[:, cols], g.DQ[o])
        deal("A", t, jnp.concatenate([left[:, 0:LANES], left[:, LANES:] + right[:, 0:LANES], right[:, LANES:]], 1))
        return c
    if "skip_job_a" not in DEV:
        lax.fori_loop(0, nz, job_a, 0)
    reduce_steps()

    sends = []
    for i, b in enumerate(m.bits):
        cp = pltpu.make_async_remote_copy(g.SM, g.SR.at[i], g.ms.at[i], g.mr.at[i], device_id=(flip(d, b), z), device_id_type=MESH)
        cp.start()
        if i < 3:
            reduce_steps()
        cp.wait()
        g.SM[...] += g.SR[i]
    g.SZ[z] = g.SM[...]
    nb = len(m.bits)
    for o in range(1, nz):
        to = lax.rem(z + o, jnp.int32(nz))
        cp = pltpu.make_async_remote_copy(g.SM, g.SZ.at[z], g.ms.at[nb + o], g.zm.at[z], device_id=(d, to), device_id_type=MESH)
        cp.start()
        sends.append(cp)
    reduce_steps()
    reduce_steps()
    for o in range(1, nz):
        frm = lax.rem(z + o, jnp.int32(nz))
        pltpu.make_async_remote_copy(g.SM, g.SZ.at[frm], g.ms.at[nb + o], g.zm.at[frm], device_id=(d, frm), device_id_type=MESH).wait_recv()
    total = g.SZ[0]
    for t in range(1, nz):
        total = total + g.SZ[t]
    g.small[...] = total
    assert calls == [len(m.gather_steps[0]), len(m.reduce_steps[0])], calls

    for cp in sends + swaps + [swap1, swap2, swap3, mix_swap]:
        cp.wait_send()
    finish_gather()
    if "nor" not in DEV:
        for cls in classes:
            @pl.when(kind == cls)
            def _():
                for c in chunks:
                    c.finish(cls)


GATHER_PLAN = (("V", 0, 16, ""), ("O", 0, 384, "xyc"), ("W", 0, 256, "xc"), ("A", 384, 384, "yxc"), ("B", 0, 256, "xc"), ("A", 0, 384, "xyc"), ("B", 640, 384,
    "xc"), ("H", 0, 768, "xyc"), ("B", 256, 384, "yc"), ("W", 256, 256, "xyc"), ("W", 512, 256, "xc"))
GATHER_ORDER = ((0, 40, 120, 200, 13, 53, 133, 213, 61, 14, 141, 54, 160, 221, 134, 69, 214, 15, 149, 77, 55, 320, 280, 62, 229, 240, 157, 173, 222, 142, 135, 237,
    63, 215, 181, 174, 70, 189, 78, 150, 293, 230, 223, 333, 158, 143, 182, 238, 175, 190, 253, 71, 301, 334, 79, 360, 231, 400, 151, 294, 183, 341, 239,
    254, 159, -1, 261, 349, 335, 191, -1, 302, 295, 269, 80, -1, 309, 262, 255, 342, 373, -1, 343, 413, 317, 303, 270, 374, 350, 351, 263, 381, 414, 271,
    -1, 310, 375, 421, 382, 93, -1, 318, 422, 415, -1, 383, 101, 94, 429, 430, 311, -1, 389, 109, 95, 423, 319, -1, 102, 397, -1, 390, 431, -1, 391, 110,
    103, -1, 398, 399, 111, -1, -1, -1, -1), (0, 4, 40, 44, 120, 124, 200, 204, 9, 13, 49, 53, 129, 133, 209, 213, 57, 14, 61, 137, 54, 160, 164, 217,
    141, 134, 221, 169, 214, 173, 65, 320, 280, 284, 324, 145, 174, 73, 240, 244, 69, 62, 153, 329, 333, 77, 225, 149, 177, 289, 293, 142, 233, 222, 157,
    249, 253, 185, 181, 334, 229, 182, 189, 237, 190, 294, 297, 70, 254, 337, 78, 345, 301, 341, 360, 364, 400, 404, 349, 369, 230, 150, 373, 257, 342,
    238, 409, 413, 158, -1, 265, 261, 350, 374, 80, 84, -1, 302, 269, 414, -1, 305, 262, 377, 381, 89, 93, -1, 417, 313, 270, -1, 309, 382, 94, 425, 421,
    -1, 317, 422, -1, 310, 97, 429, 430, -1, 318, 385, 101, 102, -1, 389, 105, -1, 393, 109, 110, -1, 397, 390, -1, 398, -1, -1, -1, -1))
REDUCE_PLAN = (("W", 128, "xzy"), ("W", 128, "yxz"), ("W", 128, "zyx"), ("H", 192, "xyz"), ("H", 64, "yxz"), ("H", 128, "yxz"), ("B", 320, "zxy"), ("B", 192,
    "yxz"), ("O", 64, "xyz"), ("O", 64, "yzx"), ("O", 64, "xzy"), ("A", 128, "yxz"), ("A", 128, "yxz"), ("A", 128, "xzy"))
REDUCE_ORDER = ((-1, -1, 3, 6, 7, 0, -1, -1, -1, -1, -1, -1, 9, 12, 15, -1, -1, 3, 0, 1, -1, 12, -1, -1, -1, 18, 19, 21, -1, 9, 8, 6, 15, -1, -1, 3, 4, 2, 0, -1, 21,
    12, 13, -1, 30, 27, 24, -1, 39, 33, 36, 15, 16, -1, 21, 22, 9, 10, 6, -1, 0, -1, 30, 31, -1, 27, 28, 20, 18, 24, -1, 5, 3, 14, 12, 33, 17, 15, 39, 40,
    23, 21, 6, 18, 3, 12, 11, 9, 36, 0, 32, 30, 33, 34, 24, 25, 29, 27, 15, 18, 21, 6, 3, 12, 3, 12, 9, 30, 36, 37, 41, 39, 15, 0, 27, 18, 35, 33, 15, 0,
    21, 26, 24, 9, 21, 27, 6, 30, 9, 39, 6, 38, 18, 36, 24, 33, 27, 18, 30, 39, 27, 36, 30, 24, 33, 24, 39, 33, 36, 39, 36), (-1, -1, 3, 6, 0, -1, -1, -1,
    -1, -1, -1, 9, 12, 7, 15, -1, 3, 7, 0, -1, -1, 12, 7, 8, -1, 8, 6, 1, 1, -1, -1, 18, 21, 9, 1, 2, 15, -1, 6, 2, 0, -1, 3, 19, -1, 12, -1, 21, -1, 19,
    30, 27, 6, 24, 15, -1, 39, 20, 21, 9, 33, 0, 36, -1, 19, 4, -1, 20, 18, 30, 13, 13, 27, 13, 4, 4, 5, 6, 16, -1, 14, 14, 12, 24, 5, 3, 22, 16, 16, -1,
    22, 22, 17, 23, -1, 10, 10, 23, 21, 33, 0, 17, 15, 10, 31, 39, 11, 31, 31, 11, 9, 18, 28, 32, 12, 28, 32, 30, 3, 28, 21, 36, 29, 29, 40, 27, 6, 6, 40,
    33, 24, 9, 41, 40, 0, 18, 34, 15, 41, 39, 12, 34, 0, 30, 34, 12, 25, 35, 25, 3, 25, 35, 33, 36, 27, 26, 21, 3, 37, 26, 24, 18, 37, 21, 37, 9, 38, 15,
    33, 38, 39, 27, 9, 36, 30, 15, 24, 18, 33, 36, 39, 18, 30, 33, 27, 24, 30, 27, 24, 36, 39, 36, 39))


def unpack(orders, decode):
    out = []
    for order in orders:
        parts = [[]]
        for code in order:
            if code < 0:
                parts.append([])
            else:
                parts[-1].append(decode(code))
        out.append(parts)
    return out


def gather_code(code):
    return code // 40, code // 8 % 5 - 1, code // 4 % 2, code % 4


def reduce_code(code):
    return code // 3, code % 3


def plans(m):
    link = dict(zip("cxy", m.bits[:3]), z="z")
    m.gather_plan = [(k, r0, rows, tuple(link[o] for o in order)) for k, r0, rows, order in GATHER_PLAN]
    m.gather_steps = unpack(GATHER_ORDER, gather_code)
    m.reduce_plan = []
    at = {}
    for k, half, order in REDUCE_PLAN:
        h0 = at.get(k, 0)
        at[k] = h0 + half
        m.reduce_plan.append((k, h0, half, tuple(link[o] for o in order)))
    m.reduce_steps = unpack(REDUCE_ORDER, reduce_code)
    assert all(at[k] * 2 == m.rows[k] for k in at) and m.nz == 4


def run_layer(m, nd, shards, vown, x, patches, rows, cot, ob, gain, shift):
    nz = m.nz
    ni, L, D = x.shape
    T = ni * L
    m.ni, m.L, m.D, m.T = ni, L, D, T
    m.NP, m.PW = patches.shape[1:]
    m.KP = (m.NP + 15) // 16 * 16
    hw = D // nz
    m.nh = hw // HEAD
    m.hp = (hw + HEAD + LANES - 1) // LANES * LANES
    hp, KP, PW = m.hp, m.KP, m.PW
    A, B, O, H, W = shards
    m.BW, m.QW, m.FZ = B.shape[1], D - LANES, W.shape[0]
    FZ = m.FZ
    m.rows = {k: s.shape[0] for k, s in zip("ABOHW", shards)}
    lanes = {k: s.shape[1] for k, s in zip("ABOHW", shards)}
    plans(m)
    m.swaps = nz + 9
    V, sem = pltpu.VMEM, pltpu.SemaphoreType.DMA
    nc, ng = len(m.reduce_plan), len(m.gather_plan)
    nb = len(m.bits)
    sums = (9 + 4 * nz + 7) // 8 * 8
    scratch = dict(
        VG=V((nz, 16, D), bf16), XF=V((T, D), f32), X=V((2 * T, D), bf16), PT=V((2 * ni * KP, PW), bf16),
        SA=V((2, D, D), bf16), SH=V((2, D, D), bf16), SB=V((2, PW, m.BW), bf16), SO=V((2, hp, D), bf16),
        ACC=V((T, D), f32), QKV=V((nz, T, m.QW), bf16), PS=V((nz * ni, m.nh * L, L), f32), MX=V((2, nz, 2 * T, hp), bf16),
        NM=V((2, T, D), f32), INV=V((2, T, LANES), f32), F=V((2 * T, D), bf16), S2=V((2 * T, D), bf16),
        CQ=V((nz, T, hp), bf16), KV=V((nz, ni * KP, m.BW), bf16), PC=V((nz * ni, m.nh * L, KP), f32),
        GP=V((nz, T, FZ), f32), HD=V((nz, 2 * T, FZ), bf16), SM=V((sums, D), f32), G3=V((2 * T, D), bf16), DP=V((nz, 2 * T, FZ), bf16),
        G12=V((2, 2 * T, D), bf16), DKV=V((nz, 2 * ni * KP, m.BW), bf16),
        TMP=V((hp, D), f32), SR=V((nb, sums, D), f32), SZ=V((nz, sums, D), f32),
        zs=sem((ng, 2, nz)), zr=sem((ng, 2, nz)), ps=sem((ng, 3, 2, nz)), pr=sem((ng, 3, 2, nz)),
        cs=sem((m.swaps,)), cr=sem((m.swaps,)), ds=sem((4, nz)), dr=sem((4, nz)),
        sa=sem((2,)), sh=sem((2,)), sb=sem((2,)), so=sem((2,)),
        ss=sem((nc, 2 * nz + 5 + nb)), rs=sem((nc, 2 * nz + 5 + nb)), ls=sem((nc,)), ms=sem((nb + nz,)), mr=sem((nb,)), zm=sem((nz,)),
    )
    for c, (k, h0, half, order) in enumerate(m.reduce_plan):
        C = lanes[k]
        scratch[f"kp{c}"] = V((nz, half, C), bf16)
        for b in m.bits[1:3]:
            lead = nz if order.index(b) < order.index("z") else 1
            scratch[f"rv{c}_{b}"] = V((lead, op_rows(half, order, b), C), bf16)
        scratch[f"ln{c}"] = V((2, nz - 1, op_rows(half, order, "z"), C), bf16)
        if nb > 3:
            scratch[f"ex{c}"] = V((nb - 3, half // 4, C), bf16)
    S = jax.ShapeDtypeStruct
    hbm, vm, sm = (pl.BlockSpec(memory_space=s) for s in (pl.ANY, pltpu.VMEM, pltpu.SMEM))
    outs = dict(
        layer_out=(S((ni, L, D), f32), vm), text_grad=(S((ni, L, D), f32), vm), patch_grad=(S((ni, m.NP, PW), f32), vm), small=(S((sums, D), f32), vm),
        **{"R" + k: (S(s.shape, bf16), hbm) for k, s in zip("ABOHW", shards)},
        **{"G" + k: (S((nz,) + s.shape, bf16), hbm) for k, s in zip("ABOHW", shards)},
    )
    ins = dict(x=(x, vm), patches=(patches, vm), rows=(rows, sm), cot=(cot, vm), A=(A, hbm), B=(B, hbm), O=(O, hbm), H=(H, hbm), W=(W, hbm),
               vown=(vown, vm), ob=(ob, vm), gain=(gain, vm), shift=(shift, vm))
    m.inputs, m.outputs, m.scratch = list(ins), list(outs), list(scratch)
    res = pl.pallas_call(
        functools.partial(layer_kernel, m),
        out_shape=tuple(o[0] for o in outs.values()),
        in_specs=[i[1] for i in ins.values()],
        out_specs=tuple(o[1] for o in outs.values()),
        scratch_shapes=list(scratch.values()),
        compiler_params=pltpu.CompilerParams(collective_id=0, has_side_effects=True, vmem_limit_bytes=67043328),
        name="layer",
    )(*[i[0] for i in ins.values()])
    return dict(zip(outs, res))


def per_device(nd, nz, text_states, patch_states, patch_rows, cotangent, w_attn, attn_bias, w_attn_out, w_query, w_patch, cross_bias, w_cross_out, w_hidden, hidden_bias, w_output, out_bias, norm_gain, norm_shift):
    m = Dims()
    m.nz, m.bits = nz, tuple(range(nd.bit_length() - 1))
    z = lax.axis_index("mp")
    hw = w_query.shape[1]
    D = text_states.shape[-1]
    A = jnp.concatenate([w_query, w_attn[0], w_attn[2], w_attn[1]], 1)
    B = jnp.concatenate([w_patch[0], w_patch[1]], 1)
    O = jnp.concatenate([w_attn_out, w_cross_out], 0)
    zero = jnp.zeros((hw,), bf16)
    vown = jnp.stack([
        jnp.concatenate([cross_bias[0], attn_bias[0], attn_bias[1], zero]),
        jnp.pad(jnp.concatenate([zero, cross_bias[1]]), (0, D - 2 * hw)), hidden_bias])
    vown = jnp.pad(vown, ((0, 13), (0, 0)))
    r = run_layer(m, nd, (A, B, O, w_hidden, w_output), vown, text_states, patch_states, patch_rows, cotangent, out_bias.astype(f32), norm_gain.astype(f32), norm_shift.astype(f32))
    RA, RB, RO, RH, RW = (r["R" + k].astype(f32) for k in "ABOHW")
    small = r["small"]
    pick = lambda base: lax.dynamic_slice_in_dim(small, base + z, 1, 0)[0]
    cq, kv, qv = pick(9 + nz), pick(9 + 2 * nz), pick(9 + 3 * nz)
    at = hw - LANES
    part = lambda a, i: a[:, i * hw:(i + 1) * hw]
    return (
        r["layer_out"], r["text_grad"], r["patch_grad"],
        jnp.stack([part(RA, 1), part(RA, 3), part(RA, 2)]),
        jnp.stack([qv[at:at + hw], qv[at + hw:at + 2 * hw]]),
        RO[:hw], part(RA, 0), jnp.stack([part(RB, 0), part(RB, 1)]),
        jnp.stack([cq[:hw], kv[hw:2 * hw]]), RO[hw:], RH, pick(9), RW,
        small[0:3], small[3:6], small[6:9],
    )


def solution(mesh):
    nd, nz = mesh.shape["dp"], mesh.shape["mp"]
    rows = P(("dp", "mp"), None, None)
    return jax.shard_map(
        functools.partial(per_device, nd, nz),
        mesh=mesh,
        in_specs=(rows, rows, P("dp"), rows, P(None, None, "mp"), P(None, "mp"), P("mp", None), P(None, "mp"), P(None, None, "mp"), P(None, "mp"), P("mp", None), P(None, "mp"), P("mp"), P("mp", None), P(), P(), P()),
        out_specs=(rows, rows, rows, P(None, None, "mp"), P(None, "mp"), P("mp", None), P(None, "mp"), P(None, None, "mp"), P(None, "mp"), P("mp", None), P(None, "mp"), P("mp"), P("mp", None), P(), P(), P()),
        check_vma=False,
    )
```

time: 293 us -> 239 us (0.82)
  Pallas kernels: 258 us -> 204 us
    pallas_call x1, Pallas kernels: 258 us -> 204 us  [run_layer(): pl.pallas_call(functools.partial(layer_kernel, m), out_shape=tuple((o[0]...]
where the time goes in v3:
time: 239 us; the launch traced here: 238 us
  Pallas kernels  204 us (85%)
  local copies, waits for them, and re-layouts  21.3 us (9%)
  other arithmetic  12.2 us (5%)
    pallas_call x1, Pallas kernels, run_layer(): pl.pallas_call(functools.partial(layer_kernel, m), out_shape=tuple((o[0]...  204 us
    unnamed x43, local copies, waits for them, and re-layouts  11.7 us

profile of v3, /device:TPU:0, one launch (start us, length us, event | category | flops | bytes accessed | tf_op | source)
XLA Modules:
  0.0 238.3 jit_solution(8762909790393160240)
XLA Ops:
  0.6 0.0 copy-start.9
  0.7 0.8 slice_reduce_fusion.2
  1.5 0.1 pad_maximum_fusion.5
  1.6 0.1 pad.35
  1.6 0.7 stack.45
  2.3 0.6 fusion.4.refs_9_
  2.9 1.2 fusion.5
  4.1 0.2 copy.44
  4.3 0.2 copy.45
  4.5 0.0 copy-start.5
  4.5 0.2 copy.46
  4.7 0.0 copy-done.9
  4.7 0.2 copy.36
  4.9 1.5 pad_maximum_fusion.2.refs_4_
  6.4 0.0 copy-done.5
  6.4 0.1 fusion.6
  6.4 0.0 copy-start.2
  6.4 0.2 copy.47
  6.6 0.2 copy.48
  6.9 0.0 copy-start.10
  6.9 0.0 copy-start.11
  6.9 1.2 pad_maximum_fusion.3.refs_5_
  8.1 0.0 copy-done.2
  8.1 1.4 copy.39.refs_1_
  9.5 0.0 copy-done.10
  9.5 0.0 copy-done.11
  9.5 0.9 pad_maximum_fusion.4.refs_6_
  10.3 0.0 copy-done.12
  10.3 0.6 convert_element_type.28.refs_10_
  10.9 0.0 copy-done.13
  10.9 0.6 convert_element_type.29.refs_11_
  11.6 0.0 copy-done.14
  11.6 0.6 convert_element_type.30.refs_12_
  12.2 203.9 %layer.1 = (f32[4,40,768]{2,1,0:T(8,128)}, f32[4,40,768]{2,1,0:T(8,128)}, f32[4,145,1024]{2,1,0:T(8,128)}, f32[32,768]{1,0:T(8,128)}, bf16[768,768]{1,0:T(8,128)...) custom-call(bf16[4,40,768]{2,1,0:T(8,128)(2,1)} %refs_0_.1, ...), custom_call_target="tpu_custom_call" | custom-call | tf_op jit(solution)/shard_map/layer/pallas_call | solution.py:918
  216.1 0.9 constant_dynamic-slice_fusion
  217.0 0.6 pad_maximum_fusion.7
  217.6 0.6 pad_maximum_fusion.6
  218.2 1.4 convert_element_type.31
  219.6 0.5 slice_bitcast_fusion.4
  220.1 0.2 pad_maximum_fusion
  220.3 0.0 copy-start.6
  220.3 1.8 copy.41
  222.1 0.0 copy-done.6
  222.1 0.1 convert_element_type.33
  222.2 0.3 slice_bitcast_fusion.1
  222.5 0.1 pad_maximum_fusion.1
  222.7 0.0 copy-start
  222.7 1.7 copy.43
  224.4 1.3 dynamic-slice_reduce_fusion
  225.7 1.5 fusion.8
  227.2 0.0 copy-done
  227.2 0.1 slice.104
  227.3 0.0 copy-start.1
  227.3 1.1 copy.42
  228.4 2.1 fusion.7
  230.5 0.0 copy-done.1
  230.5 2.9 %copy.40 = f32[4,145,1024]{2,0,1:T(4,128)} copy(f32[4,145,1024]{2,1,0:T(8,128)S(1)} %copy-done.1) | data formatting | bytes 4751360
  233.4 0.0 copy-done.4
  233.5 1.6 convert_element_type.34
  235.0 0.1 copy-done.3
  235.1 1.6 convert_element_type.35
  236.7 0.0 copy-done.8
  236.7 0.8 copy.51
  237.5 0.8 copy.52
  (11 shorter events, 0.0 us)
Async XLA Ops:
  0.6 4.0 %copy-start.9 = (bf16[768,192]{0,1:T(8,128)(2,1)S(1)}, bf16[768,192]{0,1:T(8,128)(2,1)}, u32[]{:S(2)}) copy-start(bf16[768,192]{0,1:T(8,128)(2,1)} %param.24) | copy-start | bytes 884740
  4.5 1.9 copy-start.5
  6.4 1.6 copy-start.2
  6.9 2.6 %copy-start.10 = (bf16[192,768]{1,0:T(8,128)(2,1)S(1)}, bf16[192,768]{1,0:T(8,128)(2,1)}, u32[]{:S(2)}) copy-start(bf16[192,768]{1,0:T(8,128)(2,1)} %param.27) | copy-start | bytes 884740
  6.9 2.6 %copy-start.11 = (bf16[192,768]{1,0:T(8,128)(2,1)S(1)}, bf16[192,768]{1,0:T(8,128)(2,1)}, u32[]{:S(2)}) copy-start(bf16[192,768]{1,0:T(8,128)(2,1)} %param.23) | copy-start | bytes 884740
  8.1 2.3 copy-start.12
  8.1 2.9 %copy-start.13 = (bf16[3,768]{1,0:T(4,128)(2,1)S(1)}, bf16[3,768]{1,0:T(4,128)(2,1)}, u32[]{:S(2)}) copy-start(bf16[3,768]{1,0:T(4,128)(2,1)} %param.32) | copy-start | bytes 13828
  8.1 3.5 %copy-start.14 = (bf16[3,768]{1,0:T(4,128)(2,1)S(1)}, bf16[3,768]{1,0:T(4,128)(2,1)}, u32[]{:S(2)}) copy-start(bf16[3,768]{1,0:T(4,128)(2,1)} %param.33) | copy-start | bytes 13828
  220.3 1.8 copy-start.6
  222.7 4.5 %copy-start = (bf16[768,768]{1,0:T(8,128)(2,1)S(1)}, bf16[768,768]{1,0:T(8,128)(2,1)}, u32[]{:S(2)}) copy-start(bf16[768,768]{1,0:T(8,128)(2,1)} %get-tuple-element.28) | copy-start | bytes 3538948
  227.3 3.2 %copy-start.1 = (f32[4,145,1024]{2,1,0:T(8,128)S(1)}, f32[4,145,1024]{2,1,0:T(8,128)}, u32[]{:S(2)}) copy-start(f32[4,145,1024]{2,1,0:T(8,128)} %get-tuple-element.36) | copy-start | bytes 7127044
  230.5 2.9 %copy-start.4 = (bf16[768,768]{1,0:T(8,128)(2,1)S(1)}, bf16[768,768]{1,0:T(8,128)(2,1)}, u32[]{:S(2)}) copy-start(bf16[768,768]{1,0:T(8,128)(2,1)} %get-tuple-element.32) | copy-start | bytes 3538948
  233.4 1.7 copy-start.3
  235.0 1.7 copy-start.8
  235.1 2.4 copy-start.7

commit v4 on v3

--- a/solution.py
+++ b/solution.py
@@ -12,7 +12,6 @@
 HEAD = 64
 LANES = 128
 epsilon = 1e-06
-DEV = set()
 score_scale = 1.0 / math.sqrt(HEAD)
 bf16, f32 = jnp.bfloat16, jnp.float32
 
@@ -292,6 +291,13 @@
     return jnp.sum(v, axis=0, keepdims=True)
 
 
+def nth_shard(z, nz, o):
+    t = z
+    for b in range(nz.bit_length() - 1):
+        t = t + lax.rem(lax.div(o, jnp.int32(2 ** b)), jnp.int32(2)) * (1 - 2 * bit_of(z, b)) * (2 ** b)
+    return t
+
+
 class Dims:
     pass
 
@@ -307,14 +313,11 @@
     core = bit_of(d, m.bits[0])
     partner = flip(d, m.bits[0])
 
-    def shard(o):
-        t = z
-        for b in range(nz.bit_length() - 1):
-            t = t + lax.rem(lax.div(o, jnp.int32(2 ** b)), jnp.int32(2)) * (1 - 2 * bit_of(z, b)) * (2 ** b)
-        return t
+    shard = functools.partial(nth_shard, z, nz)
 
     g.DCQ = g.HD.at[:, :, 0:hp]
     g.DQ = g.DP.at[:, :, 0:m.QW]
+    g.KV = g.DKV.at[:, 0:ni * KP]
 
     pos = Dims()
     pos.d, pos.z = d, z
@@ -323,10 +326,26 @@
     kind = z * (1 - pos.upper) + (nz - 1 - z) * pos.upper
     classes = range(nz // 2)
 
-    g.VG[z] = g.vown[...]
+    hw = m.hw
+    joins = [(g.wq, g.AO.at[pl.ds(0, hw)]), (g.wa.at[0], g.AO.at[pl.ds(hw, hw)]), (g.wa.at[2], g.AO.at[pl.ds(2 * hw, hw)]), (g.wa.at[1], g.AO.at[pl.ds(3 * hw, hw)]),
+             (g.wp.at[0], g.BO.at[pl.ds(0, hw)]), (g.wp.at[1], g.BO.at[pl.ds(hw, hw)]), (g.wao, g.OO.at[pl.ds(0, hw)]), (g.wco, g.OO.at[pl.ds(hw, hw)])]
+    joins = [pltpu.make_async_copy(a, b, g.js.at[i]) for i, (a, b) in enumerate(joins)]
+    for cp in joins:
+        cp.start()
+    g.TMP[0:16, 0:D] = jnp.zeros((16, D), f32)
+    ab, cb = g.ab[...].astype(f32), g.cb[...].astype(f32)
+    g.TMP[0:1, 0:hw] = cb[0:1]
+    g.TMP[0:1, hw:2 * hw] = ab[0:1]
+    g.TMP[0:1, 2 * hw:3 * hw] = ab[1:2]
+    g.TMP[1:2, hw:2 * hw] = cb[1:2]
+    g.TMP[2:3, 0:D] = g.hb[...].astype(f32).reshape(1, D)
+    g.VO[...] = g.TMP[0:16, 0:D].astype(bf16)
+    g.VG[z] = g.VO[...]
     enter(d, z, nz, m.bits)
+    for cp in joins:
+        cp.wait()
     gsem = (g.zs, g.zr, g.ps, g.pr)
-    own = {"A": g.A, "B": g.B, "O": g.O, "H": g.H, "W": g.W, "V": g.vown}
+    own = {"A": g.AO, "B": g.BO, "O": g.OO, "H": g.H, "W": g.W, "V": g.VO}
     far = {"A": g.GA, "B": g.GB, "O": g.GO, "H": g.GH, "W": g.GW, "V": g.VG}
     gathers = [Gather(own[k], far[k], r0, rows, order, pos, gsem, c) for c, (k, r0, rows, order) in enumerate(m.gather_plan)]
     calls = [0, 0]
@@ -334,8 +353,6 @@
     def gather_steps():
         at = calls[0]
         calls[0] += 1
-        if "nog" in DEV:
-            return
         for cls in classes:
             todo = m.gather_steps[cls][at]
             if todo:
@@ -344,11 +361,40 @@
                     for c, st, dr, j in todo:
                         gathers[c].item(cls, nz, st, dr, j)
 
+    nb = len(m.bits)
+
+    def small_copy(i):
+        return pltpu.make_async_remote_copy(g.SM, g.SR.at[i], g.ms.at[i], g.mr.at[i], device_id=(flip(d, m.bits[i]), z), device_id_type=MESH)
+
+    def small_spread(o, frm):
+        to = lax.rem(z + o, jnp.int32(nz))
+        return pltpu.make_async_remote_copy(g.SM, g.SZ.at[frm(to)], g.ms.at[nb + o], g.zm.at[frm(to)], device_id=(d, to), device_id_type=MESH)
+
+    def small_step(i):
+        if i > 0 and i < 4:
+            small_copy(i - 1).wait()
+            g.SM[...] += g.SR[i - 1]
+        if i < 3:
+            small_copy(i).start()
+        elif i == 3:
+            for e in range(3, nb):
+                small_copy(e).start()
+                small_copy(e).wait()
+                g.SM[...] += g.SR[e]
+            g.SZ[z] = g.SM[...]
+            for o in range(1, nz):
+                small_spread(o, lambda to: z).start()
+        elif i == 5:
+            for o in range(1, nz):
+                small_spread(o, lambda to: to).wait_recv()
+            total = g.SZ[0]
+            for t in range(1, nz):
+                total = total + g.SZ[t]
+            g.small[...] = total
+
     def reduce_steps():
         at = calls[1]
         calls[1] += 1
-        if "nor" in DEV:
-            return
         for cls in classes:
             todo = m.reduce_steps[cls][at]
             if todo:
@@ -357,7 +403,9 @@
                     for c, what in todo:
                         i = progress[cls, c, what]
                         progress[cls, c, what] += 1
-                        if what == 0:
+                        if c == len(chunks):
+                            small_step(i)
+                        elif what == 0:
                             chunks[c].steps[i]()
                         else:
                             chunks[c].along(cls, what, i)
@@ -369,12 +417,11 @@
         return between
 
     def finish_gather():
-        if "nog" not in DEV:
-            for cls in classes:
-                @pl.when(kind == cls)
-                def _():
-                    for q in gathers:
-                        q.finish(cls, nz)
+        for cls in classes:
+            @pl.when(kind == cls)
+            def _():
+                for q in gathers:
+                    q.finish(cls, nz)
 
     pair_slot = [0]
 
@@ -408,33 +455,37 @@
         dst, done = place(block, slot)
         pltpu.make_async_copy(own[key].at[pl.ds(*rows), pl.ds(*cols)], dst, done).wait()
 
-    def stream(blocks, body, between, ahead):
+    def stream(blocks, body, between, ahead, refill=()):
         def step(o, c):
-            slot = lax.rem(o, jnp.int32(2))
-
-            @pl.when(o + 1 < nz)
-            def _():
-                for b in blocks:
-                    fetch(b, 1 - slot, o + 1)
-
-            @pl.when(o + 1 == nz)
-            def _():
-                for b in ahead:
-                    fetch(b, 0, 0)
+            if blocks:
+                @pl.when(o + 1 < nz)
+                def _():
+                    for b in blocks:
+                        fetch(b, slot_of(b, o + 1), o + 1)
+            if ahead:
+                @pl.when(o + 1 == nz)
+                def _():
+                    for b in ahead:
+                        fetch(b, 0, 0)
             for b in blocks:
-                arrived(b, slot)
-            body(o, slot)
+                arrived(b, slot_of(b, o))
+            body(o, lax.rem(o, jnp.int32(2)))
+            for b in refill:
+                fetch(b, o, o)
             between(o)
             return c
         lax.fori_loop(0, nz, step, 0)
 
+    def slot_of(block, o):
+        return lax.rem(o, jnp.int32(block[0].shape[0]))
+
     FZ, PW, BW = m.FZ, m.PW, m.BW
-    self_blocks = [(g.SA, g.sa, "A", (0, D), (LANES, D - LANES)), (g.SO, g.so, "O", (0, hp), (0, D))]
-    cross_blocks = [(g.SA, g.sa, "A", (0, D), (0, hp)), (g.SB, g.sb, "B", (0, PW), (0, BW)), (g.SO, g.so, "O", (LANES, hp), (0, D))]
+    self_blocks = [(g.SA, g.sa, "A", (LANES, D - LANES), (0, D)), (g.SO, g.so, "O", (0, hp), (0, D))]
+    cross_blocks = [(g.SA, g.sa, "A", (0, hp), (0, D)), (g.SB, g.sb, "B", (0, BW), (0, PW)), (g.SO, g.so, "O", (LANES, hp), (0, D))]
     hidden_blocks = [(g.SA, g.sa, "H", (0, D), (0, FZ))]
     output_blocks = [(g.SA, g.sa, "W", (0, FZ), (0, D))]
-    back_blocks = output_blocks + [(g.SH, g.sh, "H", (0, D), (0, FZ))]
-    self_back = [(g.SA, g.sa, "A", (0, D), (LANES, D - LANES)), (g.SO, g.so, "O", (0, hp), (0, D))]
+    back_blocks = [(g.SH, g.sh, "H", (0, D), (0, FZ))]
+    cross_back = [cross_blocks[0], cross_blocks[2]]
     for b in self_blocks:
         fetch(b, 0, 0)
 
@@ -457,8 +508,8 @@
 
     for i in range(ni):
         g.XF[i * L:(i + 1) * L] = g.x[i].astype(f32)
-        g.PT[i * KP:i * KP + NP] = g.patches[i]
-        g.PT[i * KP + NP // 16 * 16:(i + 1) * KP] = jnp.concatenate([g.patches[i, NP // 16 * 16:NP].astype(f32), jnp.zeros((KP - NP, m.PW), f32)], 0).astype(bf16)
+        mine = jnp.concatenate([g.patches[:, i, :].astype(f32), jnp.zeros((KP - NP, m.PW), f32)], 0)
+        g.PT[i * KP:(i + 1) * KP] = mine.astype(bf16)
     g.X[0:T] = g.XF[...].astype(bf16)
     swaps = [pair(g.X, T), pair(g.PT, ni * KP)]
     for s in swaps:
@@ -470,7 +521,7 @@
     def self_forward(o, slot):
         t = shard(o)
         bias = g.VG[t].astype(f32)[0:1, LANES:]
-        qkv = (dot(g.X[0:T], g.SA[slot, :, LANES:]) + bias).astype(bf16)
+        qkv = (dot_nt(g.X[0:T], g.SA[o, 0:m.QW]) + bias).astype(bf16)
         g.QKV[o] = qkv
         qf = qkv.astype(f32)
         outs = []
@@ -484,12 +535,12 @@
             outs.append(unstack(dot(p.astype(bf16), v_i), low))
         mixed = jnp.concatenate(outs, 0).astype(bf16)
         g.MX[0, o, 0:T] = mixed
-        g.ACC[...] += dot(mixed, g.SO[slot])
+        g.ACC[...] += dot(mixed, g.SO[o])
 
     stream(self_blocks, self_forward, after_each(gather_steps), cross_blocks)
 
     def out_row(j):
-        return g.ob[j:j + 1, :], g.gain[j:j + 1, :], g.shift[j:j + 1, :]
+        return tuple(v[...].astype(f32)[j:j + 1, :] for v in (g.ob, g.gain, g.shift))
 
     ob, gn, sh = out_row(0)
     first, normed, inv = norm_forward(g.XF[...] + g.ACC[...] + ob, gn, sh)
@@ -504,10 +555,10 @@
     def cross_forward(o, slot):
         t = shard(o)
         vb = g.VG[t].astype(f32)
-        cq = (dot(g.F[0:T], g.SA[slot, :, 0:hp]) + vb[0:1, 0:hp]).astype(bf16)
+        cq = (dot_nt(g.F[0:T], g.SA[o, 0:hp]) + vb[0:1, 0:hp]).astype(bf16)
         g.CQ[o] = cq
         cqf = cq.astype(f32)
-        kv = (dot(g.PT[0:ni * KP], g.SB[slot]) + vb[1:2, 0:m.BW]).astype(bf16)
+        kv = (dot_nt(g.PT[0:ni * KP], g.SB[slot]) + vb[1:2, 0:m.BW]).astype(bf16)
         g.KV[o] = kv
         outs = []
         for i in range(ni):
@@ -520,7 +571,7 @@
             outs.append(unstack(dot(p.astype(bf16), kvi[:, LANES:LANES + hp]), high))
         mixed = jnp.concatenate(outs, 0).astype(bf16)
         g.MX[1, o, 0:T] = mixed
-        g.ACC[...] += dot(mixed, g.SO[slot])
+        g.ACC[...] += dot(mixed, g.SO[o])
 
     stream(cross_blocks, cross_forward, after_each(gather_steps), hidden_blocks)
     ob, gn, sh = out_row(1)
@@ -538,7 +589,7 @@
 
     def hidden_forward(o, slot):
         t = shard(o)
-        pre = dot(g.S2[0:T], g.SA[slot]) + g.VG[t].astype(f32)[2:3, :]
+        pre = dot(g.S2[0:T], g.SA[o]) + g.VG[t].astype(f32)[2:3, :]
         cdf = 0.5 * (1.0 + lax.erf(pre * math.sqrt(0.5)))
         g.GP[o] = cdf + pre * jnp.exp(-0.5 * pre * pre) * (1.0 / math.sqrt(2.0 * math.pi))
         g.HD[o, 0:T] = (pre * cdf).astype(bf16)
@@ -551,19 +602,16 @@
     gather_steps()
 
     def output_forward(o, slot):
-        g.ACC[...] += dot(g.HD[o, 0:T], g.SA[slot])
+        g.ACC[...] += dot(g.HD[o, 0:T], g.SA[o])
 
     stream(output_blocks, output_forward, after_each(gather_steps), back_blocks)
     gather_steps()
     ob, gn, sh = out_row(2)
     final, normed, inv = norm_forward(g.S2[0:T].astype(f32) + g.ACC[...] + ob, gn, sh)
-    g.layer_out[...] = final.reshape(ni, L, D)
-
-    if "fwd" in DEV:
-        for cp in swaps + hid_swaps + [mix_swap]:
-            cp.wait()
-        finish_gather()
-        return
+    g.FO[...] = final.reshape(ni, L, D)
+    layer_store = pltpu.make_async_copy(g.FO, g.layer_out, g.js.at[8])
+    layer_store.start()
+
     for i in range(ni):
         g.ACC[i * L:(i + 1) * L] = g.cot[i].astype(f32)
     cot = g.ACC[...]
@@ -588,12 +636,13 @@
         recvs = {b: R[f"rv{c}_{b}"] for b in m.bits[1:3]}
         whole = m.rows[k] // 2
         chunks.append(Reduce(R[f"kp{c}"], recvs, R[f"ln{c}"], R.get(f"ex{c}"), results[k], core * whole + h0, half, order, pos, nz, m.bits, rsem, c))
-        for cls in classes:
+    for cls in classes:
+        for c in range(len(chunks) + 1):
             for what in range(3):
                 progress[cls, c, what] = 0
 
-    def half_columns(whole):
-        return pl.ds(pl.multiple_of(core * whole, LANES), whole)
+    def half_columns(apart, count=None):
+        return pl.ds(pl.multiple_of(core * apart, LANES), count or apart)
 
     def deal(k, t, value):
         for c, p in enumerate(m.reduce_plan):
@@ -611,8 +660,7 @@
         t = shard(o)
         deal("W", t, dot_tn(g.HD[o, :, half_columns(m.FZ // 2)], g.G3[...]))
         return c
-    if "skip_job_w" not in DEV:
-        lax.fori_loop(0, nz, job_w, 0)
+    lax.fori_loop(0, nz, job_w, 0)
     for s in hid_swaps:
         s.wait_send()
     reduce_steps()
@@ -623,13 +671,13 @@
 
     def hidden_backward(o, slot):
         t = shard(o)
-        pre = (dot_nt(g.G3[0:T], g.SA[slot]) * g.GP[o]).astype(bf16)
+        pre = (dot_nt(g.G3[0:T], g.SA[o]) * g.GP[o]).astype(bf16)
         g.DP[o, 0:T] = pre
         g.SM[pl.ds(9 + t, 1)] = col_sum(pre.astype(f32))
         loop_send(g.DP, T, 0, o)
         g.ACC[...] += dot_nt(pre, g.SH[slot])
 
-    stream(back_blocks, hidden_backward, after_each(reduce_steps), cross_blocks)
+    stream(back_blocks, hidden_backward, after_each(reduce_steps), [], cross_back)
     reduce_steps()
 
     def loop_wait(ref, rows, kind):
@@ -637,7 +685,7 @@
             cp = pltpu.make_async_remote_copy(ref.at[o, pl.ds(0, rows)], ref.at[o, pl.ds(rows, rows)], g.ds.at[kind, o], g.dr.at[kind, o], device_id=(partner, z), device_id_type=MESH)
             cp.wait()
 
-    gn = g.gain[1:2, :]
+    gn = out_row(1)[1]
     normed, inv = g.NM[1], g.INV[1][:, 0:1]
     grad = g.ACC[...]
     secondg = norm_backward(grad, normed, inv, gn)
@@ -653,12 +701,10 @@
         t = shard(o)
         deal("H", t, dot_tn(g.S2[:, half_columns(D // 2)], g.DP[o]))
         return c
-    if "skip_job_h" not in DEV:
-        lax.fori_loop(0, nz, job_h, 0)
+    lax.fori_loop(0, nz, job_h, 0)
     reduce_steps()
 
     g.ACC[...] = secondg
-    g.patch_grad[...] = jnp.zeros(g.patch_grad.shape, f32)
 
     def backward_unit(qs, k_i, v_i, p, ms, masks):
         grad_v = dot_tn(p.astype(bf16), ms)
@@ -670,7 +716,9 @@
 
     def cross_backward(o, slot):
         t = shard(o)
-        gm = dot_nt(g.G12[1, 0:T], g.SO[slot]).astype(bf16).astype(f32)
+        for b in cross_back:
+            arrived(b, o)
+        gm = dot_nt(g.G12[1, 0:T], g.SO[o]).astype(bf16).astype(f32)
         cqf = g.CQ[o].astype(f32)
         grads = []
         for i in range(ni):
@@ -686,13 +734,12 @@
         dkv = g.DKV[o, 0:ni * KP]
         g.SM[pl.ds(9 + nz + t, 1), 0:hp] = col_sum(dcq.astype(f32))
         g.SM[pl.ds(9 + 2 * nz + t, 1), 0:m.BW] = col_sum(dkv.astype(f32))
-        g.ACC[...] += dot_nt(dcq, g.SA[slot, :, 0:hp])
-        for i in range(ni):
-            g.patch_grad[i] += dot_nt(g.DKV[o, i * KP:(i + 1) * KP], g.SB[slot])[0:NP]
-
-    stream(cross_blocks, cross_backward, after_each(reduce_steps), self_blocks)
-    reduce_steps()
-    gn = g.gain[0:1, :]
+        g.ACC[...] += dot(dcq, g.SA[o, 0:hp])
+        pltpu.make_async_copy(g.DKV.at[o, pl.ds(0, ni * KP)], g.DK.at[o], g.dk.at[o]).start()
+
+    stream([], cross_backward, after_each(reduce_steps), [], self_blocks)
+    reduce_steps()
+    gn = out_row(0)[1]
     normed, inv = g.NM[0], g.INV[0][:, 0:1]
     grad = g.ACC[...]
     firstg = norm_backward(grad, normed, inv, gn)
@@ -707,17 +754,19 @@
 
     def job_b(o, c):
         t = shard(o)
-        deal("B", t, dot_tn(g.PT[:, half_columns(m.PW // 2)], g.DKV[o]))
+        g.TMP[...] = dot_tn(g.DKV[o, :, half_columns(LANES, hp)], g.PT[...])
+        deal("B", t, g.TMP[pl.ds(pl.multiple_of(core * HEAD, 16), BW // 2)])
         return c
-    if "skip_job_b" not in DEV:
-        lax.fori_loop(0, nz, job_b, 0)
+    lax.fori_loop(0, nz, job_b, 0)
     reduce_steps()
 
     g.ACC[...] = firstg
 
     def self_backward(o, slot):
         t = shard(o)
-        gm = dot_nt(g.G12[0, 0:T], g.SO[slot]).astype(bf16).astype(f32)
+        for b in self_blocks:
+            arrived(b, o)
+        gm = dot_nt(g.G12[0, 0:T], g.SO[o]).astype(bf16).astype(f32)
         qf = g.QKV[o].astype(f32)
         gqs, gks, gvs = [], [], []
         for i in range(ni):
@@ -733,10 +782,13 @@
         g.DQ[o, 0:T] = dq
         loop_send(g.DQ, T, 3, o)
         g.SM[pl.ds(9 + 3 * nz + t, 1), 0:m.QW] = col_sum(dq.astype(f32))
-        g.ACC[...] += dot_nt(dq, g.SA[slot, :, LANES:])
-
-    stream(self_blocks, self_backward, after_each(reduce_steps), [])
-    g.text_grad[...] = g.ACC[...].reshape(ni, L, D)
+        g.ACC[...] += dot(dq, g.SA[o, 0:m.QW])
+
+    stream([], self_backward, after_each(reduce_steps), [])
+    layer_store.wait()
+    g.FO[...] = g.ACC[...].reshape(ni, L, D)
+    text_store = pltpu.make_async_copy(g.FO, g.text_grad, g.js.at[8])
+    text_store.start()
     reduce_steps()
     loop_wait(g.DQ, T, 3)
     swap1.wait_recv()
@@ -746,83 +798,69 @@
 
     def job_o(o, c):
         t = shard(o)
-        g.TMP[...] = dot_tn(g.MX[core, o], g.G12[core])
-        deal("O", t, g.TMP[pl.ds(pl.multiple_of(core * HEAD, 16), m.rows["O"] // 2)])
+        g.TMP[:, 0:D] = dot_tn(g.MX[core, o], g.G12[core])
+        deal("O", t, g.TMP[pl.ds(pl.multiple_of(core * HEAD, 16), hw), 0:D])
         return c
-    if "skip_job_o" not in DEV:
-        lax.fori_loop(0, nz, job_o, 0)
+    lax.fori_loop(0, nz, job_o, 0)
     reduce_steps()
 
     def job_a(o, c):
         t = shard(o)
-        cols = half_columns(D // 2)
-        left = dot_tn(g.F[:, cols], g.DCQ[o])
-        right = dot_tn(g.X[:, cols], g.DQ[o])
-        deal("A", t, jnp.concatenate([left[:, 0:LANES], left[:, LANES:] + right[:, 0:LANES], right[:, LANES:]], 1))
+
+        @pl.when(core == 0)
+        def _():
+            left = dot_tn(g.DCQ[o], g.F[...])
+            right = dot_tn(g.DQ[o, :, 0:hp], g.X[...])
+            deal("A", t, jnp.concatenate([left[0:LANES], left[LANES:] + right[0:LANES], right[LANES:]], 0))
+
+        @pl.when(core == 1)
+        def _():
+            deal("A", t, dot_tn(g.DQ[o, :, hp:], g.X[...]))
         return c
-    if "skip_job_a" not in DEV:
-        lax.fori_loop(0, nz, job_a, 0)
-    reduce_steps()
-
-    sends = []
-    for i, b in enumerate(m.bits):
-        cp = pltpu.make_async_remote_copy(g.SM, g.SR.at[i], g.ms.at[i], g.mr.at[i], device_id=(flip(d, b), z), device_id_type=MESH)
-        cp.start()
-        if i < 3:
-            reduce_steps()
-        cp.wait()
-        g.SM[...] += g.SR[i]
-    g.SZ[z] = g.SM[...]
-    nb = len(m.bits)
-    for o in range(1, nz):
-        to = lax.rem(z + o, jnp.int32(nz))
-        cp = pltpu.make_async_remote_copy(g.SM, g.SZ.at[z], g.ms.at[nb + o], g.zm.at[z], device_id=(d, to), device_id_type=MESH)
-        cp.start()
-        sends.append(cp)
-    reduce_steps()
-    reduce_steps()
-    for o in range(1, nz):
-        frm = lax.rem(z + o, jnp.int32(nz))
-        pltpu.make_async_remote_copy(g.SM, g.SZ.at[frm], g.ms.at[nb + o], g.zm.at[frm], device_id=(d, frm), device_id_type=MESH).wait_recv()
-    total = g.SZ[0]
-    for t in range(1, nz):
-        total = total + g.SZ[t]
-    g.small[...] = total
+    lax.fori_loop(0, nz, job_a, 0)
+    reduce_steps()
+
+    reduce_steps()
     assert calls == [len(m.gather_steps[0]), len(m.reduce_steps[0])], calls
-
+    assert all(sum(len(p) for p in m.reduce_steps[cls]) == sum(progress[cls, c, w] for c in range(len(chunks) + 1) for w in range(3)) for cls in classes)
+
+    sends = [small_spread(o, lambda to: z) for o in range(1, nz)]
     for cp in sends + swaps + [swap1, swap2, swap3, mix_swap]:
         cp.wait_send()
+    for o in range(nz):
+        pltpu.make_async_copy(g.DKV.at[o, pl.ds(0, ni * KP)], g.DK.at[o], g.dk.at[o]).wait()
+    text_store.wait()
     finish_gather()
-    if "nor" not in DEV:
-        for cls in classes:
-            @pl.when(kind == cls)
-            def _():
-                for c in chunks:
-                    c.finish(cls)
-
-
-GATHER_PLAN = (("V", 0, 16, ""), ("O", 0, 384, "xyc"), ("W", 0, 256, "xc"), ("A", 384, 384, "yxc"), ("B", 0, 256, "xc"), ("A", 0, 384, "xyc"), ("B", 640, 384,
-    "xc"), ("H", 0, 768, "xyc"), ("B", 256, 384, "yc"), ("W", 256, 256, "xyc"), ("W", 512, 256, "xc"))
-GATHER_ORDER = ((0, 40, 120, 200, 13, 53, 133, 213, 61, 14, 141, 54, 160, 221, 134, 69, 214, 15, 149, 77, 55, 320, 280, 62, 229, 240, 157, 173, 222, 142, 135, 237,
-    63, 215, 181, 174, 70, 189, 78, 150, 293, 230, 223, 333, 158, 143, 182, 238, 175, 190, 253, 71, 301, 334, 79, 360, 231, 400, 151, 294, 183, 341, 239,
-    254, 159, -1, 261, 349, 335, 191, -1, 302, 295, 269, 80, -1, 309, 262, 255, 342, 373, -1, 343, 413, 317, 303, 270, 374, 350, 351, 263, 381, 414, 271,
-    -1, 310, 375, 421, 382, 93, -1, 318, 422, 415, -1, 383, 101, 94, 429, 430, 311, -1, 389, 109, 95, 423, 319, -1, 102, 397, -1, 390, 431, -1, 391, 110,
-    103, -1, 398, 399, 111, -1, -1, -1, -1), (0, 4, 40, 44, 120, 124, 200, 204, 9, 13, 49, 53, 129, 133, 209, 213, 57, 14, 61, 137, 54, 160, 164, 217,
-    141, 134, 221, 169, 214, 173, 65, 320, 280, 284, 324, 145, 174, 73, 240, 244, 69, 62, 153, 329, 333, 77, 225, 149, 177, 289, 293, 142, 233, 222, 157,
-    249, 253, 185, 181, 334, 229, 182, 189, 237, 190, 294, 297, 70, 254, 337, 78, 345, 301, 341, 360, 364, 400, 404, 349, 369, 230, 150, 373, 257, 342,
-    238, 409, 413, 158, -1, 265, 261, 350, 374, 80, 84, -1, 302, 269, 414, -1, 305, 262, 377, 381, 89, 93, -1, 417, 313, 270, -1, 309, 382, 94, 425, 421,
-    -1, 317, 422, -1, 310, 97, 429, 430, -1, 318, 385, 101, 102, -1, 389, 105, -1, 393, 109, 110, -1, 397, 390, -1, 398, -1, -1, -1, -1))
-REDUCE_PLAN = (("W", 128, "xzy"), ("W", 128, "yxz"), ("W", 128, "zyx"), ("H", 192, "xyz"), ("H", 64, "yxz"), ("H", 128, "yxz"), ("B", 320, "zxy"), ("B", 192,
-    "yxz"), ("O", 64, "xyz"), ("O", 64, "yzx"), ("O", 64, "xzy"), ("A", 128, "yxz"), ("A", 128, "yxz"), ("A", 128, "xzy"))
-REDUCE_ORDER = ((-1, -1, 3, 6, 7, 0, -1, -1, -1, -1, -1, -1, 9, 12, 15, -1, -1, 3, 0, 1, -1, 12, -1, -1, -1, 18, 19, 21, -1, 9, 8, 6, 15, -1, -1, 3, 4, 2, 0, -1, 21,
-    12, 13, -1, 30, 27, 24, -1, 39, 33, 36, 15, 16, -1, 21, 22, 9, 10, 6, -1, 0, -1, 30, 31, -1, 27, 28, 20, 18, 24, -1, 5, 3, 14, 12, 33, 17, 15, 39, 40,
-    23, 21, 6, 18, 3, 12, 11, 9, 36, 0, 32, 30, 33, 34, 24, 25, 29, 27, 15, 18, 21, 6, 3, 12, 3, 12, 9, 30, 36, 37, 41, 39, 15, 0, 27, 18, 35, 33, 15, 0,
-    21, 26, 24, 9, 21, 27, 6, 30, 9, 39, 6, 38, 18, 36, 24, 33, 27, 18, 30, 39, 27, 36, 30, 24, 33, 24, 39, 33, 36, 39, 36), (-1, -1, 3, 6, 0, -1, -1, -1,
-    -1, -1, -1, 9, 12, 7, 15, -1, 3, 7, 0, -1, -1, 12, 7, 8, -1, 8, 6, 1, 1, -1, -1, 18, 21, 9, 1, 2, 15, -1, 6, 2, 0, -1, 3, 19, -1, 12, -1, 21, -1, 19,
-    30, 27, 6, 24, 15, -1, 39, 20, 21, 9, 33, 0, 36, -1, 19, 4, -1, 20, 18, 30, 13, 13, 27, 13, 4, 4, 5, 6, 16, -1, 14, 14, 12, 24, 5, 3, 22, 16, 16, -1,
-    22, 22, 17, 23, -1, 10, 10, 23, 21, 33, 0, 17, 15, 10, 31, 39, 11, 31, 31, 11, 9, 18, 28, 32, 12, 28, 32, 30, 3, 28, 21, 36, 29, 29, 40, 27, 6, 6, 40,
-    33, 24, 9, 41, 40, 0, 18, 34, 15, 41, 39, 12, 34, 0, 30, 34, 12, 25, 35, 25, 3, 25, 35, 33, 36, 27, 26, 21, 3, 37, 26, 24, 18, 37, 21, 37, 9, 38, 15,
-    33, 38, 39, 27, 9, 36, 30, 15, 24, 18, 33, 36, 39, 18, 30, 33, 27, 24, 30, 27, 24, 36, 39, 36, 39))
+    for cls in classes:
+        @pl.when(kind == cls)
+        def _():
+            for c in chunks:
+                c.finish(cls)
+
+
+GATHER_PLAN = (("V", 0, 16, ""), ("A", 0, 256, "yxc"), ("A", 256, 256, "yxc"), ("A", 512, 256, "xyc"), ("B", 0, 384, "xc"), ("O", 0, 384, "xyc"), ("H", 0, 256,
+    "yxc"), ("H", 256, 256, "yc"), ("H", 512, 256, "xyc"), ("W", 512, 256, "xc"), ("W", 256, 256, "xyc"), ("W", 0, 256, "yc"))
+GATHER_ORDER = ((0, 80, 120, 40, 200, 400, 13, 93, 133, 53, 101, 213, 141, 413, 61, 14, 94, 109, 134, 149, 221, 117, 54, 102, 421, 157, 214, 414, 69, 160, 15, 142,
+    95, 77, 229, 135, 320, 62, 110, 55, 237, -1, 118, 222, 215, 429, 422, 415, 143, 150, 240, 280, 103, 437, 158, 70, 63, 173, 223, 78, 333, 423, 230,
+    111, 238, -1, 119, 71, 430, 151, 334, 174, 253, 79, 438, 159, 231, 293, 181, 360, 341, 440, 239, -1, 431, 342, 189, 175, 261, -1, 439, 335, 182, 254,
+    301, -1, 349, 350, 190, 262, 183, 255, 309, 294, -1, 453, 357, 358, 343, 191, 269, 263, 295, -1, 373, 277, 270, 302, -1, 461, 454, 278, 374, 271, 351,
+    310, -1, 469, 359, 381, 375, 279, 303, -1, 455, 382, 462, 389, 311, -1, 390, -1, 470, 383, -1, 463, -1, 391, 471, -1, -1), (0, 4, 80, 84, 120, 124,
+    40, 44, 200, 204, 400, 404, 9, 13, 89, 93, 129, 133, 49, 53, 97, 209, 213, 101, 137, 409, 413, 141, 57, 14, 61, 94, 105, 134, 145, 54, 217, 113, 153,
+    214, 149, 221, 414, 102, 160, 164, 157, 109, 62, 417, 117, 320, 421, 324, 225, 65, 233, 169, 173, 73, -1, 142, 69, 229, 425, 329, 333, 222, 240, 244,
+    280, 249, 284, 422, 77, 429, 237, 174, 433, 289, 110, 437, 334, 150, 253, 118, 70, 158, 293, 230, 78, 254, 257, 238, -1, 430, 177, 294, -1, 440, 444,
+    438, 360, 185, 364, 181, 261, 297, -1, 337, 341, 189, 369, 262, 305, 301, -1, 449, 453, 182, 345, 373, 309, 302, 342, 374, 190, 349, -1, 457, 454,
+    353, 357, 265, 269, 310, -1, 465, 461, 377, 273, 277, -1, 469, 462, 350, 385, 270, 381, -1, 470, 358, 382, 278, -1, 389, -1, 390, -1, -1, -1, -1, -1))
+REDUCE_PLAN = (("W", 128, "zyx"), ("W", 128, "yxz"), ("W", 128, "xyz"), ("H", 128, "xyz"), ("H", 128, "zxy"), ("H", 128, "yxz"), ("B", 64, "xyz"), ("B", 128,
+    "yzx"), ("O", 64, "xyz"), ("O", 64, "zyx"), ("O", 64, "zxy"), ("A", 128, "yxz"), ("A", 128, "yxz"), ("A", 128, "xzy"))
+REDUCE_ORDER = ((-1, -1, 0, 1, 6, 3, -1, -1, -1, -1, -1, -1, 15, 9, 12, 13, -1, 6, 3, -1, -1, -1, 2, 0, 15, 9, -1, -1, 0, 18, 6, 7, 3, 4, 21, -1, 0, 15, 16, -1, 9,
+    10, -1, -1, 0, 18, 14, 12, 8, 6, -1, 27, 28, 24, 30, 31, -1, 39, 33, 36, 5, 0, 3, 21, 22, 12, 17, 15, -1, 0, 42, 24, 18, 19, 42, 6, 11, 9, 39, 40, 29,
+    27, 3, 33, 15, 32, 42, 30, 6, 6, 36, 33, 34, 12, 30, 23, 21, 24, 25, 20, 18, 9, 27, 36, 37, 3, 21, 3, 15, 9, 27, 41, 39, 15, 42, 21, 9, 27, 12, 30,
+    35, 33, 18, 39, 26, 24, 12, 33, 21, 12, 38, 36, 27, 18, 30, 21, 27, 39, 42, 18, 24, 36, 42, 30, 33, 30, 39, 33, 36, 24, 39, 36, 24), (-1, -1, 0, 6, 3,
+    -1, -1, -1, -1, -1, 1, -1, 15, 9, 12, -1, 1, 6, 3, 2, -1, 1, -1, 2, 0, 13, -1, 15, 9, -1, 6, 3, 13, -1, 0, 18, 21, 15, 13, 14, -1, 0, 7, 7, 7, 9, 14,
+    12, -1, 8, 4, 4, 4, 8, 6, -1, 0, 18, 5, 16, 16, 16, 5, 3, 10, -1, 17, 21, 3, 10, 17, 6, 15, 10, 12, -1, 0, 11, 11, 9, 27, 28, 28, 24, 30, -1, 39, 0,
+    33, 18, 6, 36, 3, 15, 28, 29, 31, 12, -1, 6, 42, 9, 3, 29, 27, 24, 31, 42, 31, 32, 32, 30, 22, 22, 33, 39, 23, 22, 9, 19, 19, 9, 23, 19, 42, 21, 20,
+    30, 20, 18, 40, 36, 40, 33, 15, 41, 40, 21, 12, 34, 15, 27, 41, 39, 34, 34, 24, 35, 25, 25, 36, 25, 35, 33, 37, 42, 21, 30, 26, 37, 26, 18, 24, 37,
+    39, 12, 38, 27, 38, 33, 36, 12, 21, 18, 30, 27, 24, 21, 36, 39, 18, 42, 30, 42, 33, 24, 30, 27, 33, 24, 39, 27, 36, 39, 36))
 
 
 def unpack(orders, decode):
@@ -860,22 +898,22 @@
     assert all(at[k] * 2 == m.rows[k] for k in at) and m.nz == 4
 
 
-def run_layer(m, nd, shards, vown, x, patches, rows, cot, ob, gain, shift):
+def run_layer(m, x, patches, rows, cot, wa, ab, wao, wq, wp, cb, wco, H, hb, W, ob, gain, shift):
     nz = m.nz
     ni, L, D = x.shape
     T = ni * L
     m.ni, m.L, m.D, m.T = ni, L, D, T
     m.NP, m.PW = patches.shape[1:]
+    by_patch = jnp.swapaxes(patches, 0, 1)
     m.KP = (m.NP + 15) // 16 * 16
-    hw = D // nz
+    hw = m.hw = D // nz
     m.nh = hw // HEAD
     m.hp = (hw + HEAD + LANES - 1) // LANES * LANES
     hp, KP, PW = m.hp, m.KP, m.PW
-    A, B, O, H, W = shards
-    m.BW, m.QW, m.FZ = B.shape[1], D - LANES, W.shape[0]
-    FZ = m.FZ
-    m.rows = {k: s.shape[0] for k, s in zip("ABOHW", shards)}
-    lanes = {k: s.shape[1] for k, s in zip("ABOHW", shards)}
+    m.BW, m.QW, m.FZ = 2 * hw, D - LANES, W.shape[0]
+    FZ, BW = m.FZ, m.BW
+    m.rows = dict(A=D, B=BW, O=2 * hw, H=D, W=FZ)
+    lanes = dict(A=D, B=PW, O=D, H=FZ, W=D)
     plans(m)
     m.swaps = nz + 9
     V, sem = pltpu.VMEM, pltpu.SemaphoreType.DMA
@@ -884,16 +922,16 @@
     sums = (9 + 4 * nz + 7) // 8 * 8
     scratch = dict(
         VG=V((nz, 16, D), bf16), XF=V((T, D), f32), X=V((2 * T, D), bf16), PT=V((2 * ni * KP, PW), bf16),
-        SA=V((2, D, D), bf16), SH=V((2, D, D), bf16), SB=V((2, PW, m.BW), bf16), SO=V((2, hp, D), bf16),
+        SA=V((nz, D, D), bf16), SH=V((2, D, D), bf16), SB=V((2, BW, PW), bf16), SO=V((nz, hp, D), bf16),
         ACC=V((T, D), f32), QKV=V((nz, T, m.QW), bf16), PS=V((nz * ni, m.nh * L, L), f32), MX=V((2, nz, 2 * T, hp), bf16),
         NM=V((2, T, D), f32), INV=V((2, T, LANES), f32), F=V((2 * T, D), bf16), S2=V((2 * T, D), bf16),
-        CQ=V((nz, T, hp), bf16), KV=V((nz, ni * KP, m.BW), bf16), PC=V((nz * ni, m.nh * L, KP), f32),
+        CQ=V((nz, T, hp), bf16), PC=V((nz * ni, m.nh * L, KP), f32),
         GP=V((nz, T, FZ), f32), HD=V((nz, 2 * T, FZ), bf16), SM=V((sums, D), f32), G3=V((2 * T, D), bf16), DP=V((nz, 2 * T, FZ), bf16),
         G12=V((2, 2 * T, D), bf16), DKV=V((nz, 2 * ni * KP, m.BW), bf16),
-        TMP=V((hp, D), f32), SR=V((nb, sums, D), f32), SZ=V((nz, sums, D), f32),
+        TMP=V((hp, PW), f32), FO=V((ni, L, D), f32), AO=V((D, D), bf16), BO=V((BW, PW), bf16), OO=V((2 * hw, D), bf16), VO=V((16, D), bf16), SR=V((nb, sums, D), f32), SZ=V((nz, sums, D), f32),
         zs=sem((ng, 2, nz)), zr=sem((ng, 2, nz)), ps=sem((ng, 3, 2, nz)), pr=sem((ng, 3, 2, nz)),
         cs=sem((m.swaps,)), cr=sem((m.swaps,)), ds=sem((4, nz)), dr=sem((4, nz)),
-        sa=sem((2,)), sh=sem((2,)), sb=sem((2,)), so=sem((2,)),
+        dk=sem((nz,)), js=sem((9,)), sa=sem((nz,)), sh=sem((2,)), sb=sem((2,)), so=sem((nz,)),
         ss=sem((nc, 2 * nz + 5 + nb)), rs=sem((nc, 2 * nz + 5 + nb)), ls=sem((nc,)), ms=sem((nb + nz,)), mr=sem((nb,)), zm=sem((nz,)),
     )
     for c, (k, h0, half, order) in enumerate(m.reduce_plan):
@@ -908,12 +946,13 @@
     S = jax.ShapeDtypeStruct
     hbm, vm, sm = (pl.BlockSpec(memory_space=s) for s in (pl.ANY, pltpu.VMEM, pltpu.SMEM))
     outs = dict(
-        layer_out=(S((ni, L, D), f32), vm), text_grad=(S((ni, L, D), f32), vm), patch_grad=(S((ni, m.NP, PW), f32), vm), small=(S((sums, D), f32), vm),
-        **{"R" + k: (S(s.shape, bf16), hbm) for k, s in zip("ABOHW", shards)},
-        **{"G" + k: (S((nz,) + s.shape, bf16), hbm) for k, s in zip("ABOHW", shards)},
+        layer_out=(S((ni, L, D), f32), hbm), text_grad=(S((ni, L, D), f32), hbm), DK=(S((nz, ni * KP, m.BW), bf16), hbm), small=(S((sums, D), f32), vm),
+        **{"R" + k: (S((m.rows[k], lanes[k]), bf16), hbm) for k in "ABOHW"},
+        **{"G" + k: (S((nz, m.rows[k], lanes[k]), bf16), hbm) for k in "ABOHW"},
     )
-    ins = dict(x=(x, vm), patches=(patches, vm), rows=(rows, sm), cot=(cot, vm), A=(A, hbm), B=(B, hbm), O=(O, hbm), H=(H, hbm), W=(W, hbm),
-               vown=(vown, vm), ob=(ob, vm), gain=(gain, vm), shift=(shift, vm))
+    turn = lambda a: jnp.swapaxes(a, -1, -2)
+    ins = dict(x=(x, vm), patches=(by_patch, vm), rows=(rows, sm), cot=(cot, vm), wa=(turn(wa), hbm), ab=(ab, vm), wao=(wao, hbm), wq=(turn(wq), hbm), wp=(turn(wp), hbm),
+               cb=(cb, vm), wco=(wco, hbm), H=(H, hbm), hb=(hb, vm), W=(W, hbm), ob=(ob, vm), gain=(gain, vm), shift=(shift, vm))
     m.inputs, m.outputs, m.scratch = list(ins), list(outs), list(scratch)
     res = pl.pallas_call(
         functools.partial(layer_kernel, m),
@@ -927,35 +966,133 @@
     return dict(zip(outs, res))
 
 
+finish_ins = ("RA", "RB", "RO", "RH", "RW", "layer_out", "text_grad", "DK", "GB", "wp", "small")
+finish_outs = ("layer_out_", "text_grad_", "patch_grad", "attn", "attn_bias", "attn_out", "query", "patch", "cross_bias", "cross_out", "hidden", "hidden_bias", "output", "out_bias", "gain", "shift")
+
+
+def finish_kernel(m, names, *refs):
+    g = Dims()
+    for k, v in zip(names, refs):
+        setattr(g, k, v)
+    nz, hw, ni, KP, NP = m.nz, m.hw, m.ni, m.KP, m.NP
+    z = lax.axis_index("mp")
+    loads = {}
+
+    def load(name, src, dst):
+        cp = pltpu.make_async_copy(src, dst, g.isem.at[len(loads)])
+        cp.start()
+        loads[name] = cp
+    load("W", g.RW, g.vW)
+    load("H", g.RH, g.vH)
+    load("DK", g.DK, g.vD)
+    for j in range(2):
+        load(f"B0{j}", g.wp.at[j], g.vB.at[0, pl.ds(j * hw, hw)])
+    for o in range(1, nz):
+        load(f"B{o}", g.GB.at[nth_shard(z, nz, jnp.int32(o))], g.vB.at[o])
+    load("lo", g.layer_out, g.vL)
+    load("tg", g.text_grad, g.vT)
+    load("B", g.RB, g.vP)
+    load("O", g.RO, g.vO)
+    load("A", g.RA, g.vA)
+    stores = []
+
+    def store(src, dst):
+        cp = pltpu.make_async_copy(src, dst, g.osem.at[len(stores)])
+        cp.start()
+        stores.append(cp)
+
+    def widen(src, dst, row0=0):
+        step = HEAD
+
+        def body(i, c):
+            r = pl.multiple_of(i * step, step)
+            dst[pl.ds(r, step), :] = src[pl.ds(row0 + r, step), :].astype(f32)
+            return c
+        lax.fori_loop(0, dst.shape[0] // step, body, 0)
+
+    loads["W"].wait()
+    widen(g.vW, g.fW)
+    store(g.fW, g.output)
+    loads["H"].wait()
+    widen(g.vH, g.fH)
+    store(g.fH, g.hidden)
+    loads["DK"].wait()
+    for k in ["B00", "B01"] + [f"B{o}" for o in range(1, nz)]:
+        loads[k].wait()
+    for i in range(ni):
+        total = dot(g.vD[0, i * KP:(i + 1) * KP], g.vB[0])
+        for o in range(1, nz):
+            total = total + dot(g.vD[o, i * KP:(i + 1) * KP], g.vB[o])
+        g.fG[:, i, :] = total[0:NP]
+    store(g.fG, g.patch_grad)
+    loads["lo"].wait()
+    store(g.vL, g.layer_out_)
+    loads["tg"].wait()
+    store(g.vT, g.text_grad_)
+    loads["B"].wait()
+    for j in range(2):
+        widen(g.vP, g.fP.at[j], j * hw)
+    store(g.fP, g.patch)
+    loads["O"].wait()
+    widen(g.vO, g.fO)
+    store(g.fO.at[pl.ds(0, hw)], g.attn_out)
+    store(g.fO.at[pl.ds(hw, hw)], g.cross_out)
+    loads["A"].wait()
+    widen(g.vA, g.fQ)
+    for j, part in ((0, 1), (1, 3), (2, 2)):
+        widen(g.vA, g.fA.at[j], part * hw)
+    store(g.fQ, g.query)
+    store(g.fA, g.attn)
+    row = lambda k: g.small[pl.ds(9 + k * nz + z, 1), :]
+    qv = row(3)[:, 0:5 * LANES]
+    at = hw - LANES
+    g.attn_bias[0:1] = qv[:, at:at + hw]
+    g.attn_bias[1:2] = qv[:, at + hw:at + 2 * hw]
+    g.cross_bias[0:1] = row(1)[:, 0:hw]
+    g.cross_bias[1:2] = row(2)[:, hw:2 * hw]
+    g.hidden_bias[...] = row(0).reshape(m.FZ)
+    g.out_bias[...] = g.small[0:3, :]
+    g.gain[...] = g.small[3:6, :]
+    g.shift[...] = g.small[6:9, :]
+    for cp in stores:
+        cp.wait()
+
+
+def finish(m, r, wp):
+    nz, ni, L, D, PW, FZ, BW, KP, NP = m.nz, m.ni, m.L, m.D, m.PW, m.FZ, m.BW, m.KP, m.NP
+    hw = m.hw = D // nz
+    S, V, sem = jax.ShapeDtypeStruct, pltpu.VMEM, pltpu.SemaphoreType.DMA
+    hbm, vm = pl.BlockSpec(memory_space=pl.ANY), pl.BlockSpec(memory_space=pltpu.VMEM)
+    shapes = ((ni, L, D), (ni, L, D), (NP, ni, PW), (3, hw, D), (2, hw), (hw, D), (hw, D), (2, hw, PW), (2, hw), (hw, D), (D, FZ), (FZ,), (FZ, D), (3, D), (3, D), (3, D))
+    small = {"attn_bias", "cross_bias", "hidden_bias", "out_bias", "gain", "shift"}
+    scratch = dict(
+        vW=V((FZ, D), bf16), vH=V((D, FZ), bf16), vD=V((nz, ni * KP, BW), bf16), vB=V((nz, BW, PW), bf16), vL=V((ni, L, D), f32), vT=V((ni, L, D), f32),
+        vP=V((BW, PW), bf16), vO=V((2 * hw, D), bf16), vA=V((D, D), bf16), fW=V((FZ, D), f32), fH=V((D, FZ), f32), fG=V((NP, ni, PW), f32),
+        fP=V((2, hw, PW), f32), fO=V((2 * hw, D), f32), fQ=V((hw, D), f32), fA=V((3, hw, D), f32), isem=sem((9 + nz,)), osem=sem((9 + ni,)),
+    )
+    ins = [r[k] if k != "wp" else jnp.swapaxes(wp, -1, -2) for k in finish_ins]
+    return pl.pallas_call(
+        functools.partial(finish_kernel, m, finish_ins + finish_outs + tuple(scratch)),
+        out_shape=tuple(S(s, f32) for s in shapes),
+        in_specs=[vm if k == "small" else hbm for k in finish_ins],
+        out_specs=tuple(vm if k in small else hbm for k in finish_outs),
+        scratch_shapes=list(scratch.values()),
+        compiler_params=pltpu.CompilerParams(vmem_limit_bytes=56 << 20),
+        name="finish",
+    )(*ins)
+
+
 def per_device(nd, nz, text_states, patch_states, patch_rows, cotangent, w_attn, attn_bias, w_attn_out, w_query, w_patch, cross_bias, w_cross_out, w_hidden, hidden_bias, w_output, out_bias, norm_gain, norm_shift):
     m = Dims()
     m.nz, m.bits = nz, tuple(range(nd.bit_length() - 1))
-    z = lax.axis_index("mp")
-    hw = w_query.shape[1]
-    D = text_states.shape[-1]
-    A = jnp.concatenate([w_query, w_attn[0], w_attn[2], w_attn[1]], 1)
-    B = jnp.concatenate([w_patch[0], w_patch[1]], 1)
-    O = jnp.concatenate([w_attn_out, w_cross_out], 0)
-    zero = jnp.zeros((hw,), bf16)
-    vown = jnp.stack([
-        jnp.concatenate([cross_bias[0], attn_bias[0], attn_bias[1], zero]),
-        jnp.pad(jnp.concatenate([zero, cross_bias[1]]), (0, D - 2 * hw)), hidden_bias])
-    vown = jnp.pad(vown, ((0, 13), (0, 0)))
-    r = run_layer(m, nd, (A, B, O, w_hidden, w_output), vown, text_states, patch_states, patch_rows, cotangent, out_bias.astype(f32), norm_gain.astype(f32), norm_shift.astype(f32))
-    RA, RB, RO, RH, RW = (r["R" + k].astype(f32) for k in "ABOHW")
-    small = r["small"]
-    pick = lambda base: lax.dynamic_slice_in_dim(small, base + z, 1, 0)[0]
-    cq, kv, qv = pick(9 + nz), pick(9 + 2 * nz), pick(9 + 3 * nz)
-    at = hw - LANES
-    part = lambda a, i: a[:, i * hw:(i + 1) * hw]
-    return (
-        r["layer_out"], r["text_grad"], r["patch_grad"],
-        jnp.stack([part(RA, 1), part(RA, 3), part(RA, 2)]),
-        jnp.stack([qv[at:at + hw], qv[at + hw:at + 2 * hw]]),
-        RO[:hw], part(RA, 0), jnp.stack([part(RB, 0), part(RB, 1)]),
-        jnp.stack([cq[:hw], kv[hw:2 * hw]]), RO[hw:], RH, pick(9), RW,
-        small[0:3], small[3:6], small[6:9],
-    )
+    r = run_layer(m, text_states, patch_states, patch_rows, cotangent, w_attn, attn_bias, w_attn_out, w_query, w_patch, cross_bias, w_cross_out, w_hidden, hidden_bias, w_output, out_bias, norm_gain, norm_shift)
+    outs = list(finish(m, r, w_patch))
+    for k in ("attn", "query", "patch"):
+        at = finish_outs.index(k)
+        outs[at] = jnp.swapaxes(outs[at], -1, -2)
+    at = finish_outs.index("patch_grad")
+    outs[at] = jnp.swapaxes(outs[at], 0, 1)
+    return tuple(outs)
 
 
 def solution(mesh):

time: 239 us -> 204 us (0.85)
  local copies, waits for them, and re-layouts: 21.3 us -> 0 us
  other arithmetic: 12.2 us -> 0 us
  Pallas kernels: 204 us -> 201 us
    pallas_call x1, Pallas kernels: 204 us -> 188 us  [run_layer(): pl.pallas_call(functools.partial(layer_kernel, m), out_shape=tuple((o[0]...]
    pallas_call x0 -> x1, Pallas kernels: none -> 13 us  [finish(): pl.pallas_call(functools.partial(finish_kernel, m, finish_ins + finish_ou...]
    unnamed x43 -> x0, local copies, waits for them, and re-layouts: 11.7 us -> none
    slice x7 -> x0, local copies, waits for them, and re-layouts: 6.63 us -> none  [the longest x1 2.14 us: per_device(): RO[hw:]]
    convert_element_type x7 -> x0, other arithmetic: 6.5 us -> none  [the longest x4 4.69 us: per_device(): RA, RB, RO, RH, RW = (r['R' + k].astype(f32) for k in 'ABOHW')]
    concatenate x4 -> x0, other arithmetic: 3.63 us -> none  [the longest x1 1.5 us: per_device(): A = jnp.concatenate([w_query, w_attn[0], w_attn[2], w_attn[1]], 1)]
where the time goes in v4:
time: 204 us; the launch traced here: 202 us
  Pallas kernels  201 us (99%)
    pallas_call x1, Pallas kernels, run_layer(): pl.pallas_call(functools.partial(layer_kernel, m), out_shape=tuple((o[0]...  188 us
    pallas_call x1, Pallas kernels, finish(): pl.pallas_call(functools.partial(finish_kernel, m, finish_ins + finish_ou...  13 us

profile of v4, /device:TPU:0, one launch (start us, length us, event | category | flops | bytes accessed | tf_op | source)
XLA Modules:
  0.0 202.2 jit_solution(5046115131564534735)
XLA Ops:
  0.7 188.3 %layer.1 = (f32[4,40,768]{2,1,0:T(8,128)}, f32[4,40,768]{2,1,0:T(8,128)}, bf16[4,640,384]{2,1,0:T(8,128)(2,1)}, f32[32,768]{1,0:T(8,128)}, bf16[768,768]{1,0:T(8...) custom-call(bf16[4,40,768]{2,1,0:T(8,128)(2,1)} %refs_0_.1, ...), custom_call_target="tpu_custom_call" | custom-call | tf_op jit(solution)/shard_map/layer/pallas_call | solution.py:957
  189.0 13.0 %finish.1 = (f32[4,40,768]{2,1,0:T(8,128)}, f32[4,40,768]{2,1,0:T(8,128)}, f32[145,4,1024]{2,1,0:T(4,128)}, f32[3,192,768]{2,1,0:T(8,128)}, f32[2,192]{1,0:T(2,1...) custom-call(bf16[768,768]{1,0:T(8,128)(2,1)} %get-tuple-element.42.r, ...), custom_call_target="tpu_custom_call" | custom-call | tf_op jit(solution)/shard_map/finish/pallas_call | solution.py:1074

commit v5 on v4

--- a/solution.py
+++ b/solution.py
@@ -32,7 +32,8 @@
 
 
 class Gather:
-    def __init__(self, src, dst, row0, rows, order, pos, sems, base):
+    def __init__(self, src, dst, row0, rows, order, pos, nz, sems, base):
+        self.nz = nz
         self.src, self.dst, self.row0, self.order, self.pos = src, dst, row0, order, pos
         self.piece = rows // (2 ** len(order))
         self.zs, self.zr, self.ps, self.pr = sems
@@ -49,17 +50,29 @@
     def shard(self, dr, j):
         return self.pos.z + j * (2 * dr - 1) * self.pos.sign
 
+    def cell(self, t, at):
+        return lax.rem(t - at - 1 + self.nz, jnp.int32(self.nz))
+
     def zcopy(self, dr, j):
         p = self.pos
         t, rows = self.shard(dr, j), self.win(0)
         src = self.src.at[rows] if j == 0 else self.dst.at[t, rows]
-        real = dr + p.upper - 2 * dr * p.upper
-        return pltpu.make_async_remote_copy(src, self.dst.at[t, rows], self.zs.at[self.base, real, j], self.zr.at[self.base, real, j], device_id=(p.d, p.z + (1 - 2 * dr) * p.sign), device_id_type=MESH)
+        to = p.z + (1 - 2 * dr) * p.sign
+        s = dr if j == 0 else 2 + self.cell(t, p.z)
+        return pltpu.make_async_remote_copy(src, self.dst.at[t, rows], self.zs.at[self.base, s], self.zr.at[self.base, self.cell(t, to)], device_id=(p.d, to), device_id_type=MESH)
+
+    def zwait(self, dr, j):
+        p = self.pos
+        t = self.shard(dr, j)
+        part = self.dst.at[t, self.win(0)]
+        pltpu.make_async_remote_copy(part, part, self.zs.at[self.base, 0], self.zr.at[self.base, self.cell(t, p.z)], device_id=(p.d, p.z - (1 - 2 * dr) * p.sign), device_id_type=MESH).wait_recv()
 
     def pcopy(self, s, dr, j):
         p = self.pos
-        part = self.dst.at[self.shard(dr, j), self.win(s)]
-        return pltpu.make_async_remote_copy(part, part, self.ps.at[self.base, s, dr, j - 1], self.pr.at[self.base, s, dr, j - 1], device_id=(flip(p.d, self.order[s]), p.z), device_id_type=MESH)
+        t = self.shard(dr, j)
+        part = self.dst.at[t, self.win(s)]
+        c = self.cell(t, p.z)
+        return pltpu.make_async_remote_copy(part, part, self.ps.at[self.base, c], self.pr.at[self.base, s, c], device_id=(flip(p.d, self.order[s]), p.z), device_id_type=MESH)
 
     @staticmethod
     def has(cls, nz, dr, j):
@@ -74,11 +87,11 @@
             self.zcopy(dr, 0).start()
             return
         if st == 0:
-            self.zcopy(dr, j - 1).wait_recv()
+            self.zwait(dr, j)
             if j <= nz - 2 and self.ahead(cls, dr):
                 self.zcopy(dr, j).start()
         else:
-            self.pcopy(st - 1, dr, j).wait_recv()
+            self.pcopy(st - 1, dr, j).wait()
         if st < self.k:
             self.pcopy(st, dr, j).start()
 
@@ -87,10 +100,6 @@
             for j in range(nz - 1):
                 if self.ahead(cls, dr) and self.has(cls, nz, dr, j):
                     self.zcopy(dr, j).wait_send()
-            for s in range(self.k):
-                for j in range(1, nz):
-                    if self.has(cls, nz, dr, j):
-                        self.pcopy(s, dr, j).wait_send()
 
 
 def add_into(dst, src, rows):
@@ -130,20 +139,22 @@
         self.pos, self.nz, self.bits = pos, nz, bits
         self.ss, self.rs, self.ls = sems
         self.base = base
-        self.slot = 2 * nz
-        self.pending = []
+        self.slot = 0
+        self.last = None
         self.steps = []
         self.build()
 
-    def copy(self, s, src, dst, to):
-        return lambda: pltpu.make_async_remote_copy(src, dst, self.ss.at[self.base, s], self.rs.at[self.base, s], device_id=to, device_id_type=MESH)
-
-    def remote(self, src, dst, b, keep=True):
-        cp = self.copy(self.slot, src, dst, (flip(self.pos.d, b), self.pos.z))
+    def remote(self, src, dst, b):
+        r = self.slot
         self.slot += 1
-        if keep:
-            self.pending.append(cp)
-        return cp
+        cp = lambda: pltpu.make_async_remote_copy(src, dst, self.ss.at[self.base, 0], self.rs.at[self.base, r], device_id=(flip(self.pos.d, b), self.pos.z), device_id_type=MESH)
+        before, self.last = self.last, cp
+
+        def start():
+            if before is not None:
+                before().wait_send()
+            cp().start()
+        return cp, start
 
     def build(self):
         d, z, nz = self.pos.d, self.pos.z, self.nz
@@ -151,10 +162,10 @@
         start, size, whole = jnp.int32(0), self.half, True
         taken = []
 
-        def then(prev, cp):
+        def then(prev, start):
             def step():
                 prev()
-                cp().start()
+                start()
             self.steps.append(step)
 
         for op in self.order:
@@ -170,10 +181,10 @@
             send0 = pl.multiple_of(start + (1 - m) * size, 16)
             buf = self.recvs[op]
             if whole:
-                cp = self.remote(self.keep.at[:, pl.ds(send0, size), :], buf, op)
+                cp, leave = self.remote(self.keep.at[:, pl.ds(send0, size), :], buf, op)
             else:
-                cp = self.remote(self.keep.at[z, pl.ds(send0, size), :], buf.at[0], op)
-            then(prev, cp)
+                cp, leave = self.remote(self.keep.at[z, pl.ds(send0, size), :], buf.at[0], op)
+            then(prev, leave)
 
             def prev(cp=cp, keep0=keep0, size=size, whole=whole, buf=buf):
                 cp().wait_recv()
@@ -184,24 +195,25 @@
             taken.append(op)
             start = keep0
         for e, b in enumerate(self.bits[3:]):
-            cp = self.remote(self.keep.at[z, pl.ds(start, size), :], self.extra.at[e], b, False)
-
-            def prev(before=prev, cp=cp, e=e, start=start, size=size):
+            cp, leave = self.remote(self.keep.at[z, pl.ds(start, size), :], self.extra.at[e], b)
+
+            def prev(before=prev, cp=cp, leave=leave, e=e, start=start, size=size):
                 before()
-                cp().start()
-                cp().wait()
+                leave()
+                cp().wait_recv()
+                cp().wait_send()
                 add_into(self.keep.at[z, pl.ds(start, size), :], self.extra.at[e], size)
         at = pl.multiple_of(self.row + start, 16)
         total = self.keep.at[z, pl.ds(start, size), :]
         win = self.result.at[pl.ds(at, size), :]
         own = lambda win=win: pltpu.make_async_copy(total, win, self.ls.at[self.base])
         op = taken[-1]
-        cp = self.remote(total, win, op)
-
-        def step(prev=prev, cp=cp):
+        cp, leave = self.remote(total, win, op)
+
+        def step(prev=prev, leave=leave):
             prev()
             own().start()
-            cp().start()
+            leave()
         self.steps.append(step)
 
         def prev(cp=cp):
@@ -212,24 +224,25 @@
             size *= 2
             op = nxt
             win = self.result.at[pl.ds(at, size), :]
-            cp = self.remote(win, win, op)
-            then(prev, cp)
+            cp, leave = self.remote(win, win, op)
+            then(prev, leave)
             prev = lambda cp=cp: cp().wait_recv()
         self.steps.append(prev)
 
-    def hop(self, kind, i):
+    def hop(self, cls, kind, i, arriving):
         p, nz = self.pos, self.nz
         far, near = nz - 1 - i, i
         if kind == 1:
-            t = far * (1 - p.upper) + near * p.upper
-            flow, to = p.upper, p.z + p.sign
+            t, way = far * (1 - p.upper) + near * p.upper, p.sign
         else:
-            t = near * (1 - p.upper) + far * p.upper
-            flow, to = 1 - p.upper, p.z - p.sign
+            t, way = near * (1 - p.upper) + far * p.upper, -p.sign
         cell = self.keep.at[t, self.rows, :]
-        land = self.line.at[flow, nz - 2 - i]
-        s = flow * nz + i
-        cp = lambda: pltpu.make_async_remote_copy(cell, land, self.ss.at[self.base, s], self.rs.at[self.base, s], device_id=(p.d, to), device_id_type=MESH)
+        s = 1 + (i if kind == 1 else nz - 1 - cls + i)
+        first = kind == 1 and (arriving or cls < nz // 2 - 1)
+        r = i if first else nz - 1 + i
+        to = p.z - way if arriving else p.z + way
+        land = self.line.at[r]
+        cp = pltpu.make_async_remote_copy(cell, land, self.ss.at[self.base, s], self.rs.at[self.base, 5 + len(self.bits) - 3 + r], device_id=(p.d, to), device_id_type=MESH)
         return cp, cell, land
 
     def sends(self, cls, kind):
@@ -238,20 +251,19 @@
     def along(self, cls, kind, i):
         if kind == 1 and cls == 0:
             for k in range(self.nz - 1):
-                self.hop(1, k)[0]().start()
+                self.hop(cls, 1, k, False)[0].start()
             return
-        cp, cell, land = self.hop(kind, i)
-        cp().wait_recv()
+        cp, cell, land = self.hop(cls, kind, i, True)
+        cp.wait_recv()
         add_into(cell, land, self.size)
         if i < self.sends(cls, kind):
-            cp().start()
+            self.hop(cls, kind, i, False)[0].start()
 
     def finish(self, cls):
-        for cp in self.pending:
-            cp().wait_send()
+        self.last().wait_send()
         for kind in (1, 2):
             for i in range(self.sends(cls, kind)):
-                self.hop(kind, i)[0]().wait_send()
+                self.hop(cls, kind, i, False)[0].wait_send()
 
 
 def enter(d, z, nz, bits):
@@ -347,7 +359,7 @@
     gsem = (g.zs, g.zr, g.ps, g.pr)
     own = {"A": g.AO, "B": g.BO, "O": g.OO, "H": g.H, "W": g.W, "V": g.VO}
     far = {"A": g.GA, "B": g.GB, "O": g.GO, "H": g.GH, "W": g.GW, "V": g.VG}
-    gathers = [Gather(own[k], far[k], r0, rows, order, pos, gsem, c) for c, (k, r0, rows, order) in enumerate(m.gather_plan)]
+    gathers = [Gather(own[k], far[k], r0, rows, order, pos, nz, gsem, c) for c, (k, r0, rows, order) in enumerate(m.gather_plan)]
     calls = [0, 0]
 
     def gather_steps():
@@ -445,7 +457,7 @@
         def other():
             pltpu.make_async_copy(far[key].at[shard(o), r, c], dst, done).start()
         if isinstance(o, int):
-            mine()
+            mine() if o == 0 else other()
         else:
             pl.when(o == 0)(mine)
             pl.when(o != 0)(other)
@@ -506,11 +518,12 @@
         e = jnp.exp(s - jnp.max(s, -1, keepdims=True))
         return e / jnp.sum(e, -1, keepdims=True)
 
+    gather_steps()
     for i in range(ni):
-        g.XF[i * L:(i + 1) * L] = g.x[i].astype(f32)
+        g.ACC[i * L:(i + 1) * L] = g.x[i].astype(f32)
         mine = jnp.concatenate([g.patches[:, i, :].astype(f32), jnp.zeros((KP - NP, m.PW), f32)], 0)
         g.PT[i * KP:(i + 1) * KP] = mine.astype(bf16)
-    g.X[0:T] = g.XF[...].astype(bf16)
+    g.X[0:T] = g.ACC[...].astype(bf16)
     swaps = [pair(g.X, T), pair(g.PT, ni * KP)]
     for s in swaps:
         s.start()
@@ -543,9 +556,9 @@
         return tuple(v[...].astype(f32)[j:j + 1, :] for v in (g.ob, g.gain, g.shift))
 
     ob, gn, sh = out_row(0)
-    first, normed, inv = norm_forward(g.XF[...] + g.ACC[...] + ob, gn, sh)
+    first, normed, inv = norm_forward(g.X[0:T].astype(f32) + g.ACC[...] + ob, gn, sh)
     g.NM[0] = normed
-    g.INV[0] = jnp.broadcast_to(inv, (T, LANES))
+    g.INV[...] = jnp.broadcast_to(inv, (T, LANES))
     g.F[0:T] = first.astype(bf16)
     g.ACC[...] = jnp.zeros((T, D), f32)
     gather_steps()
@@ -577,7 +590,7 @@
     ob, gn, sh = out_row(1)
     second, normed, inv = norm_forward(g.F[0:T].astype(f32) + g.ACC[...] + ob, gn, sh)
     g.NM[1] = normed
-    g.INV[1] = jnp.broadcast_to(inv, (T, LANES))
+    g.INV[:, HEAD:] = jnp.broadcast_to(inv, (T, LANES - HEAD))
     g.S2[0:T] = second.astype(bf16)
     gather_steps()
     other = g.MX.at[1 - core]
@@ -686,7 +699,7 @@
             cp.wait()
 
     gn = out_row(1)[1]
-    normed, inv = g.NM[1], g.INV[1][:, 0:1]
+    normed, inv = g.NM[1], g.INV[:, HEAD:HEAD + 1]
     grad = g.ACC[...]
     secondg = norm_backward(grad, normed, inv, gn)
     record(1, secondg, grad, normed)
@@ -735,12 +748,11 @@
         g.SM[pl.ds(9 + nz + t, 1), 0:hp] = col_sum(dcq.astype(f32))
         g.SM[pl.ds(9 + 2 * nz + t, 1), 0:m.BW] = col_sum(dkv.astype(f32))
         g.ACC[...] += dot(dcq, g.SA[o, 0:hp])
-        pltpu.make_async_copy(g.DKV.at[o, pl.ds(0, ni * KP)], g.DK.at[o], g.dk.at[o]).start()
 
     stream([], cross_backward, after_each(reduce_steps), [], self_blocks)
     reduce_steps()
     gn = out_row(0)[1]
-    normed, inv = g.NM[0], g.INV[0][:, 0:1]
+    normed, inv = g.NM[0], g.INV[:, 0:1]
     grad = g.ACC[...]
     firstg = norm_backward(grad, normed, inv, gn)
     record(0, firstg, grad, normed)
@@ -758,6 +770,8 @@
         deal("B", t, g.TMP[pl.ds(pl.multiple_of(core * HEAD, 16), BW // 2)])
         return c
     lax.fori_loop(0, nz, job_b, 0)
+    for o in range(2):
+        fetch(cross_blocks[1], o, o)
     reduce_steps()
 
     g.ACC[...] = firstg
@@ -821,15 +835,29 @@
     reduce_steps()
 
     reduce_steps()
+    for part in range(nz // 2):
+        for slot in range(2):
+            arrived(cross_blocks[1], slot)
+        for i in range(ni):
+            r = pl.ds(i * KP, KP)
+            total = (dot(g.DKV[2 * part, r], g.SB[0]) + dot(g.DKV[2 * part + 1, r], g.SB[1]))[0:NP]
+            g.PG[:, i, :] = total if part == 0 else g.PG[:, i, :] + total
+            if i == ni - 1 and part < nz // 2 - 1:
+                for slot in range(2):
+                    fetch(cross_blocks[1], slot, 2 * part + 2 + slot)
+            if i == ni - 1 and part == nz // 2 - 1:
+                patch_store = pltpu.make_async_copy(g.PG, g.patch_out, g.js.at[9])
+                patch_store.start()
+            if i % 2 == 1:
+                reduce_steps()
     assert calls == [len(m.gather_steps[0]), len(m.reduce_steps[0])], calls
     assert all(sum(len(p) for p in m.reduce_steps[cls]) == sum(progress[cls, c, w] for c in range(len(chunks) + 1) for w in range(3)) for cls in classes)
 
     sends = [small_spread(o, lambda to: z) for o in range(1, nz)]
     for cp in sends + swaps + [swap1, swap2, swap3, mix_swap]:
         cp.wait_send()
-    for o in range(nz):
-        pltpu.make_async_copy(g.DKV.at[o, pl.ds(0, ni * KP)], g.DK.at[o], g.dk.at[o]).wait()
     text_store.wait()
+    patch_store.wait()
     finish_gather()
     for cls in classes:
         @pl.when(kind == cls)
@@ -838,29 +866,33 @@
                 c.finish(cls)
 
 
-GATHER_PLAN = (("V", 0, 16, ""), ("A", 0, 256, "yxc"), ("A", 256, 256, "yxc"), ("A", 512, 256, "xyc"), ("B", 0, 384, "xc"), ("O", 0, 384, "xyc"), ("H", 0, 256,
-    "yxc"), ("H", 256, 256, "yc"), ("H", 512, 256, "xyc"), ("W", 512, 256, "xc"), ("W", 256, 256, "xyc"), ("W", 0, 256, "yc"))
-GATHER_ORDER = ((0, 80, 120, 40, 200, 400, 13, 93, 133, 53, 101, 213, 141, 413, 61, 14, 94, 109, 134, 149, 221, 117, 54, 102, 421, 157, 214, 414, 69, 160, 15, 142,
-    95, 77, 229, 135, 320, 62, 110, 55, 237, -1, 118, 222, 215, 429, 422, 415, 143, 150, 240, 280, 103, 437, 158, 70, 63, 173, 223, 78, 333, 423, 230,
-    111, 238, -1, 119, 71, 430, 151, 334, 174, 253, 79, 438, 159, 231, 293, 181, 360, 341, 440, 239, -1, 431, 342, 189, 175, 261, -1, 439, 335, 182, 254,
-    301, -1, 349, 350, 190, 262, 183, 255, 309, 294, -1, 453, 357, 358, 343, 191, 269, 263, 295, -1, 373, 277, 270, 302, -1, 461, 454, 278, 374, 271, 351,
-    310, -1, 469, 359, 381, 375, 279, 303, -1, 455, 382, 462, 389, 311, -1, 390, -1, 470, 383, -1, 463, -1, 391, 471, -1, -1), (0, 4, 80, 84, 120, 124,
-    40, 44, 200, 204, 400, 404, 9, 13, 89, 93, 129, 133, 49, 53, 97, 209, 213, 101, 137, 409, 413, 141, 57, 14, 61, 94, 105, 134, 145, 54, 217, 113, 153,
-    214, 149, 221, 414, 102, 160, 164, 157, 109, 62, 417, 117, 320, 421, 324, 225, 65, 233, 169, 173, 73, -1, 142, 69, 229, 425, 329, 333, 222, 240, 244,
-    280, 249, 284, 422, 77, 429, 237, 174, 433, 289, 110, 437, 334, 150, 253, 118, 70, 158, 293, 230, 78, 254, 257, 238, -1, 430, 177, 294, -1, 440, 444,
-    438, 360, 185, 364, 181, 261, 297, -1, 337, 341, 189, 369, 262, 305, 301, -1, 449, 453, 182, 345, 373, 309, 302, 342, 374, 190, 349, -1, 457, 454,
-    353, 357, 265, 269, 310, -1, 465, 461, 377, 273, 277, -1, 469, 462, 350, 385, 270, 381, -1, 470, 358, 382, 278, -1, 389, -1, 390, -1, -1, -1, -1, -1))
-REDUCE_PLAN = (("W", 128, "zyx"), ("W", 128, "yxz"), ("W", 128, "xyz"), ("H", 128, "xyz"), ("H", 128, "zxy"), ("H", 128, "yxz"), ("B", 64, "xyz"), ("B", 128,
-    "yzx"), ("O", 64, "xyz"), ("O", 64, "zyx"), ("O", 64, "zxy"), ("A", 128, "yxz"), ("A", 128, "yxz"), ("A", 128, "xzy"))
-REDUCE_ORDER = ((-1, -1, 0, 1, 6, 3, -1, -1, -1, -1, -1, -1, 15, 9, 12, 13, -1, 6, 3, -1, -1, -1, 2, 0, 15, 9, -1, -1, 0, 18, 6, 7, 3, 4, 21, -1, 0, 15, 16, -1, 9,
-    10, -1, -1, 0, 18, 14, 12, 8, 6, -1, 27, 28, 24, 30, 31, -1, 39, 33, 36, 5, 0, 3, 21, 22, 12, 17, 15, -1, 0, 42, 24, 18, 19, 42, 6, 11, 9, 39, 40, 29,
-    27, 3, 33, 15, 32, 42, 30, 6, 6, 36, 33, 34, 12, 30, 23, 21, 24, 25, 20, 18, 9, 27, 36, 37, 3, 21, 3, 15, 9, 27, 41, 39, 15, 42, 21, 9, 27, 12, 30,
-    35, 33, 18, 39, 26, 24, 12, 33, 21, 12, 38, 36, 27, 18, 30, 21, 27, 39, 42, 18, 24, 36, 42, 30, 33, 30, 39, 33, 36, 24, 39, 36, 24), (-1, -1, 0, 6, 3,
-    -1, -1, -1, -1, -1, 1, -1, 15, 9, 12, -1, 1, 6, 3, 2, -1, 1, -1, 2, 0, 13, -1, 15, 9, -1, 6, 3, 13, -1, 0, 18, 21, 15, 13, 14, -1, 0, 7, 7, 7, 9, 14,
-    12, -1, 8, 4, 4, 4, 8, 6, -1, 0, 18, 5, 16, 16, 16, 5, 3, 10, -1, 17, 21, 3, 10, 17, 6, 15, 10, 12, -1, 0, 11, 11, 9, 27, 28, 28, 24, 30, -1, 39, 0,
-    33, 18, 6, 36, 3, 15, 28, 29, 31, 12, -1, 6, 42, 9, 3, 29, 27, 24, 31, 42, 31, 32, 32, 30, 22, 22, 33, 39, 23, 22, 9, 19, 19, 9, 23, 19, 42, 21, 20,
-    30, 20, 18, 40, 36, 40, 33, 15, 41, 40, 21, 12, 34, 15, 27, 41, 39, 34, 34, 24, 35, 25, 25, 36, 25, 35, 33, 37, 42, 21, 30, 26, 37, 26, 18, 24, 37,
-    39, 12, 38, 27, 38, 33, 36, 12, 21, 18, 30, 27, 24, 21, 36, 39, 18, 42, 30, 42, 33, 24, 30, 27, 33, 24, 39, 27, 36, 39, 36))
+GATHER_PLAN = (("V", 0, 16, ""), ("H", 256, 256, "yxc"), ("A", 256, 256, "yxc"), ("A", 512, 256, "yc"), ("O", 0, 384, "yxc"), ("B", 0, 128, "yxc"), ("B", 128, 256,
+    "yc"), ("H", 0, 256, "xc"), ("A", 0, 256, "yxc"), ("H", 512, 256, "xyc"), ("W", 0, 256, "xc"), ("W", 256, 256, "xyc"), ("W", 512, 256, "yc"))
+GATHER_ORDER = ((0, 320, 160, 80, -1, 13, 360, 93, 333, 373, 101, 173, 120, 14, 341, 381, 94, 334, 200, 181, 374, 109, 174, 117, 389, 349, 102, 133, 397, 342, 15,
+    357, 189, 335, 182, 382, 240, 40, 175, 197, 213, 141, 110, 440, 95, 343, 149, -1, 390, 375, 118, 134, 350, 214, 183, 221, 398, 190, 358, 103, 135,
+    280, 198, 351, 480, 142, 383, 222, 253, 359, 150, 215, -1, 143, 53, 191, 453, 391, 229, 151, 199, 254, 399, 400, 111, 237, 54, 261, 223, 230, 454,
+    119, -1, 269, 238, 61, 293, 461, -1, 262, 231, 255, 62, 462, -1, 270, 239, 69, 55, 301, 469, 455, 493, 263, -1, 77, 271, 70, 309, 294, 63, 477, 470,
+    463, 494, -1, 78, 413, 478, 501, -1, 302, 71, 295, 471, 414, 509, 502, -1, 79, 421, 310, 479, 510, 303, 495, 415, -1, 429, 311, 422, -1, -1, 430, 423,
+    503, -1, -1, 431, 511, -1, -1), (0, 4, 320, 80, 84, 324, 360, 364, 160, 164, -1, 9, 13, 93, 329, 333, 169, 373, 89, 369, 173, 120, 124, 14, 101, 381,
+    334, 337, 341, 377, 174, 200, 204, 94, 177, 129, 109, 374, 97, 209, 117, 181, 345, 133, 213, 353, 389, 349, 134, 240, 244, 342, 397, 214, 40, 357, 44,
+    440, 385, 185, 444, 382, 182, 393, 193, 102, 249, 253, 105, 49, 53, 137, 449, 113, 453, 217, 145, 189, 280, 284, -1, 254, 221, 141, 350, 54, 197, 454,
+    480, 142, 289, 484, 222, 149, 358, 190, 293, 150, 489, 390, 198, 110, 493, 400, 398, 404, 457, 118, -1, 257, 225, 294, 461, -1, 265, 261, 233, 229,
+    57, 409, 61, 413, 462, 494, -1, 269, 237, 262, 230, 297, -1, 270, 238, 62, 414, 305, 301, 302, 497, -1, 65, 309, 310, 465, 505, 501, 417, -1, 73, 69,
+    425, 473, 469, 509, -1, 77, 421, 477, 470, 502, 70, -1, 429, 78, 422, 478, 510, -1, 430, -1, -1, -1, -1, -1, -1))
+REDUCE_PLAN = (("W", 128, "xyz"), ("W", 128, "yxz"), ("W", 128, "zyx"), ("H", 128, "zyx"), ("H", 128, "xyz"), ("H", 128, "xzy"), ("B", 128, "yzx"), ("B", 64,
+    "xyz"), ("O", 64, "yzx"), ("O", 64, "xyz"), ("O", 64, "zxy"), ("A", 64, "xyz"), ("A", 64, "yxz"), ("A", 64, "zxy"), ("A", 64, "yzx"), ("A", 64,
+    "xyz"), ("A", 64, "xyz"))
+REDUCE_ORDER = ((-1, -1, 6, 7, 0, 3, -1, -1, -1, -1, -1, -1, 12, 9, 10, 15, -1, 0, 3, -1, -1, -1, 0, 1, 12, -1, 8, 6, -1, 18, 21, 12, 13, -1, 6, 15, 16, -1, 3, 4,
+    -1, -1, 2, 0, 21, 11, 9, 6, -1, 30, 31, 0, 18, 6, 19, 24, 27, 14, 12, -1, 48, 36, 0, 39, 40, 45, 33, 21, 22, 42, 9, 0, 6, 17, 15, 5, 3, -1, 51, -1, 6,
+    51, 27, -1, 24, 25, 12, -1, 48, -1, 36, 32, 30, 45, 42, 43, 33, 15, 9, 3, 20, 18, 27, 28, 51, 48, 49, 12, 45, 46, 41, 39, 12, 36, 37, 33, 34, 23, 30,
+    21, 15, 9, 26, 24, 18, 3, 39, 3, 51, 30, 44, 42, 15, 21, 24, 29, 27, 15, 18, 9, 42, 50, 48, 39, 30, 21, 27, 9, 24, 47, 45, 42, 21, 38, 30, 36, 18, 48,
+    27, 51, 39, 30, 35, 33, 18, 24, 27, 36, 45, 24, 48, 42, 33, 39, 48, 42, 36, 45, 39, 51, 36, 33, 45, 33), (-1, -1, 6, 0, 3, -1, -1, -1, -1, -1, 7, -1,
+    12, 9, 15, -1, 7, 0, 3, -1, 7, 8, -1, -1, 8, 6, 0, 12, 10, -1, 10, -1, 6, 18, 21, 10, 1, 12, 11, 15, 1, -1, 1, 13, 13, 2, 6, 3, 13, 11, 2, 0, 9, -1,
+    14, 14, 12, 16, 16, -1, 6, 21, 16, 18, 4, 17, 4, 0, -1, 4, 9, 5, 12, 17, 15, 5, 3, 0, -1, 30, 31, 31, 6, 0, 31, 24, 27, 12, 21, 9, 6, -1, 48, 32, 36,
+    39, 45, 19, 33, 42, 32, 30, 19, 12, 24, 27, 3, 15, -1, 51, 9, -1, 19, 51, 20, -1, 36, 40, 48, -1, 40, 20, 18, -1, 40, 22, 41, 45, 22, 22, 42, 27, 25,
+    41, 39, 23, 25, 3, 23, 21, 25, 15, 33, 26, 43, 3, 30, 43, 26, 24, 9, 43, 51, 28, 28, 44, 48, 28, 9, 49, 44, 42, 49, 36, 49, 29, 45, 46, 18, 46, 21,
+    50, 46, 39, 50, 48, 37, 37, 29, 37, 47, 33, 30, 47, 45, 34, 34, 34, 24, 38, 27, 38, 36, 51, 39, 18, 42, 48, 35, 30, 15, 35, 45, 33, 21, 24, 27, 39,
+    36, 51, 42, 15, 21, 48, 30, 18, 48, 33, 45, 30, 24, 27, 18, 45, 36, 39, 24, 51, 27, 42, 33, 36, 39, 42, 33))
 
 
 def unpack(orders, decode):
@@ -921,18 +953,18 @@
     nb = len(m.bits)
     sums = (9 + 4 * nz + 7) // 8 * 8
     scratch = dict(
-        VG=V((nz, 16, D), bf16), XF=V((T, D), f32), X=V((2 * T, D), bf16), PT=V((2 * ni * KP, PW), bf16),
+        VG=V((nz, 16, D), bf16), X=V((2 * T, D), bf16), PT=V((2 * ni * KP, PW), bf16),
         SA=V((nz, D, D), bf16), SH=V((2, D, D), bf16), SB=V((2, BW, PW), bf16), SO=V((nz, hp, D), bf16),
         ACC=V((T, D), f32), QKV=V((nz, T, m.QW), bf16), PS=V((nz * ni, m.nh * L, L), f32), MX=V((2, nz, 2 * T, hp), bf16),
-        NM=V((2, T, D), f32), INV=V((2, T, LANES), f32), F=V((2 * T, D), bf16), S2=V((2 * T, D), bf16),
+        NM=V((2, T, D), f32), INV=V((T, LANES), f32), F=V((2 * T, D), bf16), S2=V((2 * T, D), bf16),
         CQ=V((nz, T, hp), bf16), PC=V((nz * ni, m.nh * L, KP), f32),
         GP=V((nz, T, FZ), f32), HD=V((nz, 2 * T, FZ), bf16), SM=V((sums, D), f32), G3=V((2 * T, D), bf16), DP=V((nz, 2 * T, FZ), bf16),
         G12=V((2, 2 * T, D), bf16), DKV=V((nz, 2 * ni * KP, m.BW), bf16),
-        TMP=V((hp, PW), f32), FO=V((ni, L, D), f32), AO=V((D, D), bf16), BO=V((BW, PW), bf16), OO=V((2 * hw, D), bf16), VO=V((16, D), bf16), SR=V((nb, sums, D), f32), SZ=V((nz, sums, D), f32),
-        zs=sem((ng, 2, nz)), zr=sem((ng, 2, nz)), ps=sem((ng, 3, 2, nz)), pr=sem((ng, 3, 2, nz)),
+        TMP=V((hp, PW), f32), FO=V((ni, L, D), f32), PG=V((m.NP, ni, PW), f32), AO=V((D, D), bf16), BO=V((BW, PW), bf16), OO=V((2 * hw, D), bf16), VO=V((16, D), bf16), SR=V((nb, sums, D), f32), SZ=V((nz, sums, D), f32),
+        zs=sem((ng, nz + 1)), zr=sem((ng, nz - 1)), ps=sem((ng, nz - 1)), pr=sem((ng, 3, nz - 1)),
         cs=sem((m.swaps,)), cr=sem((m.swaps,)), ds=sem((4, nz)), dr=sem((4, nz)),
-        dk=sem((nz,)), js=sem((9,)), sa=sem((nz,)), sh=sem((2,)), sb=sem((2,)), so=sem((nz,)),
-        ss=sem((nc, 2 * nz + 5 + nb)), rs=sem((nc, 2 * nz + 5 + nb)), ls=sem((nc,)), ms=sem((nb + nz,)), mr=sem((nb,)), zm=sem((nz,)),
+        js=sem((10,)), sa=sem((nz,)), sh=sem((2,)), sb=sem((2,)), so=sem((nz,)),
+        ss=sem((nc, nz)), rs=sem((nc, 5 + nb - 3 + nz - 1 + nz // 2)), ls=sem((nc,)), ms=sem((nb + nz,)), mr=sem((nb,)), zm=sem((nz,)),
     )
     for c, (k, h0, half, order) in enumerate(m.reduce_plan):
         C = lanes[k]
@@ -940,13 +972,13 @@
         for b in m.bits[1:3]:
             lead = nz if order.index(b) < order.index("z") else 1
             scratch[f"rv{c}_{b}"] = V((lead, op_rows(half, order, b), C), bf16)
-        scratch[f"ln{c}"] = V((2, nz - 1, op_rows(half, order, "z"), C), bf16)
+        scratch[f"ln{c}"] = V((nz - 1 + nz // 2, op_rows(half, order, "z"), C), bf16)
         if nb > 3:
             scratch[f"ex{c}"] = V((nb - 3, half // 4, C), bf16)
     S = jax.ShapeDtypeStruct
     hbm, vm, sm = (pl.BlockSpec(memory_space=s) for s in (pl.ANY, pltpu.VMEM, pltpu.SMEM))
     outs = dict(
-        layer_out=(S((ni, L, D), f32), hbm), text_grad=(S((ni, L, D), f32), hbm), DK=(S((nz, ni * KP, m.BW), bf16), hbm), small=(S((sums, D), f32), vm),
+        layer_out=(S((ni, L, D), f32), hbm), text_grad=(S((ni, L, D), f32), hbm), patch_out=(S((m.NP, ni, PW), f32), hbm), small=(S((sums, D), f32), vm),
         **{"R" + k: (S((m.rows[k], lanes[k]), bf16), hbm) for k in "ABOHW"},
         **{"G" + k: (S((nz, m.rows[k], lanes[k]), bf16), hbm) for k in "ABOHW"},
     )
@@ -966,7 +998,7 @@
     return dict(zip(outs, res))
 
 
-finish_ins = ("RA", "RB", "RO", "RH", "RW", "layer_out", "text_grad", "DK", "GB", "wp", "small")
+finish_ins = ("RA", "RB", "RO", "RH", "RW", "layer_out", "text_grad", "patch_out", "small")
 finish_outs = ("layer_out_", "text_grad_", "patch_grad", "attn", "attn_bias", "attn_out", "query", "patch", "cross_bias", "cross_out", "hidden", "hidden_bias", "output", "out_bias", "gain", "shift")
 
 
@@ -984,11 +1016,7 @@
         loads[name] = cp
     load("W", g.RW, g.vW)
     load("H", g.RH, g.vH)
-    load("DK", g.DK, g.vD)
-    for j in range(2):
-        load(f"B0{j}", g.wp.at[j], g.vB.at[0, pl.ds(j * hw, hw)])
-    for o in range(1, nz):
-        load(f"B{o}", g.GB.at[nth_shard(z, nz, jnp.int32(o))], g.vB.at[o])
+    load("pg", g.patch_out, g.fG)
     load("lo", g.layer_out, g.vL)
     load("tg", g.text_grad, g.vT)
     load("B", g.RB, g.vP)
@@ -1016,14 +1044,7 @@
     loads["H"].wait()
     widen(g.vH, g.fH)
     store(g.fH, g.hidden)
-    loads["DK"].wait()
-    for k in ["B00", "B01"] + [f"B{o}" for o in range(1, nz)]:
-        loads[k].wait()
-    for i in range(ni):
-        total = dot(g.vD[0, i * KP:(i + 1) * KP], g.vB[0])
-        for o in range(1, nz):
-            total = total + dot(g.vD[o, i * KP:(i + 1) * KP], g.vB[o])
-        g.fG[:, i, :] = total[0:NP]
+    loads["pg"].wait()
     store(g.fG, g.patch_grad)
     loads["lo"].wait()
     store(g.vL, g.layer_out_)
@@ -1058,7 +1079,7 @@
         cp.wait()
 
 
-def finish(m, r, wp):
+def finish(m, r):
     nz, ni, L, D, PW, FZ, BW, KP, NP = m.nz, m.ni, m.L, m.D, m.PW, m.FZ, m.BW, m.KP, m.NP
     hw = m.hw = D // nz
     S, V, sem = jax.ShapeDtypeStruct, pltpu.VMEM, pltpu.SemaphoreType.DMA
@@ -1066,11 +1087,11 @@
     shapes = ((ni, L, D), (ni, L, D), (NP, ni, PW), (3, hw, D), (2, hw), (hw, D), (hw, D), (2, hw, PW), (2, hw), (hw, D), (D, FZ), (FZ,), (FZ, D), (3, D), (3, D), (3, D))
     small = {"attn_bias", "cross_bias", "hidden_bias", "out_bias", "gain", "shift"}
     scratch = dict(
-        vW=V((FZ, D), bf16), vH=V((D, FZ), bf16), vD=V((nz, ni * KP, BW), bf16), vB=V((nz, BW, PW), bf16), vL=V((ni, L, D), f32), vT=V((ni, L, D), f32),
+        vW=V((FZ, D), bf16), vH=V((D, FZ), bf16), vL=V((ni, L, D), f32), vT=V((ni, L, D), f32),
         vP=V((BW, PW), bf16), vO=V((2 * hw, D), bf16), vA=V((D, D), bf16), fW=V((FZ, D), f32), fH=V((D, FZ), f32), fG=V((NP, ni, PW), f32),
-        fP=V((2, hw, PW), f32), fO=V((2 * hw, D), f32), fQ=V((hw, D), f32), fA=V((3, hw, D), f32), isem=sem((9 + nz,)), osem=sem((9 + ni,)),
+        fP=V((2, hw, PW), f32), fO=V((2 * hw, D), f32), fQ=V((hw, D), f32), fA=V((3, hw, D), f32), isem=sem((8,)), osem=sem((11,)),
     )
-    ins = [r[k] if k != "wp" else jnp.swapaxes(wp, -1, -2) for k in finish_ins]
+    ins = [r[k] for k in finish_ins]
     return pl.pallas_call(
         functools.partial(finish_kernel, m, finish_ins + finish_outs + tuple(scratch)),
         out_shape=tuple(S(s, f32) for s in shapes),
@@ -1086,7 +1107,7 @@
     m = Dims()
     m.nz, m.bits = nz, tuple(range(nd.bit_length() - 1))
     r = run_layer(m, text_states, patch_states, patch_rows, cotangent, w_attn, attn_bias, w_attn_out, w_query, w_patch, cross_bias, w_cross_out, w_hidden, hidden_bias, w_output, out_bias, norm_gain, norm_shift)
-    outs = list(finish(m, r, w_patch))
+    outs = list(finish(m, r))
     for k in ("attn", "query", "patch"):
         at = finish_outs.index(k)
         outs[at] = jnp.swapaxes(outs[at], -1, -2)

time: 204 us -> 194 us (0.951)
  Pallas kernels: 201 us -> 193 us
    pallas_call x1, Pallas kernels: 188 us -> 184 us  [run_layer(): pl.pallas_call(functools.partial(layer_kernel, m), out_shape=tuple((o[0]...]
    pallas_call x1, Pallas kernels: 13 us -> 9.02 us  [finish(): pl.pallas_call(functools.partial(finish_kernel, m, finish_ins + finish_ou...]
where the time goes in v5:
time: 194 us
  Pallas kernels  193 us (99%)
    pallas_call x1, Pallas kernels, run_layer(): pl.pallas_call(functools.partial(layer_kernel, m), out_shape=tuple((o[0]...  184 us
    pallas_call x1, Pallas kernels, finish(): pl.pallas_call(functools.partial(finish_kernel, m, finish_ins + finish_ou...  9.02 us

profile of v5, /device:TPU:0, one launch (start us, length us, event | category | flops | bytes accessed | tf_op | source)
XLA Modules:
  0.0 194.1 jit_solution(16867840244935093080)
XLA Ops:
  0.7 184.2 %layer.1 = (f32[4,40,768]{2,1,0:T(8,128)}, f32[4,40,768]{2,1,0:T(8,128)}, f32[145,4,1024]{2,1,0:T(4,128)}, f32[32,768]{1,0:T(8,128)}, bf16[768,768]{1,0:T(8,128)...) custom-call(bf16[4,40,768]{2,1,0:T(8,128)(2,1)} %refs_0_.1, ...), custom_call_target="tpu_custom_call" | custom-call | tf_op jit(solution)/shard_map/layer/pallas_call | solution.py:989
  184.9 9.0 %finish.1 = (f32[4,40,768]{2,1,0:T(8,128)}, f32[4,40,768]{2,1,0:T(8,128)}, f32[145,4,1024]{2,1,0:T(4,128)}, f32[3,192,768]{2,1,0:T(8,128)}, f32[2,192]{1,0:T(2,1...) custom-call(bf16[768,768]{1,0:T(8,128)(2,1)} %get-tuple-element.41.r, ...), custom_call_target="tpu_custom_call" | custom-call | tf_op jit(solution)/shard_map/finish/pallas_call | solution.py:1095

commit v6 on v5

--- a/solution.py
+++ b/solution.py
@@ -36,8 +36,8 @@
         self.nz = nz
         self.src, self.dst, self.row0, self.order, self.pos = src, dst, row0, order, pos
         self.piece = rows // (2 ** len(order))
-        self.zs, self.zr, self.ps, self.pr = sems
-        self.base = base
+        self.zs, self.zr, self.pr = sems
+        self.rbase, self.base = base, base * 2 * nz
         self.k = len(order)
 
     def win(self, s):
@@ -58,21 +58,21 @@
         t, rows = self.shard(dr, j), self.win(0)
         src = self.src.at[rows] if j == 0 else self.dst.at[t, rows]
         to = p.z + (1 - 2 * dr) * p.sign
-        s = dr if j == 0 else 2 + self.cell(t, p.z)
-        return pltpu.make_async_remote_copy(src, self.dst.at[t, rows], self.zs.at[self.base, s], self.zr.at[self.base, self.cell(t, to)], device_id=(p.d, to), device_id_type=MESH)
+        s = self.base + (dr if j == 0 else 2 + self.cell(t, p.z))
+        return pltpu.make_async_remote_copy(src, self.dst.at[t, rows], self.zs.at[s], self.zr.at[self.rbase, self.cell(t, to)], device_id=(p.d, to), device_id_type=MESH)
 
     def zwait(self, dr, j):
         p = self.pos
         t = self.shard(dr, j)
         part = self.dst.at[t, self.win(0)]
-        pltpu.make_async_remote_copy(part, part, self.zs.at[self.base, 0], self.zr.at[self.base, self.cell(t, p.z)], device_id=(p.d, p.z - (1 - 2 * dr) * p.sign), device_id_type=MESH).wait_recv()
+        pltpu.make_async_remote_copy(part, part, self.zs.at[self.base], self.zr.at[self.rbase, self.cell(t, p.z)], device_id=(p.d, p.z - (1 - 2 * dr) * p.sign), device_id_type=MESH).wait_recv()
 
     def pcopy(self, s, dr, j):
         p = self.pos
         t = self.shard(dr, j)
         part = self.dst.at[t, self.win(s)]
         c = self.cell(t, p.z)
-        return pltpu.make_async_remote_copy(part, part, self.ps.at[self.base, c], self.pr.at[self.base, s, c], device_id=(flip(p.d, self.order[s]), p.z), device_id_type=MESH)
+        return pltpu.make_async_remote_copy(part, part, self.zs.at[self.base + self.nz + 1 + c], self.pr.at[self.rbase, s, c], device_id=(flip(p.d, self.order[s]), p.z), device_id_type=MESH)
 
     @staticmethod
     def has(cls, nz, dr, j):
@@ -147,7 +147,7 @@
     def remote(self, src, dst, b):
         r = self.slot
         self.slot += 1
-        cp = lambda: pltpu.make_async_remote_copy(src, dst, self.ss.at[self.base, 0], self.rs.at[self.base, r], device_id=(flip(self.pos.d, b), self.pos.z), device_id_type=MESH)
+        cp = lambda: pltpu.make_async_remote_copy(src, dst, self.ss.at[self.base * self.nz], self.rs.at[self.base, r], device_id=(flip(self.pos.d, b), self.pos.z), device_id_type=MESH)
         before, self.last = self.last, cp
 
         def start():
@@ -242,7 +242,7 @@
         r = i if first else nz - 1 + i
         to = p.z - way if arriving else p.z + way
         land = self.line.at[r]
-        cp = pltpu.make_async_remote_copy(cell, land, self.ss.at[self.base, s], self.rs.at[self.base, 5 + len(self.bits) - 3 + r], device_id=(p.d, to), device_id_type=MESH)
+        cp = pltpu.make_async_remote_copy(cell, land, self.ss.at[self.base * self.nz + s], self.rs.at[self.base, 5 + len(self.bits) - 3 + r], device_id=(p.d, to), device_id_type=MESH)
         return cp, cell, land
 
     def sends(self, cls, kind):
@@ -270,9 +270,15 @@
     bar = pltpu.get_barrier_semaphore()
     for b in bits:
         pl.semaphore_signal(bar, inc=1, device_id=(flip(d, b), z), device_id_type=MESH)
-    for o in range(1, nz):
-        pl.semaphore_signal(bar, inc=1, device_id=(d, lax.rem(z + o, jnp.int32(nz))), device_id_type=MESH)
-    pl.semaphore_wait(bar, len(bits) + nz - 1)
+    @pl.when(z + 1 < nz)
+    def _():
+        pl.semaphore_signal(bar, inc=1, device_id=(d, z + 1), device_id_type=MESH)
+
+    @pl.when(z >= 1)
+    def _():
+        pl.semaphore_signal(bar, inc=1, device_id=(d, z - 1), device_id_type=MESH)
+    last = nz - 1
+    pl.semaphore_wait(bar, len(bits) + lax.div(z + last, jnp.int32(nz)) + lax.div(last - z + last, jnp.int32(nz)))
 
 
 def dot(a, b):
@@ -343,6 +349,9 @@
              (g.wp.at[0], g.BO.at[pl.ds(0, hw)]), (g.wp.at[1], g.BO.at[pl.ds(hw, hw)]), (g.wao, g.OO.at[pl.ds(0, hw)]), (g.wco, g.OO.at[pl.ds(hw, hw)])]
     joins = [pltpu.make_async_copy(a, b, g.js.at[i]) for i, (a, b) in enumerate(joins)]
     for cp in joins:
+        cp.start()
+    loads = [pltpu.make_async_copy(a, b, g.js.at[10 + i]) for i, (a, b) in enumerate(((g.x, g.XV), (g.patches, g.PV)))]
+    for cp in loads:
         cp.start()
     g.TMP[0:16, 0:D] = jnp.zeros((16, D), f32)
     ab, cb = g.ab[...].astype(f32), g.cb[...].astype(f32)
@@ -356,7 +365,7 @@
     enter(d, z, nz, m.bits)
     for cp in joins:
         cp.wait()
-    gsem = (g.zs, g.zr, g.ps, g.pr)
+    gsem = (g.out, g.zr, g.pr)
     own = {"A": g.AO, "B": g.BO, "O": g.OO, "H": g.H, "W": g.W, "V": g.VO}
     far = {"A": g.GA, "B": g.GB, "O": g.GO, "H": g.GH, "W": g.GW, "V": g.VG}
     gathers = [Gather(own[k], far[k], r0, rows, order, pos, nz, gsem, c) for c, (k, r0, rows, order) in enumerate(m.gather_plan)]
@@ -381,6 +390,8 @@
     def small_spread(o, frm):
         to = lax.rem(z + o, jnp.int32(nz))
         return pltpu.make_async_remote_copy(g.SM, g.SZ.at[frm(to)], g.ms.at[nb + o], g.zm.at[frm(to)], device_id=(d, to), device_id_type=MESH)
+
+    small_store = lambda: pltpu.make_async_copy(g.SM, g.small, g.js.at[13])
 
     def small_step(i):
         if i > 0 and i < 4:
@@ -399,10 +410,13 @@
         elif i == 5:
             for o in range(1, nz):
                 small_spread(o, lambda to: to).wait_recv()
+            for o in range(1, nz):
+                small_spread(o, lambda to: z).wait_send()
             total = g.SZ[0]
             for t in range(1, nz):
                 total = total + g.SZ[t]
-            g.small[...] = total
+            g.SM[...] = total
+            small_store().start()
 
     def reduce_steps():
         at = calls[1]
@@ -519,11 +533,15 @@
         return e / jnp.sum(e, -1, keepdims=True)
 
     gather_steps()
+    for cp in loads:
+        cp.wait()
     for i in range(ni):
-        g.ACC[i * L:(i + 1) * L] = g.x[i].astype(f32)
-        mine = jnp.concatenate([g.patches[:, i, :].astype(f32), jnp.zeros((KP - NP, m.PW), f32)], 0)
+        g.ACC[i * L:(i + 1) * L] = g.XV[i].astype(f32)
+        mine = jnp.concatenate([g.PV[:, i, :].astype(f32), jnp.zeros((KP - NP, m.PW), f32)], 0)
         g.PT[i * KP:(i + 1) * KP] = mine.astype(bf16)
     g.X[0:T] = g.ACC[...].astype(bf16)
+    cot_load = pltpu.make_async_copy(g.cot, g.XV, g.js.at[12])
+    cot_load.start()
     swaps = [pair(g.X, T), pair(g.PT, ni * KP)]
     for s in swaps:
         s.start()
@@ -621,12 +639,13 @@
     gather_steps()
     ob, gn, sh = out_row(2)
     final, normed, inv = norm_forward(g.S2[0:T].astype(f32) + g.ACC[...] + ob, gn, sh)
-    g.FO[...] = final.reshape(ni, L, D)
-    layer_store = pltpu.make_async_copy(g.FO, g.layer_out, g.js.at[8])
+    g.TMP[0:T, 0:D] = final
+    layer_store = pltpu.make_async_copy(g.TMP.at[pl.ds(0, T), pl.ds(0, D)], g.layer_out, g.js.at[8])
     layer_store.start()
 
+    cot_load.wait()
     for i in range(ni):
-        g.ACC[i * L:(i + 1) * L] = g.cot[i].astype(f32)
+        g.ACC[i * L:(i + 1) * L] = g.XV[i].astype(f32)
     cot = g.ACC[...]
     g.SM[...] = jnp.zeros(g.SM.shape, f32)
 
@@ -641,7 +660,8 @@
     swap3 = pair(g.G3, T)
     swap3.start()
 
-    rsem = (g.ss, g.rs, g.ls)
+    finish_gather()
+    rsem = (g.out, g.rs, g.ls)
     results = {"A": g.RA, "B": g.RB, "O": g.RO, "H": g.RH, "W": g.RW}
     chunks = []
     progress = {}
@@ -745,8 +765,8 @@
         loop_send(g.DCQ, T, 1, o)
         loop_send(g.DKV, ni * KP, 2, o)
         dkv = g.DKV[o, 0:ni * KP]
-        g.SM[pl.ds(9 + nz + t, 1), 0:hp] = col_sum(dcq.astype(f32))
-        g.SM[pl.ds(9 + 2 * nz + t, 1), 0:m.BW] = col_sum(dkv.astype(f32))
+        g.SM[pl.ds(9 + nz + t, 1), BW:BW + hp] = col_sum(dcq.astype(f32))
+        g.SM[pl.ds(9 + nz + t, 1), 0:BW] = col_sum(dkv.astype(f32))
         g.ACC[...] += dot(dcq, g.SA[o, 0:hp])
 
     stream([], cross_backward, after_each(reduce_steps), [], self_blocks)
@@ -763,6 +783,8 @@
     loop_wait(g.DCQ, T, 1)
     loop_wait(g.DKV, ni * KP, 2)
     swaps[1].wait_recv()
+
+    layer_store.wait()
 
     def job_b(o, c):
         t = shard(o)
@@ -795,13 +817,11 @@
         dq = jnp.concatenate([gq, gv[:, 0:LANES], gv[:, LANES:] + gk[:, 0:LANES], gk[:, LANES:]], 1).astype(bf16)
         g.DQ[o, 0:T] = dq
         loop_send(g.DQ, T, 3, o)
-        g.SM[pl.ds(9 + 3 * nz + t, 1), 0:m.QW] = col_sum(dq.astype(f32))
+        g.SM[pl.ds(9 + 2 * nz + t, 1), 0:m.QW] = col_sum(dq.astype(f32))
         g.ACC[...] += dot(dq, g.SA[o, 0:m.QW])
 
     stream([], self_backward, after_each(reduce_steps), [])
-    layer_store.wait()
-    g.FO[...] = g.ACC[...].reshape(ni, L, D)
-    text_store = pltpu.make_async_copy(g.FO, g.text_grad, g.js.at[8])
+    text_store = pltpu.make_async_copy(g.ACC, g.text_grad, g.js.at[8])
     text_store.start()
     reduce_steps()
     loop_wait(g.DQ, T, 3)
@@ -853,12 +873,11 @@
     assert calls == [len(m.gather_steps[0]), len(m.reduce_steps[0])], calls
     assert all(sum(len(p) for p in m.reduce_steps[cls]) == sum(progress[cls, c, w] for c in range(len(chunks) + 1) for w in range(3)) for cls in classes)
 
-    sends = [small_spread(o, lambda to: z) for o in range(1, nz)]
-    for cp in sends + swaps + [swap1, swap2, swap3, mix_swap]:
+    for cp in swaps + [swap1, swap2, swap3, mix_swap]:
         cp.wait_send()
     text_store.wait()
     patch_store.wait()
-    finish_gather()
+    small_store().wait()
     for cls in classes:
         @pl.when(kind == cls)
         def _():
@@ -866,19 +885,17 @@
                 c.finish(cls)
 
 
-GATHER_PLAN = (("V", 0, 16, ""), ("H", 256, 256, "yxc"), ("A", 256, 256, "yxc"), ("A", 512, 256, "yc"), ("O", 0, 384, "yxc"), ("B", 0, 128, "yxc"), ("B", 128, 256,
-    "yc"), ("H", 0, 256, "xc"), ("A", 0, 256, "yxc"), ("H", 512, 256, "xyc"), ("W", 0, 256, "xc"), ("W", 256, 256, "xyc"), ("W", 512, 256, "yc"))
-GATHER_ORDER = ((0, 320, 160, 80, -1, 13, 360, 93, 333, 373, 101, 173, 120, 14, 341, 381, 94, 334, 200, 181, 374, 109, 174, 117, 389, 349, 102, 133, 397, 342, 15,
-    357, 189, 335, 182, 382, 240, 40, 175, 197, 213, 141, 110, 440, 95, 343, 149, -1, 390, 375, 118, 134, 350, 214, 183, 221, 398, 190, 358, 103, 135,
-    280, 198, 351, 480, 142, 383, 222, 253, 359, 150, 215, -1, 143, 53, 191, 453, 391, 229, 151, 199, 254, 399, 400, 111, 237, 54, 261, 223, 230, 454,
-    119, -1, 269, 238, 61, 293, 461, -1, 262, 231, 255, 62, 462, -1, 270, 239, 69, 55, 301, 469, 455, 493, 263, -1, 77, 271, 70, 309, 294, 63, 477, 470,
-    463, 494, -1, 78, 413, 478, 501, -1, 302, 71, 295, 471, 414, 509, 502, -1, 79, 421, 310, 479, 510, 303, 495, 415, -1, 429, 311, 422, -1, -1, 430, 423,
-    503, -1, -1, 431, 511, -1, -1), (0, 4, 320, 80, 84, 324, 360, 364, 160, 164, -1, 9, 13, 93, 329, 333, 169, 373, 89, 369, 173, 120, 124, 14, 101, 381,
-    334, 337, 341, 377, 174, 200, 204, 94, 177, 129, 109, 374, 97, 209, 117, 181, 345, 133, 213, 353, 389, 349, 134, 240, 244, 342, 397, 214, 40, 357, 44,
-    440, 385, 185, 444, 382, 182, 393, 193, 102, 249, 253, 105, 49, 53, 137, 449, 113, 453, 217, 145, 189, 280, 284, -1, 254, 221, 141, 350, 54, 197, 454,
-    480, 142, 289, 484, 222, 149, 358, 190, 293, 150, 489, 390, 198, 110, 493, 400, 398, 404, 457, 118, -1, 257, 225, 294, 461, -1, 265, 261, 233, 229,
-    57, 409, 61, 413, 462, 494, -1, 269, 237, 262, 230, 297, -1, 270, 238, 62, 414, 305, 301, 302, 497, -1, 65, 309, 310, 465, 505, 501, 417, -1, 73, 69,
-    425, 473, 469, 509, -1, 77, 421, 477, 470, 502, 70, -1, 429, 78, 422, 478, 510, -1, 430, -1, -1, -1, -1, -1, -1))
+GATHER_PLAN = (("V", 0, 16, ""), ("A", 0, 256, "yxc"), ("W", 0, 512, "yc"), ("O", 0, 384, "yxc"), ("H", 0, 384, "yxc"), ("A", 256, 256, "xyc"), ("A", 512, 256,
+    "yc"), ("H", 384, 384, "yxc"), ("W", 512, 256, "yc"), ("B", 0, 384, "yxc"))
+GATHER_ORDER = ((0, 40, 200, 120, -1, 13, 53, 213, 133, 61, 14, 360, 221, 54, 214, 141, 134, 69, 15, 229, 222, 77, 240, 62, 373, 237, 55, 142, 149, 215, 230, 135,
+    157, 70, 160, 238, 381, 374, 78, 63, 150, 253, 143, 223, 280, 158, 375, 382, 254, 261, 389, 320, 173, 269, -1, 397, 71, 231, 383, 80, 255, 293, 151,
+    79, 239, 262, 174, 159, 181, 270, 175, -1, 390, 333, 263, 301, 294, 398, 271, -1, 295, 391, 182, 183, -1, 399, 341, 93, 189, -1, 309, 302, 303, 349,
+    334, 197, -1, 317, 101, 94, 190, -1, 342, 335, 109, 198, 191, -1, 310, 350, 95, 199, 102, -1, 318, 311, 343, 110, -1, 319, -1, 351, 103, -1, -1, 111,
+    -1, -1, -1), (0, 4, 40, 44, 200, 204, 120, 124, -1, 9, 13, 49, 53, 209, 213, 129, 133, 14, 360, 364, 57, 54, 217, 61, 214, 221, 137, 134, 369, 65,
+    141, 373, 240, 62, 244, 73, 69, 222, 225, 374, 77, 233, 249, 229, 253, 160, 164, 145, 142, 237, 153, 377, 254, 169, 149, 280, 284, 173, 381, 157, 70,
+    174, 230, 78, 289, 320, 324, 293, 150, 238, 382, 158, 294, 80, 84, 257, 329, 385, 333, 265, 261, -1, 393, 269, 262, 389, 177, 93, 270, -1, 397, 334,
+    89, 181, 182, -1, 297, 390, -1, 301, 185, 398, -1, 302, 337, 94, 193, 189, -1, 345, 341, 197, 190, -1, 305, 349, 101, 198, -1, 313, 342, 309, 109, -1,
+    317, 350, 310, 97, 318, -1, 105, -1, 102, -1, -1, 110, -1, -1, -1))
 REDUCE_PLAN = (("W", 128, "xyz"), ("W", 128, "yxz"), ("W", 128, "zyx"), ("H", 128, "zyx"), ("H", 128, "xyz"), ("H", 128, "xzy"), ("B", 128, "yzx"), ("B", 64,
     "xyz"), ("O", 64, "yzx"), ("O", 64, "xyz"), ("O", 64, "zxy"), ("A", 64, "xyz"), ("A", 64, "yxz"), ("A", 64, "zxy"), ("A", 64, "yzx"), ("A", 64,
     "xyz"), ("A", 64, "xyz"))
@@ -951,7 +968,7 @@
     V, sem = pltpu.VMEM, pltpu.SemaphoreType.DMA
     nc, ng = len(m.reduce_plan), len(m.gather_plan)
     nb = len(m.bits)
-    sums = (9 + 4 * nz + 7) // 8 * 8
+    sums = (9 + 3 * nz + 7) // 8 * 8
     scratch = dict(
         VG=V((nz, 16, D), bf16), X=V((2 * T, D), bf16), PT=V((2 * ni * KP, PW), bf16),
         SA=V((nz, D, D), bf16), SH=V((2, D, D), bf16), SB=V((2, BW, PW), bf16), SO=V((nz, hp, D), bf16),
@@ -960,11 +977,11 @@
         CQ=V((nz, T, hp), bf16), PC=V((nz * ni, m.nh * L, KP), f32),
         GP=V((nz, T, FZ), f32), HD=V((nz, 2 * T, FZ), bf16), SM=V((sums, D), f32), G3=V((2 * T, D), bf16), DP=V((nz, 2 * T, FZ), bf16),
         G12=V((2, 2 * T, D), bf16), DKV=V((nz, 2 * ni * KP, m.BW), bf16),
-        TMP=V((hp, PW), f32), FO=V((ni, L, D), f32), PG=V((m.NP, ni, PW), f32), AO=V((D, D), bf16), BO=V((BW, PW), bf16), OO=V((2 * hw, D), bf16), VO=V((16, D), bf16), SR=V((nb, sums, D), f32), SZ=V((nz, sums, D), f32),
-        zs=sem((ng, nz + 1)), zr=sem((ng, nz - 1)), ps=sem((ng, nz - 1)), pr=sem((ng, 3, nz - 1)),
+        TMP=V((hp, PW), f32), XV=V(x.shape, bf16), PV=V(by_patch.shape, bf16), PG=V((m.NP, ni, PW), f32), AO=V((D, D), bf16), BO=V((BW, PW), bf16), OO=V((2 * hw, D), bf16), VO=V((16, D), bf16), SR=V((nb, sums, D), f32), SZ=V((nz, sums, D), f32),
+        out=sem((max(2 * nz * ng, nz * nc),)), zr=sem((ng, nz - 1)), pr=sem((ng, 3, nz - 1)),
         cs=sem((m.swaps,)), cr=sem((m.swaps,)), ds=sem((4, nz)), dr=sem((4, nz)),
-        js=sem((10,)), sa=sem((nz,)), sh=sem((2,)), sb=sem((2,)), so=sem((nz,)),
-        ss=sem((nc, nz)), rs=sem((nc, 5 + nb - 3 + nz - 1 + nz // 2)), ls=sem((nc,)), ms=sem((nb + nz,)), mr=sem((nb,)), zm=sem((nz,)),
+        js=sem((14,)), sa=sem((nz,)), sh=sem((2,)), sb=sem((2,)), so=sem((nz,)),
+        rs=sem((nc, 5 + nb - 3 + nz - 1 + nz // 2)), ls=sem((nc,)), ms=sem((nb + nz,)), mr=sem((nb,)), zm=sem((nz,)),
     )
     for c, (k, h0, half, order) in enumerate(m.reduce_plan):
         C = lanes[k]
@@ -978,12 +995,12 @@
     S = jax.ShapeDtypeStruct
     hbm, vm, sm = (pl.BlockSpec(memory_space=s) for s in (pl.ANY, pltpu.VMEM, pltpu.SMEM))
     outs = dict(
-        layer_out=(S((ni, L, D), f32), hbm), text_grad=(S((ni, L, D), f32), hbm), patch_out=(S((m.NP, ni, PW), f32), hbm), small=(S((sums, D), f32), vm),
+        layer_out=(S((T, D), f32), hbm), text_grad=(S((T, D), f32), hbm), patch_out=(S((m.NP, ni, PW), f32), hbm), small=(S((sums, D), f32), hbm),
         **{"R" + k: (S((m.rows[k], lanes[k]), bf16), hbm) for k in "ABOHW"},
         **{"G" + k: (S((nz, m.rows[k], lanes[k]), bf16), hbm) for k in "ABOHW"},
     )
     turn = lambda a: jnp.swapaxes(a, -1, -2)
-    ins = dict(x=(x, vm), patches=(by_patch, vm), rows=(rows, sm), cot=(cot, vm), wa=(turn(wa), hbm), ab=(ab, vm), wao=(wao, hbm), wq=(turn(wq), hbm), wp=(turn(wp), hbm),
+    ins = dict(x=(x, hbm), patches=(by_patch, hbm), rows=(rows, sm), cot=(cot, hbm), wa=(turn(wa), hbm), ab=(ab, vm), wao=(wao, hbm), wq=(turn(wq), hbm), wp=(turn(wp), hbm),
                cb=(cb, vm), wco=(wco, hbm), H=(H, hbm), hb=(hb, vm), W=(W, hbm), ob=(ob, vm), gain=(gain, vm), shift=(shift, vm))
     m.inputs, m.outputs, m.scratch = list(ins), list(outs), list(scratch)
     res = pl.pallas_call(
@@ -1065,12 +1082,12 @@
     store(g.fQ, g.query)
     store(g.fA, g.attn)
     row = lambda k: g.small[pl.ds(9 + k * nz + z, 1), :]
-    qv = row(3)[:, 0:5 * LANES]
+    qv = row(2)[:, 0:5 * LANES]
     at = hw - LANES
     g.attn_bias[0:1] = qv[:, at:at + hw]
     g.attn_bias[1:2] = qv[:, at + hw:at + 2 * hw]
-    g.cross_bias[0:1] = row(1)[:, 0:hw]
-    g.cross_bias[1:2] = row(2)[:, hw:2 * hw]
+    g.cross_bias[0:1] = row(1)[:, 2 * hw:3 * hw]
+    g.cross_bias[1:2] = row(1)[:, hw:2 * hw]
     g.hidden_bias[...] = row(0).reshape(m.FZ)
     g.out_bias[...] = g.small[0:3, :]
     g.gain[...] = g.small[3:6, :]
@@ -1084,10 +1101,10 @@
     hw = m.hw = D // nz
     S, V, sem = jax.ShapeDtypeStruct, pltpu.VMEM, pltpu.SemaphoreType.DMA
     hbm, vm = pl.BlockSpec(memory_space=pl.ANY), pl.BlockSpec(memory_space=pltpu.VMEM)
-    shapes = ((ni, L, D), (ni, L, D), (NP, ni, PW), (3, hw, D), (2, hw), (hw, D), (hw, D), (2, hw, PW), (2, hw), (hw, D), (D, FZ), (FZ,), (FZ, D), (3, D), (3, D), (3, D))
+    shapes = ((m.T, D), (m.T, D), (NP, ni, PW), (3, hw, D), (2, hw), (hw, D), (hw, D), (2, hw, PW), (2, hw), (hw, D), (D, FZ), (FZ,), (FZ, D), (3, D), (3, D), (3, D))
     small = {"attn_bias", "cross_bias", "hidden_bias", "out_bias", "gain", "shift"}
     scratch = dict(
-        vW=V((FZ, D), bf16), vH=V((D, FZ), bf16), vL=V((ni, L, D), f32), vT=V((ni, L, D), f32),
+        vW=V((FZ, D), bf16), vH=V((D, FZ), bf16), vL=V((m.T, D), f32), vT=V((m.T, D), f32),
         vP=V((BW, PW), bf16), vO=V((2 * hw, D), bf16), vA=V((D, D), bf16), fW=V((FZ, D), f32), fH=V((D, FZ), f32), fG=V((NP, ni, PW), f32),
         fP=V((2, hw, PW), f32), fO=V((2 * hw, D), f32), fQ=V((hw, D), f32), fA=V((3, hw, D), f32), isem=sem((8,)), osem=sem((11,)),
     )
@@ -1111,6 +1128,8 @@
     for k in ("attn", "query", "patch"):
         at = finish_outs.index(k)
         outs[at] = jnp.swapaxes(outs[at], -1, -2)
+    for at in range(2):
+        outs[at] = outs[at].reshape(text_states.shape)
     at = finish_outs.index("patch_grad")
     outs[at] = jnp.swapaxes(outs[at], 0, 1)
     return tuple(outs)

time: 194 us -> 189 us (0.974)
  Pallas kernels: 193 us -> 188 us
    pallas_call x1, Pallas kernels: 184 us -> 179 us  [run_layer(): pl.pallas_call(functools.partial(layer_kernel, m), out_shape=tuple((o[0]...]
where the time goes in v6:
time: 189 us; the launch traced here: 188 us
  Pallas kernels  188 us (99%)
    pallas_call x1, Pallas kernels, run_layer(): pl.pallas_call(functools.partial(layer_kernel, m), out_shape=tuple((o[0]...  179 us
    pallas_call x1, Pallas kernels, finish(): pl.pallas_call(functools.partial(finish_kernel, m, finish_ins + finish_ou...  9 us

profile of v6, /device:TPU:0, one launch (start us, length us, event | category | flops | bytes accessed | tf_op | source)
XLA Modules:
  0.0 188.5 jit_solution(10797706573604319816)
XLA Ops:
  0.7 178.6 %layer.1 = (f32[160,768]{1,0:T(8,128)}, f32[160,768]{1,0:T(8,128)}, f32[145,4,1024]{2,1,0:T(4,128)}, f32[24,768]{1,0:T(8,128)}, bf16[768,768]{1,0:T(8,128)(2,1)}...) custom-call(bf16[4,40,768]{2,1,0:T(8,128)(2,1)} %refs_0_.1, ...), custom_call_target="tpu_custom_call" | custom-call | tf_op jit(solution)/shard_map/layer/pallas_call | solution.py:1006
  179.3 9.0 %finish.1 = (f32[160,768]{1,0:T(8,128)}, f32[160,768]{1,0:T(8,128)}, f32[145,4,1024]{2,1,0:T(4,128)}, f32[3,192,768]{2,1,0:T(8,128)}, f32[2,192]{1,0:T(2,128)}, ...) custom-call(bf16[768,768]{1,0:T(8,128)(2,1)} %get-tuple-element.41.r, ...), custom_call_target="tpu_custom_call" | custom-call | tf_op jit(solution)/shard_map/finish/pallas_call | solution.py:1112

commit v7 on v6

--- a/solution.py
+++ b/solution.py
@@ -32,8 +32,8 @@
 
 
 class Gather:
-    def __init__(self, src, dst, row0, rows, order, pos, nz, sems, base):
-        self.nz = nz
+    def __init__(self, src, dst, row0, rows, order, pos, nz, sems, base, pbase):
+        self.nz, self.pbase = nz, pbase
         self.src, self.dst, self.row0, self.order, self.pos = src, dst, row0, order, pos
         self.piece = rows // (2 ** len(order))
         self.zs, self.zr, self.pr = sems
@@ -72,7 +72,7 @@
         t = self.shard(dr, j)
         part = self.dst.at[t, self.win(s)]
         c = self.cell(t, p.z)
-        return pltpu.make_async_remote_copy(part, part, self.zs.at[self.base + self.nz + 1 + c], self.pr.at[self.rbase, s, c], device_id=(flip(p.d, self.order[s]), p.z), device_id_type=MESH)
+        return pltpu.make_async_remote_copy(part, part, self.zs.at[self.base + self.nz + 1 + c], self.pr.at[self.pbase + s * (self.nz - 1) + c], device_id=(flip(p.d, self.order[s]), p.z), device_id_type=MESH)
 
     @staticmethod
     def has(cls, nz, dr, j):
@@ -368,7 +368,7 @@
     gsem = (g.out, g.zr, g.pr)
     own = {"A": g.AO, "B": g.BO, "O": g.OO, "H": g.H, "W": g.W, "V": g.VO}
     far = {"A": g.GA, "B": g.GB, "O": g.GO, "H": g.GH, "W": g.GW, "V": g.VG}
-    gathers = [Gather(own[k], far[k], r0, rows, order, pos, nz, gsem, c) for c, (k, r0, rows, order) in enumerate(m.gather_plan)]
+    gathers = [Gather(own[k], far[k], r0, rows, order, pos, nz, gsem, c, (nz - 1) * sum(len(q[3]) for q in m.gather_plan[:c])) for c, (k, r0, rows, order) in enumerate(m.gather_plan)]
     calls = [0, 0]
 
     def gather_steps():
@@ -684,16 +684,19 @@
 
     reduce_steps()
 
+    reduce_steps()
+    cols = half_columns(m.FZ // 2)
+    own_part = dot_tn(g.HD[0, 0:T, cols], g.G3[0:T])
     swap3.wait_recv()
     for s in hid_swaps:
         s.wait_recv()
-    reduce_steps()
+    deal("W", shard(jnp.int32(0)), own_part + dot_tn(g.HD[0, T:, cols], g.G3[T:]))
 
     def job_w(o, c):
         t = shard(o)
-        deal("W", t, dot_tn(g.HD[o, :, half_columns(m.FZ // 2)], g.G3[...]))
+        deal("W", t, dot_tn(g.HD[o, :, cols], g.G3[...]))
         return c
-    lax.fori_loop(0, nz, job_w, 0)
+    lax.fori_loop(1, nz, job_w, 0)
     for s in hid_swaps:
         s.wait_send()
     reduce_steps()
@@ -978,7 +981,7 @@
         GP=V((nz, T, FZ), f32), HD=V((nz, 2 * T, FZ), bf16), SM=V((sums, D), f32), G3=V((2 * T, D), bf16), DP=V((nz, 2 * T, FZ), bf16),
         G12=V((2, 2 * T, D), bf16), DKV=V((nz, 2 * ni * KP, m.BW), bf16),
         TMP=V((hp, PW), f32), XV=V(x.shape, bf16), PV=V(by_patch.shape, bf16), PG=V((m.NP, ni, PW), f32), AO=V((D, D), bf16), BO=V((BW, PW), bf16), OO=V((2 * hw, D), bf16), VO=V((16, D), bf16), SR=V((nb, sums, D), f32), SZ=V((nz, sums, D), f32),
-        out=sem((max(2 * nz * ng, nz * nc),)), zr=sem((ng, nz - 1)), pr=sem((ng, 3, nz - 1)),
+        out=sem((max(2 * nz * ng, nz * nc),)), zr=sem((ng, nz - 1)), pr=sem(((nz - 1) * sum(len(q[3]) for q in m.gather_plan),)),
         cs=sem((m.swaps,)), cr=sem((m.swaps,)), ds=sem((4, nz)), dr=sem((4, nz)),
         js=sem((14,)), sa=sem((nz,)), sh=sem((2,)), sb=sem((2,)), so=sem((nz,)),
         rs=sem((nc, 5 + nb - 3 + nz - 1 + nz // 2)), ls=sem((nc,)), ms=sem((nb + nz,)), mr=sem((nb,)), zm=sem((nz,)),

time: 189 us -> 189 us (level)
  no operation moved by 1% of the time
where the time goes in v7:
time: 189 us; the launch traced here: 188 us
  Pallas kernels  187 us (99%)
    pallas_call x1, Pallas kernels, run_layer(): pl.pallas_call(functools.partial(layer_kernel, m), out_shape=tuple((o[0]...  178 us
    pallas_call x1, Pallas kernels, finish(): pl.pallas_call(functools.partial(finish_kernel, m, finish_ins + finish_ou...  9 us

profile of v7, /device:TPU:0, one launch (start us, length us, event | category | flops | bytes accessed | tf_op | source)
XLA Modules:
  0.0 188.3 jit_solution(8918126512517932674)
XLA Ops:
  0.7 178.5 %layer.1 = (f32[160,768]{1,0:T(8,128)}, f32[160,768]{1,0:T(8,128)}, f32[145,4,1024]{2,1,0:T(4,128)}, f32[24,768]{1,0:T(8,128)}, bf16[768,768]{1,0:T(8,128)(2,1)}...) custom-call(bf16[4,40,768]{2,1,0:T(8,128)(2,1)} %refs_0_.1, ...), custom_call_target="tpu_custom_call" | custom-call | tf_op jit(solution)/shard_map/layer/pallas_call | solution.py:1009
  179.1 9.0 %finish.1 = (f32[160,768]{1,0:T(8,128)}, f32[160,768]{1,0:T(8,128)}, f32[145,4,1024]{2,1,0:T(4,128)}, f32[3,192,768]{2,1,0:T(8,128)}, f32[2,192]{1,0:T(2,128)}, ...) custom-call(bf16[768,768]{1,0:T(8,128)(2,1)} %get-tuple-element.41.r, ...), custom_call_target="tpu_custom_call" | custom-call | tf_op jit(solution)/shard_map/finish/pallas_call | solution.py:1115

commit v8 on v7

--- a/solution.py
+++ b/solution.py
@@ -1034,11 +1034,11 @@
         cp = pltpu.make_async_copy(src, dst, g.isem.at[len(loads)])
         cp.start()
         loads[name] = cp
+    load("lo", g.layer_out, g.vL)
+    load("tg", g.text_grad, g.vT)
     load("W", g.RW, g.vW)
     load("H", g.RH, g.vH)
     load("pg", g.patch_out, g.fG)
-    load("lo", g.layer_out, g.vL)
-    load("tg", g.text_grad, g.vT)
     load("B", g.RB, g.vP)
     load("O", g.RO, g.vO)
     load("A", g.RA, g.vA)
@@ -1058,6 +1058,10 @@
             return c
         lax.fori_loop(0, dst.shape[0] // step, body, 0)
 
+    loads["lo"].wait()
+    store(g.vL, g.layer_out_)
+    loads["tg"].wait()
+    store(g.vT, g.text_grad_)
     loads["W"].wait()
     widen(g.vW, g.fW)
     store(g.fW, g.output)
@@ -1066,10 +1070,6 @@
     store(g.fH, g.hidden)
     loads["pg"].wait()
     store(g.fG, g.patch_grad)
-    loads["lo"].wait()
-    store(g.vL, g.layer_out_)
-    loads["tg"].wait()
-    store(g.vT, g.text_grad_)
     loads["B"].wait()
     for j in range(2):
         widen(g.vP, g.fP.at[j], j * hw)

time: 189 us -> 189 us (level)
  no operation moved by 1% of the time
where the time goes in v8:
time: 189 us
  Pallas kernels  188 us (99%)
    pallas_call x1, Pallas kernels, run_layer(): pl.pallas_call(functools.partial(layer_kernel, m), out_shape=tuple((o[0]...  178 us
    pallas_call x1, Pallas kernels, finish(): pl.pallas_call(functools.partial(finish_kernel, m, finish_ins + finish_ou...  9.46 us

profile of v8, /device:TPU:0, one launch (start us, length us, event | category | flops | bytes accessed | tf_op | source)
XLA Modules:
  0.0 188.8 jit_solution(12689102904960790229)
XLA Ops:
  0.7 178.5 %layer.1 = (f32[160,768]{1,0:T(8,128)}, f32[160,768]{1,0:T(8,128)}, f32[145,4,1024]{2,1,0:T(4,128)}, f32[24,768]{1,0:T(8,128)}, bf16[768,768]{1,0:T(8,128)(2,1)}...) custom-call(bf16[4,40,768]{2,1,0:T(8,128)(2,1)} %refs_0_.1, ...), custom_call_target="tpu_custom_call" | custom-call | tf_op jit(solution)/shard_map/layer/pallas_call | solution.py:1009
  179.1 9.5 %finish.1 = (f32[160,768]{1,0:T(8,128)}, f32[160,768]{1,0:T(8,128)}, f32[145,4,1024]{2,1,0:T(4,128)}, f32[3,192,768]{2,1,0:T(8,128)}, f32[2,192]{1,0:T(2,128)}, ...) custom-call(bf16[768,768]{1,0:T(8,128)(2,1)} %get-tuple-element.41.r, ...), custom_call_target="tpu_custom_call" | custom-call | tf_op jit(solution)/shard_map/finish/pallas_call | solution.py:1115
